TPU v7x, 128 devices: a whole 4x4x4 slice. The times are simulated.
128 devices in a mesh: rows: 32 (over z, x, core), rep: 4 (over y).
Axes of the slice: x: 4, y: 4, z: 4, core: 2. Of those that a mesh axis runs over, the one named last changes fastest.
Arguments:
- right_side: float32 [131072, 1024], P(('rep', 'rows')), parts along dimension 0, may hold values from -6 to 6
- leaf_inverse: float32 [131072, 1024], P(('rep', 'rows')), parts along dimension 0, may hold values from -0.1875 to 0.1875
- left_factors: float32 [5, 131072, 64], P(None, ('rep', 'rows')), parts along dimension 1, may hold values from -0.75 to 0.75
- right_factors: float32 [5, 131072, 64], P(None, ('rep', 'rows')), parts along dimension 1, may hold values from -0.21875 to 0.21875, as said below
- cores: float32 [124, 128, 128], P('rep'), parts along dimension 0, may hold values from -0.5 to 0.5
Outputs:
- solution: float32 [131072, 1024], P(('rep', 'rows')), parts along dimension 0
There are 4 independent parts, one for each index of `rep`. A program takes and returns all parts, laid end to end along the dimension named above; each array names one. Nothing has to cross between parts.
Inputs may be any that keep to these rules, and one draw needn't show every extreme that they name: `right_factors`: level j's entries are of order (32768 / 2^(j+1))^(-1/2).
All inputs are finite; a program needn't handle non-finite values.
Results may differ from a plain program's by a relative error of at most 0.00016.
Values sent between devices are 32-bit elements; how exact they have to be, the bound alone decides.
No kernel may reach another device: no remote copies, remote signals or barrier semaphores. Data moves between devices by JAX's collectives and lax.ppermute only.
A program may use at most 128 MiB of HBM per device.

v0:
```python
import jax
import jax.numpy as jnp
from jax import lax
from jax.experimental import pallas as pl
from jax.experimental.pallas import tpu as pltpu
from jax.sharding import PartitionSpec as P

R = 64
F32, BF16 = jnp.float32, jnp.bfloat16
MIB = 1 << 20


def split(a):
    high = a.astype(BF16)
    return high, (a - high.astype(F32)).astype(BF16)


def dot(a, b, dims=((1,), (0,))):
    return lax.dot_general(a, b, (dims, ((), ())), preferred_element_type=F32)


def mm3(a, b, dims=((1,), (0,))):
    (ah, al), (bh, bl) = a, b
    return dot(ah, bh, dims) + (dot(ah, bl, dims) + dot(al, bh, dims))


def mm(a, b):
    return mm3(split(a), split(b))


def tall(ah, al, bh, bl):
    m = ah.shape[0]
    both = dot(jnp.concatenate([ah, al], 0), bh)
    return both[:m] + (both[m:] + dot(ah, bl))


def bits(me_ref):
    me = me_ref[0]
    return me, [lax.rem(me >> b, 2) for b in range(5)]


VM = pl.BlockSpec(memory_space=pltpu.VMEM)
SM = pl.BlockSpec(memory_space=pltpu.SMEM)
HB = pl.BlockSpec(memory_space=pltpu.HBM)


def shape(*dims, dtype=F32):
    return jax.ShapeDtypeStruct(dims, dtype)


def call(kernel, ins, outs, specs, name, flops, moved, limit, scratch=(), grid=None, aliases=None):
    out_specs = [VM] * len(outs) if grid is None else grid[1]
    extra = {} if grid is None else dict(grid=grid[0])
    return pl.pallas_call(
        kernel,
        out_shape=tuple(outs),
        in_specs=specs,
        out_specs=tuple(out_specs),
        scratch_shapes=list(scratch),
        name=name,
        input_output_aliases=aliases or {},
        cost_estimate=pl.CostEstimate(flops=flops, bytes_accessed=moved, transcendentals=0),
        compiler_params=pltpu.CompilerParams(vmem_limit_bytes=limit * MIB),
        **extra,
    )(*ins)


CH = 4


def k1(me_ref, vt_hbm, ut_hbm, l_hbm, b_hbm, cores_hbm, msg, yh_ref, yl_ref, sel, vt, ut, l, b, sems):
    me, bit = bits(me_ref)
    n = l.shape[1] // CH
    half = b.shape[1]
    where = [15 + (me >> 1), 7 + (me >> 2), 7 + ((me >> 2) ^ 1), 3 + (me >> 3), 1 + (me >> 4), 1 + ((me >> 4) ^ 1), 0]
    start = pl.multiple_of((1 - bit[0]) * half, half)

    def col(k):
        return pl.ds(k * n, n)

    copies = [pltpu.make_async_copy(vt_hbm, vt, sems.at[0])]
    copies += [
        pltpu.make_async_copy(l_hbm.at[:, col(k)], l.at[:, col(k)], sems.at[1 + k]) for k in range(CH)
    ]
    copies += [pltpu.make_async_copy(ut_hbm, ut, sems.at[1 + CH])]
    copies += [
        pltpu.make_async_copy(
            b_hbm.at[:, pl.ds(pl.multiple_of(start + k * n, n), n)], b.at[:, col(k)], sems.at[2 + CH + k]
        )
        for k in range(half // n)
    ]
    picks = [
        pltpu.make_async_copy(cores_hbm.at[i], sel.at[k], sems.at[10 + k]) for k, i in enumerate(where)
    ]
    for copy in copies + picks:
        copy.start()
    copies[0].wait()
    vh, vl = split(vt[...])
    for k in range(CH):
        copies[1 + k].wait()
        lh, ll = split(l[:, k * n : k * n + n])
        y = tall(vh, vl, lh, ll)
        yh, yl = split(y)
        yh_ref[:, k * n : k * n + n] = yh
        yl_ref[:, k * n : k * n + n] = yl
    copies[1 + CH].wait()
    uh, ul = split(ut[R:, :])
    w = mm3((vh[: 4 * R], vl[: 4 * R]), (uh, ul), ((1,), (1,)))
    msg[5 * R :, : 4 * R] = w[: 2 * R]
    msg[5 * R :, 4 * R :] = w[2 * R :]
    for k in range(half // n):
        copies[2 + CH + k].wait()
        bh, bl = split(b[:, k * n : k * n + n])
        msg[: 5 * R, k * n : k * n + n] = tall(yh_ref[...], yl_ref[...], bh, bl)
    for copy in picks:
        copy.wait()


def k2(me_ref, yh, yl, b_hbm, g, b, sems):
    me, bit = bits(me_ref)
    half = b.shape[1]
    n = half // 2
    start = pl.multiple_of(bit[0] * half, half)
    copies = [
        pltpu.make_async_copy(
            b_hbm.at[:, pl.ds(pl.multiple_of(start + k * n, n), n)], b.at[:, pl.ds(k * n, n)], sems.at[k]
        )
        for k in range(2)
    ]
    for copy in copies:
        copy.start()
    for k in range(2):
        copies[k].wait()
        bh, bl = split(b[:, k * n : k * n + n])
        g[:, k * n : k * n + n] = tall(yh[...], yl[...], bh, bl)


def k3(me_ref, g, own, got, sel, m0, m1, m2, m3, q_mine, q_other, p, q):
    me, bit = bits(me_ref)
    x = lax.rem(me >> 1, 4)
    c = bit[0]
    p[pl.ds(pl.multiple_of((1 - c) * R, R), R), :] = g[4 * R :, :]
    p[pl.ds(pl.multiple_of(c * R, R), R), :] = got[4 * R : 5 * R, :]
    q[...] = mm(sel[0], p[...])
    q_mine[...] = q[pl.ds(pl.multiple_of(c * R, R), R), :]
    q_other[...] = q[pl.ds(pl.multiple_of((1 - c) * R, R), R), :]

    def level(ref, j, rows):
        if rows <= 2:
            return ref[5 * R : (5 + rows) * R, (j - 1) * R : j * R]
        low = ref[5 * R :, (j - 1) * R : j * R]
        high = ref[5 * R : (3 + rows) * R, (j + 3) * R : (j + 4) * R]
        return jnp.concatenate([low, high], 0)

    wide = split(jnp.concatenate([level(own, 4, 4), level(got, 4, 4)], 1))
    third = level(own, 3, 3) + level(got, 3, 3)
    second = level(own, 2, 2) + level(got, 2, 2)
    first = level(own, 1, 1) + level(got, 1, 1)
    packed = jnp.concatenate([third, jnp.concatenate([second, first], 0)], 1)
    for d, out in ((2, m2), (1, m1), (3, m3), (0, m0)):
        at = pl.ds(pl.multiple_of((x ^ d) * 2 * R, 2 * R), 2 * R)
        both = split(jnp.concatenate([q_mine[:, at], q_other[:, at]], 0))
        out[: 4 * R, :] = g[: 4 * R, at] + got[: 4 * R, at] - mm3(wide, both)
        out[4 * R :, :] = packed


def pair(p, core, first, second, bit):
    p[pl.ds(pl.multiple_of((1 - bit) * R, R), R), :] = first
    p[pl.ds(pl.multiple_of(bit * R, R), R), :] = second
    return mm(core, p[...])


def rows_of(q, bit, own):
    at = bit if own else 1 - bit
    return q[pl.ds(pl.multiple_of(at * R, R), R), :]


def k4(me_ref, g0, g2, g1, g3, sel, z, q3, q2, p, q):
    me, bit = bits(me_ref)
    got = (g0, g1, g2, g3)
    sums = []
    for k in range(2):
        a, b = got[2 * k], got[2 * k + 1]
        q.at[k][...] = pair(p.at[k], sel[1 + k], a[3 * R : 4 * R, :], b[3 * R : 4 * R, :], bit[1])
    for k in range(2):
        a, b = got[2 * k], got[2 * k + 1]
        mine, theirs = rows_of(q.at[k], bit[1], True), rows_of(q.at[k], bit[1], False)
        q3[2 * k] = mine
        q3[2 * k + 1] = theirs
        w = jnp.concatenate([a[4 * R :, :R], b[4 * R :, :R]], 1)
        sums.append(a[: 3 * R, :] + b[: 3 * R, :] - mm(w, jnp.concatenate([mine, theirs], 0)))
    q.at[2][...] = pair(p.at[2], sel[3], sums[0][2 * R :], sums[1][2 * R :], bit[2])
    mine, theirs = rows_of(q.at[2], bit[2], True), rows_of(q.at[2], bit[2], False)
    q2[0] = mine
    q2[1] = theirs
    w = jnp.concatenate(
        [
            g0[4 * R : 6 * R, R:] + g1[4 * R : 6 * R, R:],
            g2[4 * R : 6 * R, R:] + g3[4 * R : 6 * R, R:],
        ],
        1,
    )
    z[: 2 * R, :] = sums[0][: 2 * R] + sums[1][: 2 * R] - mm(w, jnp.concatenate([mine, theirs], 0))
    z[2 * R :, :] = (g0[6 * R :, :] + g1[6 * R :, :]) + (g2[6 * R :, :] + g3[6 * R :, :])


def k5(me_ref, s0, s3, s1, s2, sel, q3, q2, r0, r1, r2, r3, p, q):
    me, bit = bits(me_ref)
    s = (s0, s1, s2, s3)
    sums = []
    for k in range(2):
        a, b = s[2 * k], s[2 * k + 1]
        q.at[k][...] = pair(p.at[k], sel[4 + k], a[R : 2 * R, :], b[R : 2 * R, :], bit[3])
    for k in range(2):
        a, b = s[2 * k], s[2 * k + 1]
        both = jnp.concatenate([rows_of(q.at[k], bit[3], True), rows_of(q.at[k], bit[3], False)], 0)
        w = jnp.concatenate([a[2 * R :, R:], b[2 * R :, R:]], 1)
        sums.append(a[:R, :] + b[:R, :] - mm(w, both))
    q.at[2][...] = pair(p.at[2], sel[6], sums[0], sums[1], bit[4])
    top = rows_of(q.at[2], bit[4], True)
    one = rows_of(q.at[0], bit[3], True)
    for d, out in ((2, r2), (1, r1), (3, r3), (0, r0)):
        out[:R, :] = top
        out[R : 2 * R, :] = one
        out[2 * R : 3 * R, :] = q2[d // 2]
        out[3 * R :, :] = q3[d]


def k6(me_ref, r0, r2, r1, r3, q_half):
    me, bit = bits(me_ref)
    x = lax.rem(me >> 1, 4)
    for d, r in ((0, r0), (1, r1), (2, r2), (3, r3)):
        q_half[:, pl.ds(pl.multiple_of((x ^ d) * 2 * R, 2 * R), 2 * R)] = r[...]


def ku(ut, uh_ref, ul_ref):
    uh_ref[...], ul_ref[...] = split(ut[...].T)


def kl(l, b, uh, ul, q4, x):
    x[...] = mm(l[...], b[...]) - mm3((uh[:, 4 * R :], ul[:, 4 * R :]), split(q4[...]))


def k7(x, uh, ul, q, *rest):
    rest[-1][...] = x[...] - mm3((uh[:, : 4 * R], ul[:, : 4 * R]), split(q[...]))


def to_other_core(value):
    return lax.ppermute(value, "rows", [(i, i ^ 1) for i in range(32)])


def along(value, shift, d):
    return lax.ppermute(value, "rows", [(i, i ^ (d << shift)) for i in range(32)])


def spread(values, shift, order=(0, 2, 1, 3)):
    got = {0: values[0]}
    for d in (2, 1, 3):
        got[d] = along(values[d], shift, d)
    return [got[d] for d in order]


def local(right_side, leaf_inverse, left_factors, right_factors, cores):
    me = lax.axis_index("rows").astype(jnp.int32).reshape(1)
    rows, cols = right_side.shape
    half, eighth = cols // 2, cols // 8
    vt = right_factors.transpose(0, 2, 1).reshape(5 * R, rows)
    ut = left_factors.transpose(0, 2, 1).reshape(5 * R, rows)
    n = cols // CH
    in_hbm = [pltpu.with_memory_space_constraint(v, pltpu.HBM) for v in (vt, ut, leaf_inverse, right_side, cores)]

    msg, yh, yl, sel = call(
        k1, (me, *in_hbm),
        [shape(7 * R, half), shape(5 * R, rows, dtype=BF16), shape(5 * R, rows, dtype=BF16), shape(7, 2 * R, 2 * R)],
        [SM, HB, HB, HB, HB, HB], "project", 7 * 10**9, 9 * MIB, 20,
        scratch=[
            pltpu.VMEM((5 * R, rows), F32), pltpu.VMEM((5 * R, rows), F32), pltpu.VMEM((rows, cols), F32),
            pltpu.VMEM((rows, half), F32), pltpu.SemaphoreType.DMA((20,)),
        ],
    )
    got = to_other_core(msg)
    (g,) = call(
        k2, (me, yh, yl, in_hbm[3]), [shape(5 * R, half)], [SM, VM, VM, HB], "project_own",
        2 * 10**9, 3 * MIB, 10, scratch=[pltpu.VMEM((rows, half), F32), pltpu.SemaphoreType.DMA((2,))],
    )
    c = me[0] & 1
    uh, ul = call(
        ku, (lax.optimization_barrier((ut, g))[0],), [shape(rows, 5 * R, dtype=BF16)] * 2, [VM], "turn", 10, 3 * MIB, 8,
    )
    tile = 256

    def leaf(which, q4):
        def at(i, s):
            return (0, s[0])

        return pl.pallas_call(
            lambda s, l, b, u1, u2, q, x: kl(l, b, u1, u2, q, x),
            out_shape=shape(rows, half),
            grid_spec=pltpu.PrefetchScalarGridSpec(
                num_scalar_prefetch=1,
                grid=(rows // tile,),
                in_specs=[
                    pl.BlockSpec((tile, rows), lambda i, s: (i, 0)),
                    pl.BlockSpec((rows, half), at),
                    pl.BlockSpec((tile, 5 * R), lambda i, s: (i, 0)),
                    pl.BlockSpec((tile, 5 * R), lambda i, s: (i, 0)),
                    pl.BlockSpec((R, half), lambda i, s: (0, 0)),
                ],
                out_specs=pl.BlockSpec((tile, half), lambda i, s: (i, 0)),
            ),
            name="leaf",
            cost_estimate=pl.CostEstimate(flops=4 * 10**9, bytes_accessed=8 * MIB, transcendentals=0),
            compiler_params=pltpu.CompilerParams(vmem_limit_bytes=14 * MIB),
        )(which.reshape(1), leaf_inverse, right_side, uh, ul, q4)

    *messages, q4_mine, q4_other = call(
        k3, (me, g, msg, got, sel), [shape(7 * R, eighth)] * 4 + [shape(R, half)] * 2,
        [SM] + [VM] * 4, "level4", 10**9, 4 * MIB, 10,
        scratch=[pltpu.VMEM((2 * R, half), F32)] * 2,
    )
    q4_back = to_other_core(q4_other)
    small = [pltpu.VMEM((3, 2 * R, eighth), F32)] * 2
    got, x_mine = lax.optimization_barrier((spread(messages, 1), leaf(c, q4_mine)))
    z, q3, q2 = call(
        k4, (me, *got, sel),
        [shape(3 * R, eighth), shape(4, R, eighth), shape(2, R, eighth)],
        [SM] + [VM] * 5, "levels32", 10**8, MIB, 8, scratch=small,
    )
    got, x_other = lax.optimization_barrier((spread([z] * 4, 3, (0, 3, 1, 2)), leaf(1 - c, q4_back)))
    back = call(
        k5, (me, *got, sel, q3, q2), [shape(4 * R, eighth)] * 4,
        [SM] + [VM] * 7, "levels10", 10**8, MIB, 8, scratch=small,
    )
    (q_half,) = call(
        k6, (me, *spread(back, 1)), [shape(4 * R, half)], [SM] + [VM] * 4, "assemble", 10, MIB, 8,
    )
    q_rest = to_other_core(q_half)

    def finish(which, x, q, so_far):
        extra = () if so_far is None else (so_far,)
        return pl.pallas_call(
            lambda s, *refs: k7(*refs),
            out_shape=shape(rows, cols),
            grid_spec=pltpu.PrefetchScalarGridSpec(
                num_scalar_prefetch=1,
                grid=(rows // tile,),
                in_specs=[
                    pl.BlockSpec((tile, half), lambda i, s: (i, 0)),
                    pl.BlockSpec((tile, 5 * R), lambda i, s: (i, 0)),
                    pl.BlockSpec((tile, 5 * R), lambda i, s: (i, 0)),
                    pl.BlockSpec((4 * R, half), lambda i, s: (0, 0)),
                ] + [HB] * len(extra),
                out_specs=pl.BlockSpec((tile, half), lambda i, s: (i, s[0])),
            ),
            name="finish",
            input_output_aliases={5: 0} if extra else {},
            cost_estimate=pl.CostEstimate(flops=10**9, bytes_accessed=5 * MIB, transcendentals=0),
            compiler_params=pltpu.CompilerParams(vmem_limit_bytes=12 * MIB),
        )(which.reshape(1), x, uh, ul, q, *extra)

    out = finish(c, x_mine, q_half, None)
    return finish(1 - c, x_other, q_rest, out)


def solution(mesh):
    in_specs = (
        P(("rep", "rows"), None),
        P(("rep", "rows"), None),
        P(None, ("rep", "rows"), None),
        P(None, ("rep", "rows"), None),
        P("rep", None, None),
    )
    out_specs = P(("rep", "rows"), None)
    return jax.shard_map(local, mesh=mesh, in_specs=in_specs, out_specs=out_specs, check_vma=False)
```

profile of v0, /device:TPU:1, one launch (start us, length us, event | category | flops | bytes accessed | tf_op | source)
XLA Modules:
  0.0 61.5 jit_solution(11649163544329085772)
XLA Ops:
  0.0 9.4 %project.1 = (f32[448,512]{1,0:T(8,128)S(1)}, bf16[320,1024]{1,0:T(8,128)(2,1)S(1)}, bf16[320,1024]{1,0:T(8,128)(2,1)S(1)}, f32[7,128,128]{2,1,0:T(8,128)S(1)}) custom-call(s32[1]{0:T(128)} %bitcast.1.me_ref, f32[320,1024]{1,0:T(8,128)} %bitcast.11, f32[320,1024]{1,0:T(8,128)} %bitcast.9, f32[1024,1024]{1,0:T(8,128)} %l.3, f32[1024,1024]{1,0:T(8,128)} %b.3, ...), custom_call_target="tpu_custom_call" | custom-call | flops 7000000000 | bytes 9437184 | tf_op jit(solution)/shard_map/project/pallas_call | solution.py:54
  9.4 1.5 %collective-permute-start = (f32[448,512]{1,0:T(8,128)S(1)}, f32[448,512]{1,0:T(8,128)}, u32[]{:S(2)}, u32[]{:S(2)}) collective-permute-start(f32[448,512]{1,0:T(8,128)S(1)} %get-tuple-element.37.own), channel_id=1, source_target_pairs={{0,4},{4,0},{8,12},{12,8},{16,20},{20,16},{24,28},{28,24},{32,36},... | collective-permute-start | bytes 2752520 | tf_op jit(solution)/shard_map/ppermute | solution.py:249
  10.9 0.0 copy-start
  10.9 3.7 %project_own.1.g = f32[320,512]{1,0:T(8,128)S(1)} custom-call(s32[1]{0:T(128)} %bitcast.1.me_ref, bf16[320,1024]{1,0:T(8,128)(2,1)S(1)} %get-tuple-element.35.yh, bf16[320,1024]{1,0:T(8,128)(2,1)S(1)} %get-tuple-element.36.yl, f32[1024,1024]{1,0:T(8,128)} %b.3), custom_call_target="tpu_custom_call" | custom-call | flops 2000000000 | bytes 3145728 | tf_op jit(solution)/shard_map/project_own/pallas_call | solution.py:54
  14.6 0.0 copy-start.4
  14.6 0.8 %copy-done.4 = f32[320,512]{1,0:T(8,128)} copy-done((f32[320,512]{1,0:T(8,128)}, f32[320,512]{1,0:T(8,128)S(1)}, u32[]{:S(2)}) %copy-start.4) | copy-done | bytes 655384
  15.5 0.0 copy-done
  15.5 0.5 turn.1
  15.9 0.0 collective-permute-done.got
  16.0 0.0 copy-start.5
  16.0 1.1 %copy-done.5 = f32[320,512]{1,0:T(8,128)S(1)} copy-done((f32[320,512]{1,0:T(8,128)S(1)}, f32[320,512]{1,0:T(8,128)}, u32[]{:S(2)}) %copy-start.5) | copy-done | bytes 655384
  17.0 1.9 %level4.1 = (f32[448,128]{1,0:T(8,128)S(1)}, f32[448,128]{1,0:T(8,128)S(1)}, f32[448,128]{1,0:T(8,128)S(1)}, f32[448,128]{1,0:T(8,128)S(1)}, f32[64,512]{1,0:T(8,128)S(1)}, /*index=5*/f32[64,512]{1,0:T(8,128)S(1)}) custom-call(s32[1]{0:T(128)} %bitcast.1.me_ref, f32[320,512]{1,0:T(8,128)S(1)} %copy-done.5, f32[448,512]{1,0:T(8,128)S(1)} %get-tuple-element.37.own, ...), custom_call_target="tpu_custom_call" | custom-call | flops 1000000000 | bytes 4194304 | tf_op jit(solution)/shard_map/level4/pallas_call | solution.py:54
  18.9 0.1 collective-permute-start.7
  19.0 2.9 %collective-permute-start.1 = (f32[448,128]{1,0:T(8,128)S(1)}, f32[448,128]{1,0:T(8,128)S(1)}, u32[]{:S(2)}, u32[]{:S(2)}) collective-permute-start(f32[448,128]{1,0:T(8,128)S(1)} %get-tuple-element.40), channel_id=1, source_target_pairs={{0,16},{4,20},{8,24},{12,28},{16,0},{20,4},{24,8},{28,12},{32,48},... | collective-permute-start | bytes 688136 | tf_op jit(solution)/shard_map/ppermute | solution.py:253
  21.9 0.3 collective-permute-start.2
  22.2 0.5 collective-permute-start.3
  22.8 0.0 copy-start.1
  22.8 2.2 %copy-done.1 = f32[1024,1024]{1,0:T(8,128)S(1)} copy-done((f32[1024,1024]{1,0:T(8,128)S(1)}, f32[1024,1024]{1,0:T(8,128)}, u32[]{:S(2)}) %copy-start.1) | copy-done | bytes 4194328
  25.0 0.0 copy-start.3
  25.0 2.2 %copy-done.3 = f32[1024,1024]{1,0:T(8,128)S(1)} copy-done((f32[1024,1024]{1,0:T(8,128)S(1)}, f32[1024,1024]{1,0:T(8,128)}, u32[]{:S(2)}) %copy-start.3) | copy-done | bytes 4194328
  27.2 0.0 copy-start.2
  27.2 5.0 %leaf.2.refs_0_ = f32[1024,512]{1,0:T(8,128)S(1)} custom-call(s32[1]{0:T(128)} %bitcast.6.s, f32[1024,1024]{1,0:T(8,128)S(1)} %copy-done.1, f32[1024,1024]{1,0:T(8,128)S(1)} %copy-done.3, bf16[1024,320]{1,0:T(8,128)(2,1)S(1)} %get-tuple-element.44.u1.refs_1_, bf16[1024,320]{1,0:T(8,128)(2,1)S(1)} %get-tuple-element.45.u2.refs_2_, ...), custom_call_target="tpu_custom_call" | custom-call | flops 4000000000 | bytes 8388608 | tf_op jit(solution)/shard_map/leaf/pallas_call | solution.py:296
  32.2 0.0 collective-permute-done.1.g2
  32.2 0.3 collective-permute-done.2.g1
  32.5 0.5 collective-permute-done.3.g3
  33.0 0.9 %levels32.1 = (f32[192,128]{1,0:T(8,128)S(1)}, f32[4,64,128]{2,1,0:T(8,128)S(1)}, f32[2,64,128]{2,1,0:T(8,128)S(1)}) custom-call(s32[1]{0:T(128)} %bitcast.1.me_ref, f32[448,128]{1,0:T(8,128)S(1)} %get-tuple-element.47.g0, f32[448,128]{1,0:T(8,128)S(1)} %collective-permute-done.1.g2, f32[448,128]{1,0:T(8,128)S(1)} %collective-permute-done.2.g1, ...), custom_call_target="tpu_custom_call" | custom-call | flops 100000000 | bytes 1048576 | tf_op jit(solution)/shard_map/levels32/pallas_call | solution.py:54
  33.9 3.8 %collective-permute-start.6 = (f32[192,128]{1,0:T(8,128)S(1)}, f32[192,128]{1,0:T(8,128)S(1)}, u32[]{:S(2)}, u32[]{:S(2)}) collective-permute-start(f32[192,128]{1,0:T(8,128)S(1)} %get-tuple-element.54.s0), channel_id=1, source_target_pairs={{0,64},{4,68},{8,72},{12,76},{16,80},{20,84},{24,88},{28,92},{32,9... | collective-permute-start | bytes 294920 | tf_op jit(solution)/shard_map/ppermute | solution.py:253
  37.7 0.7 %collective-permute-start.5 = (f32[192,128]{1,0:T(8,128)S(1)}, f32[192,128]{1,0:T(8,128)S(1)}, u32[]{:S(2)}, u32[]{:S(2)}) collective-permute-start(f32[192,128]{1,0:T(8,128)S(1)} %get-tuple-element.54.s0), channel_id=1, source_target_pairs={{0,32},{4,36},{8,40},{12,44},{16,48},{20,52},{24,56},{28,60},{32,0... | collective-permute-start | bytes 294920 | tf_op jit(solution)/shard_map/ppermute | solution.py:253
  38.4 0.0 collective-permute-start.4
  38.4 0.0 collective-permute-done.7.q
  38.4 0.0 copy-done.2
  38.4 5.1 %leaf.3.refs_0_ = f32[1024,512]{1,0:T(8,128)S(1)} custom-call(s32[1]{0:T(128)} %bitcast.s, f32[1024,1024]{1,0:T(8,128)S(1)} %copy-done.2, f32[1024,1024]{1,0:T(8,128)S(1)} %copy-done.3, bf16[1024,320]{1,0:T(8,128)(2,1)S(1)} %get-tuple-element.44.u1.refs_1_, bf16[1024,320]{1,0:T(8,128)(2,1)S(1)} %get-tuple-element.45.u2.refs_2_, ...), custom_call_target="tpu_custom_call" | custom-call | flops 4000000000 | bytes 8388608 | tf_op jit(solution)/shard_map/leaf/pallas_call | solution.py:296
  43.6 0.0 collective-permute-done.6.s2
  43.6 0.0 collective-permute-done.5.s1
  43.6 0.0 collective-permute-done.4.s3
  43.6 0.6 %levels10.1 = (f32[256,128]{1,0:T(8,128)S(1)}, f32[256,128]{1,0:T(8,128)S(1)}, f32[256,128]{1,0:T(8,128)S(1)}, f32[256,128]{1,0:T(8,128)S(1)}) custom-call(s32[1]{0:T(128)} %bitcast.1.me_ref, f32[192,128]{1,0:T(8,128)S(1)} %get-tuple-element.54.s0, f32[192,128]{1,0:T(8,128)S(1)} %collective-permute-done.4.s3, f32[192,128]{1,0:T(8,128)S(1)} %collective-permute-done.5.s1, ...), custom_call_target="tpu_custom_call" | custom-call | flops 100000000 | bytes 1048576 | tf_op jit(solution)/shard_map/levels10/pallas_call | solution.py:54
  44.2 2.8 %collective-permute-start.8 = (f32[256,128]{1,0:T(8,128)S(1)}, f32[256,128]{1,0:T(8,128)S(1)}, u32[]{:S(2)}, u32[]{:S(2)}) collective-permute-start(f32[256,128]{1,0:T(8,128)S(1)} %get-tuple-element.61), channel_id=1, source_target_pairs={{0,16},{4,20},{8,24},{12,28},{16,0},{20,4},{24,8},{28,12},{32,48},... | collective-permute-start | bytes 393224 | tf_op jit(solution)/shard_map/ppermute | solution.py:253
  47.1 0.3 collective-permute-start.9
  47.4 0.5 collective-permute-start.10
  47.9 1.7 %collective-permute-done.8.r2 = f32[256,128]{1,0:T(8,128)S(1)} collective-permute-done((f32[256,128]{1,0:T(8,128)S(1)}, f32[256,128]{1,0:T(8,128)S(1)}, u32[]{:S(2)}, u32[]{:S(2)}) %collective-permute-start.8) | collective-permute-done | bytes 131104 | tf_op jit(solution)/shard_map/ppermute | solution.py:253
  49.6 2.4 %collective-permute-done.9.r1 = f32[256,128]{1,0:T(8,128)S(1)} collective-permute-done((f32[256,128]{1,0:T(8,128)S(1)}, f32[256,128]{1,0:T(8,128)S(1)}, u32[]{:S(2)}, u32[]{:S(2)}) %collective-permute-start.9) | collective-permute-done | bytes 131104 | tf_op jit(solution)/shard_map/ppermute | solution.py:253
  52.0 1.5 %collective-permute-done.10.r3 = f32[256,128]{1,0:T(8,128)S(1)} collective-permute-done((f32[256,128]{1,0:T(8,128)S(1)}, f32[256,128]{1,0:T(8,128)S(1)}, u32[]{:S(2)}, u32[]{:S(2)}) %collective-permute-start.10) | collective-permute-done | bytes 131104 | tf_op jit(solution)/shard_map/ppermute | solution.py:253
  53.5 0.1 assemble.1.refs_3_
  53.6 2.3 %collective-permute-start.11 = (f32[256,512]{1,0:T(8,128)S(1)}, f32[256,512]{1,0:T(8,128)S(1)}, u32[]{:S(2)}, u32[]{:S(2)}) collective-permute-start(f32[256,512]{1,0:T(8,128)S(1)} %assemble.1.refs_3_), channel_id=1, source_target_pairs={{0,4},{4,0},{8,12},{12,8},{16,20},{20,16},{24,28},{28,24},{32,36},... | collective-permute-start | bytes 1572872 | tf_op jit(solution)/shard_map/ppermute | solution.py:249
  56.0 2.7 %finish.2.refs_4_ = f32[1024,1024]{1,0:T(8,128)} custom-call(s32[1]{0:T(128)} %bitcast.6.s, f32[1024,512]{1,0:T(8,128)S(1)} %leaf.2.refs_0_, bf16[1024,320]{1,0:T(8,128)(2,1)S(1)} %get-tuple-element.44.u1.refs_1_, bf16[1024,320]{1,0:T(8,128)(2,1)S(1)} %get-tuple-element.45.u2.refs_2_, f32[256,512]{1,0:T(8,128)S(1)} %assemble.1.refs_3_), custom_call_target="tpu_custom_call" | custom-call | flops 1000000000 | bytes 5242880 | tf_op jit(solution)/shard_map/finish/pallas_call | solution.py:341
  58.7 0.0 collective-permute-done.11.refs_3_
  58.7 2.7 %finish.3 = f32[1024,1024]{1,0:T(8,128)} custom-call(s32[1]{0:T(128)} %bitcast.s, f32[1024,512]{1,0:T(8,128)S(1)} %leaf.3.refs_0_, bf16[1024,320]{1,0:T(8,128)(2,1)S(1)} %get-tuple-element.44.u1.refs_1_, bf16[1024,320]{1,0:T(8,128)(2,1)S(1)} %get-tuple-element.45.u2.refs_2_, ...), custom_call_target="tpu_custom_call", output_to_operand_aliasing={{}: (5, {})} | custom-call | flops 1000000000 | bytes 5242880 | tf_op jit(solution)/shard_map/finish/pallas_call | solution.py:341
Async XLA Ops:
  9.4 6.5 %collective-permute-start = (f32[448,512]{1,0:T(8,128)S(1)}, f32[448,512]{1,0:T(8,128)}, u32[]{:S(2)}, u32[]{:S(2)}) collective-permute-start(f32[448,512]{1,0:T(8,128)S(1)} %get-tuple-element.37.own), channel_id=1, source_target_pairs={{0,4},{4,0},{8,12},{12,8},{16,20},{20,16},{24,28},{28,24},{32,36},... | collective-permute-start | bytes 2752520 | tf_op jit(solution)/shard_map/ppermute | solution.py:249
  10.9 4.5 %copy-start = (f32[5,1024,64]{1,2,0:T(8,128)S(1)}, f32[5,1024,64]{1,2,0:T(8,128)}, u32[]{:S(2)}) copy-start(f32[5,1024,64]{1,2,0:T(8,128)} %param.7) | copy-start | bytes 3932164
  14.6 0.8 %copy-start.4 = (f32[320,512]{1,0:T(8,128)}, f32[320,512]{1,0:T(8,128)S(1)}, u32[]{:S(2)}) copy-start(f32[320,512]{1,0:T(8,128)S(1)} %project_own.1.g) | copy-start | bytes 1966084
  16.0 1.1 %copy-start.5 = (f32[320,512]{1,0:T(8,128)S(1)}, f32[320,512]{1,0:T(8,128)}, u32[]{:S(2)}) copy-start(f32[320,512]{1,0:T(8,128)} %copy-done.4) | copy-start | bytes 1966084
  18.9 19.5 %collective-permute-start.7 = (f32[64,512]{1,0:T(8,128)S(1)}, f32[64,512]{1,0:T(8,128)S(1)}, u32[]{:S(2)}, u32[]{:S(2)}) collective-permute-start(f32[64,512]{1,0:T(8,128)S(1)} %get-tuple-element.52), channel_id=1, source_target_pairs={{0,4},{4,0},{8,12},{12,8},{16,20},{20,16},{24,28},{28,24},{32,36},... | collective-permute-start | bytes 393224 | tf_op jit(solution)/shard_map/ppermute | solution.py:249
  19.0 13.1 %collective-permute-start.1 = (f32[448,128]{1,0:T(8,128)S(1)}, f32[448,128]{1,0:T(8,128)S(1)}, u32[]{:S(2)}, u32[]{:S(2)}) collective-permute-start(f32[448,128]{1,0:T(8,128)S(1)} %get-tuple-element.40), channel_id=1, source_target_pairs={{0,16},{4,20},{8,24},{12,28},{16,0},{20,4},{24,8},{28,12},{32,48},... | collective-permute-start | bytes 688136 | tf_op jit(solution)/shard_map/ppermute | solution.py:253
  21.9 10.6 %collective-permute-start.2 = (f32[448,128]{1,0:T(8,128)S(1)}, f32[448,128]{1,0:T(8,128)S(1)}, u32[]{:S(2)}, u32[]{:S(2)}) collective-permute-start(f32[448,128]{1,0:T(8,128)S(1)} %get-tuple-element.41), channel_id=1, source_target_pairs={{0,8},{4,12},{8,0},{12,4},{16,24},{20,28},{24,16},{28,20},{32,40},... | collective-permute-start | bytes 688136 | tf_op jit(solution)/shard_map/ppermute | solution.py:253
  22.2 10.8 %collective-permute-start.3 = (f32[448,128]{1,0:T(8,128)S(1)}, f32[448,128]{1,0:T(8,128)S(1)}, u32[]{:S(2)}, u32[]{:S(2)}) collective-permute-start(f32[448,128]{1,0:T(8,128)S(1)} %get-tuple-element.42), channel_id=1, source_target_pairs={{0,24},{4,28},{8,16},{12,20},{16,8},{20,12},{24,0},{28,4},{32,56},... | collective-permute-start | bytes 688136 | tf_op jit(solution)/shard_map/ppermute | solution.py:253
  22.8 2.2 %copy-start.1 = (f32[1024,1024]{1,0:T(8,128)S(1)}, f32[1024,1024]{1,0:T(8,128)}, u32[]{:S(2)}) copy-start(f32[1024,1024]{1,0:T(8,128)} %l.3) | copy-start | bytes 12582916
  25.0 2.2 %copy-start.3 = (f32[1024,1024]{1,0:T(8,128)S(1)}, f32[1024,1024]{1,0:T(8,128)}, u32[]{:S(2)}) copy-start(f32[1024,1024]{1,0:T(8,128)} %b.3) | copy-start | bytes 12582916
  27.2 11.3 %copy-start.2 = (f32[1024,1024]{1,0:T(8,128)S(1)}, f32[1024,1024]{1,0:T(8,128)}, u32[]{:S(2)}) copy-start(f32[1024,1024]{1,0:T(8,128)} %l.3) | copy-start | bytes 12582916
  33.9 9.7 %collective-permute-start.6 = (f32[192,128]{1,0:T(8,128)S(1)}, f32[192,128]{1,0:T(8,128)S(1)}, u32[]{:S(2)}, u32[]{:S(2)}) collective-permute-start(f32[192,128]{1,0:T(8,128)S(1)} %get-tuple-element.54.s0), channel_id=1, source_target_pairs={{0,64},{4,68},{8,72},{12,76},{16,80},{20,84},{24,88},{28,92},{32,9... | collective-permute-start | bytes 294920 | tf_op jit(solution)/shard_map/ppermute | solution.py:253
  37.7 5.9 %collective-permute-start.5 = (f32[192,128]{1,0:T(8,128)S(1)}, f32[192,128]{1,0:T(8,128)S(1)}, u32[]{:S(2)}, u32[]{:S(2)}) collective-permute-start(f32[192,128]{1,0:T(8,128)S(1)} %get-tuple-element.54.s0), channel_id=1, source_target_pairs={{0,32},{4,36},{8,40},{12,44},{16,48},{20,52},{24,56},{28,60},{32,0... | collective-permute-start | bytes 294920 | tf_op jit(solution)/shard_map/ppermute | solution.py:253
  38.4 5.2 %collective-permute-start.4 = (f32[192,128]{1,0:T(8,128)S(1)}, f32[192,128]{1,0:T(8,128)S(1)}, u32[]{:S(2)}, u32[]{:S(2)}) collective-permute-start(f32[192,128]{1,0:T(8,128)S(1)} %get-tuple-element.54.s0), channel_id=1, source_target_pairs={{0,96},{4,100},{8,104},{12,108},{16,112},{20,116},{24,120},{28,124... | collective-permute-start | bytes 294920 | tf_op jit(solution)/shard_map/ppermute | solution.py:253
  44.2 5.4 %collective-permute-start.8 = (f32[256,128]{1,0:T(8,128)S(1)}, f32[256,128]{1,0:T(8,128)S(1)}, u32[]{:S(2)}, u32[]{:S(2)}) collective-permute-start(f32[256,128]{1,0:T(8,128)S(1)} %get-tuple-element.61), channel_id=1, source_target_pairs={{0,16},{4,20},{8,24},{12,28},{16,0},{20,4},{24,8},{28,12},{32,48},... | collective-permute-start | bytes 393224 | tf_op jit(solution)/shard_map/ppermute | solution.py:253
  47.1 5.0 %collective-permute-start.9 = (f32[256,128]{1,0:T(8,128)S(1)}, f32[256,128]{1,0:T(8,128)S(1)}, u32[]{:S(2)}, u32[]{:S(2)}) collective-permute-start(f32[256,128]{1,0:T(8,128)S(1)} %get-tuple-element.62), channel_id=1, source_target_pairs={{0,8},{4,12},{8,0},{12,4},{16,24},{20,28},{24,16},{28,20},{32,40},... | collective-permute-start | bytes 393224 | tf_op jit(solution)/shard_map/ppermute | solution.py:253
  47.4 6.2 %collective-permute-start.10 = (f32[256,128]{1,0:T(8,128)S(1)}, f32[256,128]{1,0:T(8,128)S(1)}, u32[]{:S(2)}, u32[]{:S(2)}) collective-permute-start(f32[256,128]{1,0:T(8,128)S(1)} %get-tuple-element.63), channel_id=1, source_target_pairs={{0,24},{4,28},{8,16},{12,20},{16,8},{20,12},{24,0},{28,4},{32,56},... | collective-permute-start | bytes 393224 | tf_op jit(solution)/shard_map/ppermute | solution.py:253
  53.6 5.1 %collective-permute-start.11 = (f32[256,512]{1,0:T(8,128)S(1)}, f32[256,512]{1,0:T(8,128)S(1)}, u32[]{:S(2)}, u32[]{:S(2)}) collective-permute-start(f32[256,512]{1,0:T(8,128)S(1)} %assemble.1.refs_3_), channel_id=1, source_target_pairs={{0,4},{4,0},{8,12},{12,8},{16,20},{20,16},{24,28},{28,24},{32,36},... | collective-permute-start | bytes 1572872 | tf_op jit(solution)/shard_map/ppermute | solution.py:249
where the time goes:
time: 61.7 us; the launch traced here: 61.5 us
  Pallas kernels  32.6 us (53%)
  starting transfers between devices  15.9 us (26%)
  waiting for transfers between devices  6.5 us (11%)
  local copies, waits for them, and re-layouts  6.3 us (10%)
    pallas_call x7, Pallas kernels, call(): pl.pallas_call(kernel, out_shape=tuple(outs), in_specs=specs, out_specs=t...  17 us
    ppermute x9, starting transfers between devices, along(): return lax.ppermute(value, 'rows', [(i, i ^ d << shift) for i in range(32)])  12 us
    pallas_call x2, Pallas kernels, leaf(): pl.pallas_call(lambda s, l, b, u1, u2, q, x: kl(l, b, u1, u2, q, x), out_...  10.1 us
    ppermute x9, waiting for transfers between devices, along(): return lax.ppermute(value, 'rows', [(i, i ^ d << shift) for i in range(32)])  6.49 us
    unnamed x12, local copies, waits for them, and re-layouts  6.3 us
    pallas_call x2, Pallas kernels, finish(): pl.pallas_call(lambda s, *refs: k7(*refs), out_shape=shape(rows, cols), g...  5.48 us
    ppermute x3, starting transfers between devices, to_other_core(): return lax.ppermute(value, 'rows', [(i, i ^ 1) for i in range(32)])  3.96 us
  transfers between devices with their start and end apart: 12, of which 5 were waited for; matrix products, arithmetic and copies ran while one was open for 0% of the time, Pallas kernels for 29%

commit v1 on v0

v1 whole, which is shorter than its diff:
```python
import jax
import jax.numpy as jnp
from jax import lax
from jax.experimental import pallas as pl
from jax.experimental.pallas import tpu as pltpu
from jax.sharding import PartitionSpec as P

R = 64
F32, BF16 = jnp.float32, jnp.bfloat16
MIB = 1 << 20


def split(a):
    high = a.astype(BF16)
    return high, (a - high.astype(F32)).astype(BF16)


def dot(a, b, dims=((1,), (0,))):
    return lax.dot_general(a, b, (dims, ((), ())), preferred_element_type=F32)


def mm3(a, b):
    (ah, al), (bh, bl) = a, b
    return dot(jnp.concatenate([ah, al, ah], 1), jnp.concatenate([bh, bh, bl], 0))


def mm(a, b):
    return mm3(split(a), split(b))


def bits(me_ref):
    me = me_ref[0]
    return me, [lax.rem(me >> b, 2) for b in range(5)]


VM = pl.BlockSpec(memory_space=pltpu.VMEM)
SM = pl.BlockSpec(memory_space=pltpu.SMEM)
HB = pl.BlockSpec(memory_space=pltpu.HBM)


def shape(*dims, dtype=F32):
    return jax.ShapeDtypeStruct(dims, dtype)


def call(kernel, ins, outs, specs, name, flops, moved, limit, scratch=(), grid=None, aliases=None):
    out_specs = [VM] * len(outs) if grid is None else grid[1]
    extra = {} if grid is None else dict(grid=grid[0])
    return pl.pallas_call(
        kernel,
        out_shape=tuple(outs),
        in_specs=specs,
        out_specs=tuple(out_specs),
        scratch_shapes=list(scratch),
        name=name,
        input_output_aliases=aliases or {},
        cost_estimate=pl.CostEstimate(flops=flops, bytes_accessed=moved, transcendentals=0),
        compiler_params=pltpu.CompilerParams(vmem_limit_bytes=limit * MIB),
        **extra,
    )(*ins)


CH = 4


def k1(me_ref, vt_hbm, ut_hbm, l_hbm, b_hbm, cores_hbm, msg, yh_ref, yl_ref, lh_ref, ll_ref, b, sel, vt, ut, l, sems):
    me, bit = bits(me_ref)
    n = l.shape[0] // CH
    half = b.shape[2]
    where = [15 + (me >> 1), 7 + (me >> 2), 7 + ((me >> 2) ^ 1), 3 + (me >> 3), 1 + (me >> 4), 1 + ((me >> 4) ^ 1), 0]
    rows = [pl.ds(k * n, n) for k in range(CH)]
    get_v = pltpu.make_async_copy(vt_hbm, vt, sems.at[0])
    get_l = [pltpu.make_async_copy(l_hbm.at[rows[k]], l.at[rows[k]], sems.at[1 + k]) for k in range(CH)]
    get_u = pltpu.make_async_copy(ut_hbm, ut, sems.at[1 + CH])
    get_b = [
        pltpu.make_async_copy(
            b_hbm.at[:, pl.ds(pl.multiple_of(at * half, half), half)], b.at[k], sems.at[2 + CH + k]
        )
        for k, at in enumerate((bit[0], 1 - bit[0]))
    ]
    picks = [pltpu.make_async_copy(cores_hbm.at[i], sel.at[k], sems.at[10 + k]) for k, i in enumerate(where)]
    for copy in [get_v, *get_l, get_b[1], get_u, *picks, get_b[0]]:
        copy.start()
    get_v.wait()
    vh, vl = split(vt[...])
    y = None
    for k in range(CH):
        get_l[k].wait()
        at = slice(k * n, k * n + n)
        lh, ll = split(l[at, :])
        lh_ref[at, :] = lh
        ll_ref[at, :] = ll
        part = mm3((vh[:, at], vl[:, at]), (lh, ll))
        y = part if y is None else y + part
    yh, yl = split(y)
    yh_ref[...] = yh
    yl_ref[...] = yl
    get_b[1].wait()
    msg[: 5 * R, :] = mm3((yh, yl), split(b[1]))
    get_u.wait()
    uh, ul = split(ut[R:, :])
    vh, vl = vh[: 4 * R], vl[: 4 * R]
    w = dot(jnp.concatenate([vh, vl, vh], 1), jnp.concatenate([uh, uh, ul], 1), ((1,), (1,)))
    msg[5 * R :, : 4 * R] = w[: 2 * R]
    msg[5 * R :, 4 * R :] = w[2 * R :]
    for copy in picks + [get_b[0]]:
        copy.wait()


def k2(yh, yl, b, g):
    g[...] = mm3((yh[...], yl[...]), split(b[0]))


def k3(me_ref, g, own, got, sel, m0, m1, m2, m3, q_mine, q_other, p, q):
    me, bit = bits(me_ref)
    x = lax.rem(me >> 1, 4)
    c = bit[0]
    p[pl.ds(pl.multiple_of((1 - c) * R, R), R), :] = g[4 * R :, :]
    p[pl.ds(pl.multiple_of(c * R, R), R), :] = got[4 * R : 5 * R, :]
    q[...] = mm(sel[0], p[...])
    q_mine[...] = q[pl.ds(pl.multiple_of(c * R, R), R), :]
    q_other[...] = q[pl.ds(pl.multiple_of((1 - c) * R, R), R), :]

    def level(ref, j, rows):
        if rows <= 2:
            return ref[5 * R : (5 + rows) * R, (j - 1) * R : j * R]
        low = ref[5 * R :, (j - 1) * R : j * R]
        high = ref[5 * R : (3 + rows) * R, (j + 3) * R : (j + 4) * R]
        return jnp.concatenate([low, high], 0)

    wide = split(jnp.concatenate([level(own, 4, 4), level(got, 4, 4)], 1))
    third = level(own, 3, 3) + level(got, 3, 3)
    second = level(own, 2, 2) + level(got, 2, 2)
    first = level(own, 1, 1) + level(got, 1, 1)
    packed = jnp.concatenate([third, jnp.concatenate([second, first], 0)], 1)
    for d, out in ((2, m2), (1, m1), (3, m3), (0, m0)):
        at = pl.ds(pl.multiple_of((x ^ d) * 2 * R, 2 * R), 2 * R)
        both = split(jnp.concatenate([q_mine[:, at], q_other[:, at]], 0))
        out[: 4 * R, :] = g[: 4 * R, at] + got[: 4 * R, at] - mm3(wide, both)
        out[4 * R :, :] = packed


def pair(p, core, first, second, bit):
    p[pl.ds(pl.multiple_of((1 - bit) * R, R), R), :] = first
    p[pl.ds(pl.multiple_of(bit * R, R), R), :] = second
    return mm(core, p[...])


def rows_of(q, bit, own):
    at = bit if own else 1 - bit
    return q[pl.ds(pl.multiple_of(at * R, R), R), :]


def k4(me_ref, g0, g2, g1, g3, sel, z, q3, q2, p, q):
    me, bit = bits(me_ref)
    got = (g0, g1, g2, g3)
    sums = []
    for k in range(2):
        a, b = got[2 * k], got[2 * k + 1]
        q.at[k][...] = pair(p.at[k], sel[1 + k], a[3 * R : 4 * R, :], b[3 * R : 4 * R, :], bit[1])
    for k in range(2):
        a, b = got[2 * k], got[2 * k + 1]
        mine, theirs = rows_of(q.at[k], bit[1], True), rows_of(q.at[k], bit[1], False)
        q3[2 * k] = mine
        q3[2 * k + 1] = theirs
        w = jnp.concatenate([a[4 * R :, :R], b[4 * R :, :R]], 1)
        sums.append(a[: 3 * R, :] + b[: 3 * R, :] - mm(w, jnp.concatenate([mine, theirs], 0)))
    q.at[2][...] = pair(p.at[2], sel[3], sums[0][2 * R :], sums[1][2 * R :], bit[2])
    mine, theirs = rows_of(q.at[2], bit[2], True), rows_of(q.at[2], bit[2], False)
    q2[0] = mine
    q2[1] = theirs
    w = jnp.concatenate(
        [
            g0[4 * R : 6 * R, R:] + g1[4 * R : 6 * R, R:],
            g2[4 * R : 6 * R, R:] + g3[4 * R : 6 * R, R:],
        ],
        1,
    )
    z[: 2 * R, :] = sums[0][: 2 * R] + sums[1][: 2 * R] - mm(w, jnp.concatenate([mine, theirs], 0))
    z[2 * R :, :] = (g0[6 * R :, :] + g1[6 * R :, :]) + (g2[6 * R :, :] + g3[6 * R :, :])


def k5(me_ref, s0, s2, s1, s3, sel, q3, q2, r0, r1, r2, r3, p, q):
    me, bit = bits(me_ref)
    s = (s0, s1, s2, s3)
    sums = []
    for k in range(2):
        a, b = s[2 * k], s[2 * k + 1]
        q.at[k][...] = pair(p.at[k], sel[4 + k], a[R : 2 * R, :], b[R : 2 * R, :], bit[3])
    for k in range(2):
        a, b = s[2 * k], s[2 * k + 1]
        both = jnp.concatenate([rows_of(q.at[k], bit[3], True), rows_of(q.at[k], bit[3], False)], 0)
        w = jnp.concatenate([a[2 * R :, R:], b[2 * R :, R:]], 1)
        sums.append(a[:R, :] + b[:R, :] - mm(w, both))
    q.at[2][...] = pair(p.at[2], sel[6], sums[0], sums[1], bit[4])
    top = rows_of(q.at[2], bit[4], True)
    one = rows_of(q.at[0], bit[3], True)
    for d, out in ((2, r2), (1, r1), (3, r3), (0, r0)):
        out[:R, :] = top
        out[R : 2 * R, :] = one
        out[2 * R : 3 * R, :] = q2[d // 2]
        out[3 * R :, :] = q3[d]


def k6(me_ref, r0, r2, r1, r3, q_half):
    me, bit = bits(me_ref)
    x = lax.rem(me >> 1, 4)
    for d, r in ((0, r0), (1, r1), (2, r2), (3, r3)):
        q_half[:, pl.ds(pl.multiple_of((x ^ d) * 2 * R, 2 * R), 2 * R)] = r[...]


def ku(ut, uh_ref, ul_ref):
    uh_ref[...], ul_ref[...] = split(ut[...].T)


def kl(piece, lh, ll, b, uh, ul, q4, x):
    n = x.shape[1]
    at = slice(piece % 2 * n, piece % 2 * n + n)
    bh, bl = split(b[piece // 2, :, at])
    qh, ql = split(q4[:, at])
    right = jnp.concatenate([bh, bh, bl], 0)
    below = jnp.concatenate([qh, qh, ql], 0)
    for k in range(4):
        r = slice(k * 2 * 128, (k + 1) * 2 * 128)
        u4h, u4l = uh[r, 4 * R :], ul[r, 4 * R :]
        x[r, :] = dot(jnp.concatenate([lh[r, :], ll[r, :], lh[r, :]], 1), right) - dot(
            jnp.concatenate([u4h, u4l, u4h], 1), below
        )


def k7(mine, me_ref, xa, xb, uh, ul, q, *rest):
    out, buf, sems = rest[-3:]
    me, bit = bits(me_ref)
    half = q.shape[1]
    at = pl.multiple_of((bit[0] if mine else 1 - bit[0]) * half, half)
    qh, ql = split(q[...])
    right = jnp.concatenate([qh, qh, ql], 0)
    copies = []
    for k in range(4):
        r = slice(k * 256, k * 256 + 256)
        u3h, u3l = uh[r, : 4 * R], ul[r, : 4 * R]
        buf[r, :] = jnp.concatenate([xa[r, :], xb[r, :]], 1) - dot(jnp.concatenate([u3h, u3l, u3h], 1), right)
        copies.append(
            pltpu.make_async_copy(
                buf.at[pl.ds(k * 256, 256)], out.at[pl.ds(k * 256, 256), pl.ds(at, half)], sems.at[k]
            )
        )
        copies[-1].start()
    for copy in copies:
        copy.wait()


def to_other_core(value):
    return lax.ppermute(value, "rows", [(i, i ^ 1) for i in range(32)])


def along(value, shift, d):
    return lax.ppermute(value, "rows", [(i, i ^ (d << shift)) for i in range(32)])


def spread(values, shift, order=(0, 2, 1, 3)):
    got = {0: values[0]}
    for d in (2, 1, 3):
        got[d] = along(values[d], shift, d)
    return [got[d] for d in order]


def local(right_side, leaf_inverse, left_factors, right_factors, cores):
    me = lax.axis_index("rows").astype(jnp.int32).reshape(1)
    rows, cols = right_side.shape
    half, eighth = cols // 2, cols // 8
    vt = right_factors.transpose(0, 2, 1).reshape(5 * R, rows)
    ut = left_factors.transpose(0, 2, 1).reshape(5 * R, rows)
    in_hbm = [pltpu.with_memory_space_constraint(v, pltpu.HBM) for v in (vt, ut, leaf_inverse, right_side, cores)]

    def pieces(dims, *more):
        return [shape(*dims, **kw) for kw in more]

    half_type = dict(dtype=BF16)
    msg, yh, yl, lh, ll, b, sel = call(
        k1, (me, *in_hbm),
        [shape(7 * R, half), *pieces((5 * R, rows), half_type, half_type), *pieces((rows, rows), half_type, half_type),
         shape(2, rows, half), shape(7, 2 * R, 2 * R)],
        [SM, HB, HB, HB, HB, HB], "project", 7 * 10**9, 9 * MIB, 28,
        scratch=[
            pltpu.VMEM((5 * R, rows), F32), pltpu.VMEM((5 * R, rows), F32), pltpu.VMEM((rows, rows), F32),
            pltpu.SemaphoreType.DMA((20,)),
        ],
    )
    got = to_other_core(msg)
    (g,) = call(k2, (yh, yl, b), [shape(5 * R, half)], [VM, VM, VM], "project_own", 2 * 10**9, 3 * MIB, 10)
    uh, ul = call(
        ku, (lax.optimization_barrier((ut, g))[0],), [shape(rows, 5 * R, dtype=BF16)] * 2, [VM], "turn", 10, 3 * MIB, 8,
    )

    def leaf(piece, q4):
        return call(
            lambda *refs: kl(piece, *refs), (lh, ll, b, uh, ul, q4), [shape(rows, half // 2)], [VM] * 6, "leaf",
            2 * 10**9, 6 * MIB, 12,
        )[0]

    *messages, q4_mine, q4_other = call(
        k3, (me, g, msg, got, sel), [shape(7 * R, eighth)] * 4 + [shape(R, half)] * 2,
        [SM] + [VM] * 4, "level4", 10**9, 4 * MIB, 10,
        scratch=[pltpu.VMEM((2 * R, half), F32)] * 2,
    )
    q4_back = to_other_core(q4_other)
    small = [pltpu.VMEM((3, 2 * R, eighth), F32)] * 2
    got, x0 = lax.optimization_barrier((spread(messages, 1), leaf(0, q4_mine)))
    z, q3, q2 = call(
        k4, (me, *got, sel),
        [shape(3 * R, eighth), shape(4, R, eighth), shape(2, R, eighth)],
        [SM] + [VM] * 5, "levels32", 10**8, MIB, 8, scratch=small,
    )
    got, x1 = lax.optimization_barrier((spread([z] * 4, 3), leaf(1, q4_mine)))
    back = call(
        k5, (me, *got, sel, q3, q2), [shape(4 * R, eighth)] * 4,
        [SM] + [VM] * 7, "levels10", 10**8, MIB, 8, scratch=small,
    )
    got, x2, x3 = lax.optimization_barrier((spread(back, 1), leaf(2, q4_back), leaf(3, q4_back)))
    (q_half,) = call(k6, (me, *got), [shape(4 * R, half)], [SM] + [VM] * 4, "assemble", 10, MIB, 8)
    q_rest = to_other_core(q_half)

    def finish(mine, xa, xb, q, *so_far):
        return pl.pallas_call(
            lambda *refs: k7(mine, *refs),
            out_shape=shape(rows, cols),
            in_specs=[SM] + [VM] * 5 + [HB] * len(so_far),
            out_specs=HB,
            scratch_shapes=[pltpu.VMEM((rows, half), F32), pltpu.SemaphoreType.DMA((4,))],
            name="finish",
            input_output_aliases={6: 0} if so_far else {},
            cost_estimate=pl.CostEstimate(flops=10**9, bytes_accessed=5 * MIB, transcendentals=0),
            compiler_params=pltpu.CompilerParams(vmem_limit_bytes=10 * MIB),
        )(me, xa, xb, uh, ul, q, *so_far)

    out = finish(True, x0, x1, q_half)
    return finish(False, x2, x3, q_rest, out)


def solution(mesh):
    in_specs = (
        P(("rep", "rows"), None),
        P(("rep", "rows"), None),
        P(None, ("rep", "rows"), None),
        P(None, ("rep", "rows"), None),
        P("rep", None, None),
    )
    out_specs = P(("rep", "rows"), None)
    return jax.shard_map(local, mesh=mesh, in_specs=in_specs, out_specs=out_specs, check_vma=False)
```

time: 61.7 us -> 52.2 us (0.85)
  Pallas kernels: 32.6 us -> 22.6 us
  local copies, waits for them, and re-layouts: 6.3 us -> 0.01 us
  waiting for transfers between devices: 6.5 us -> 12.2 us
  starting transfers between devices: 15.9 us -> 16.9 us
    pallas_call x4 -> x2, Pallas kernels: 15.6 us -> 3.75 us  [finish(): pl.pallas_call(lambda *refs: k7(mine, *refs), out_shape=shape(rows, cols)...]
    unnamed x12 -> x2, local copies, waits for them, and re-layouts: 6.3 us -> 0.01 us
    ppermute x9, waiting for transfers between devices: 6.49 us -> 11.8 us  [along(): return lax.ppermute(value, 'rows', [(i, i ^ d << shift) for i in range(32)])]
    pallas_call x7 -> x11, Pallas kernels: 17 us -> 18.9 us  [call(): pl.pallas_call(kernel, out_shape=tuple(outs), in_specs=specs, out_specs=t...]
    ppermute x3, starting transfers between devices: 3.96 us -> 5.03 us  [to_other_core(): return lax.ppermute(value, 'rows', [(i, i ^ 1) for i in range(32)])]
  transfers between devices with their start and end apart: 12 -> 12, of which waited for: 5 -> 7; matrix products, arithmetic and copies ran while one was open for 0% -> 0% of each run, Pallas kernels for 29% -> 24%
where the time goes in v1:
time: 52.2 us; the launch traced here: 52.1 us
  Pallas kernels  22.6 us (43%)
  starting transfers between devices  16.9 us (32%)
  waiting for transfers between devices  12.2 us (23%)
    pallas_call x11, Pallas kernels, call(): pl.pallas_call(kernel, out_shape=tuple(outs), in_specs=specs, out_specs=t...  18.9 us
    ppermute x9, starting transfers between devices, along(): return lax.ppermute(value, 'rows', [(i, i ^ d << shift) for i in range(32)])  11.9 us
    ppermute x9, waiting for transfers between devices, along(): return lax.ppermute(value, 'rows', [(i, i ^ d << shift) for i in range(32)])  11.8 us
    ppermute x3, starting transfers between devices, to_other_core(): return lax.ppermute(value, 'rows', [(i, i ^ 1) for i in range(32)])  5.03 us
    pallas_call x2, Pallas kernels, finish(): pl.pallas_call(lambda *refs: k7(mine, *refs), out_shape=shape(rows, cols)...  3.75 us
  transfers between devices with their start and end apart: 12, of which 7 were waited for; matrix products, arithmetic and copies ran while one was open for 0% of the time, Pallas kernels for 24%

profile of v1, /device:TPU:1, one launch (start us, length us, event | category | flops | bytes accessed | tf_op | source)
XLA Modules:
  0.0 52.1 jit_solution(2159396033808143618)
XLA Ops:
  0.0 7.0 %project.1 = (f32[448,512]{1,0:T(8,128)S(1)}, bf16[320,1024]{1,0:T(8,128)(2,1)S(1)}, bf16[320,1024]{1,0:T(8,128)(2,1)S(1)}, bf16[1024,1024]{1,0:T(8,128)(2,1)S(1...) custom-call(s32[1]{0:T(128)} %bitcast.me_ref.refs_0_, ...), custom_call_target="tpu_custom_call" | custom-call | flops 7000000000 | bytes 9437184 | tf_op jit(solution)/shard_map/project/pallas_call | solution.py:48
  7.0 0.0 copy-start
  7.1 1.5 %collective-permute-start = (f32[448,512]{1,0:T(8,128)S(1)}, f32[448,512]{1,0:T(8,128)S(1)}, u32[]{:S(2)}, u32[]{:S(2)}) collective-permute-start(f32[448,512]{1,0:T(8,128)S(1)} %get-tuple-element.47.own), channel_id=1, source_target_pairs={{0,4},{4,0},{8,12},{12,8},{16,20},{20,16},{24,28},{28,24},{32,36},... | collective-permute-start | bytes 2752520 | tf_op jit(solution)/shard_map/ppermute | solution.py:253
  8.6 1.2 %project_own.1.g = f32[320,512]{1,0:T(8,128)S(1)} custom-call(bf16[320,1024]{1,0:T(8,128)(2,1)S(1)} %get-tuple-element.44.yh, bf16[320,1024]{1,0:T(8,128)(2,1)S(1)} %get-tuple-element.45.yl, f32[2,1024,512]{2,1,0:T(8,128)S(1)} %get-tuple-element.46.b.refs_2_), custom_call_target="tpu_custom_call" | custom-call | flops 2000000000 | bytes 3145728 | tf_op jit(solution)/shard_map/project_own/pallas_call | solution.py:48
  9.8 0.0 copy-done
  9.8 0.5 turn.1
  10.3 0.4 collective-permute-done.got
  10.7 0.7 %level4.1 = (f32[448,128]{1,0:T(8,128)S(1)}, f32[448,128]{1,0:T(8,128)S(1)}, f32[448,128]{1,0:T(8,128)S(1)}, f32[448,128]{1,0:T(8,128)S(1)}, f32[64,512]{1,0:T(8,128)S(1)}, /*index=5*/f32[64,512]{1,0:T(8,128)S(1)}) custom-call(s32[1]{0:T(128)} %bitcast.me_ref.refs_0_, f32[320,512]{1,0:T(8,128)S(1)} %project_own.1.g, f32[448,512]{1,0:T(8,128)S(1)} %get-tuple-element.47.own, ...), custom_call_target="tpu_custom_call" | custom-call | flops 1000000000 | bytes 4194304 | tf_op jit(solution)/shard_map/level4/pallas_call | solution.py:48
  11.3 2.9 %collective-permute-start.1 = (f32[448,128]{1,0:T(8,128)S(1)}, f32[448,128]{1,0:T(8,128)S(1)}, u32[]{:S(2)}, u32[]{:S(2)}) collective-permute-start(f32[448,128]{1,0:T(8,128)S(1)} %get-tuple-element.50), channel_id=1, source_target_pairs={{0,16},{4,20},{8,24},{12,28},{16,0},{20,4},{24,8},{28,12},{32,48},... | collective-permute-start | bytes 688136 | tf_op jit(solution)/shard_map/ppermute | solution.py:257
  14.2 0.3 collective-permute-start.2
  14.6 0.5 %collective-permute-start.3 = (f32[448,128]{1,0:T(8,128)S(1)}, f32[448,128]{1,0:T(8,128)S(1)}, u32[]{:S(2)}, u32[]{:S(2)}) collective-permute-start(f32[448,128]{1,0:T(8,128)S(1)} %get-tuple-element.52), channel_id=1, source_target_pairs={{0,24},{4,28},{8,16},{12,20},{16,8},{20,12},{24,0},{28,4},{32,56},... | collective-permute-start | bytes 688136 | tf_op jit(solution)/shard_map/ppermute | solution.py:257
  15.1 0.9 %collective-permute-start.10 = (f32[64,512]{1,0:T(8,128)S(1)}, f32[64,512]{1,0:T(8,128)S(1)}, u32[]{:S(2)}, u32[]{:S(2)}) collective-permute-start(f32[64,512]{1,0:T(8,128)S(1)} %get-tuple-element.74), channel_id=1, source_target_pairs={{0,4},{4,0},{8,12},{12,8},{16,20},{20,16},{24,28},{28,24},{32,36},... | collective-permute-start | bytes 393224 | tf_op jit(solution)/shard_map/ppermute | solution.py:253
  16.0 2.0 %leaf.4.refs_1_ = f32[1024,256]{1,0:T(8,128)S(1)} custom-call(bf16[1024,1024]{1,0:T(8,128)(2,1)S(1)} %get-tuple-element.53.refs_0_, bf16[1024,1024]{1,0:T(8,128)(2,1)S(1)} %get-tuple-element.54.refs_1_, f32[2,1024,512]{2,1,0:T(8,128)S(1)} %get-tuple-element.46.b.refs_2_, bf16[1024,320]{1,0:T(8,128)(2,1)S(1)} %get-tuple-element.56.refs_3_, ...), custom_call_target="tpu_custom_call" | custom-call | flops 2000000000 | bytes 6291456 | tf_op jit(solution)/shard_map/leaf/pallas_call | solution.py:48
  18.0 2.0 %leaf.5.refs_2_ = f32[1024,256]{1,0:T(8,128)S(1)} custom-call(bf16[1024,1024]{1,0:T(8,128)(2,1)S(1)} %get-tuple-element.53.refs_0_, bf16[1024,1024]{1,0:T(8,128)(2,1)S(1)} %get-tuple-element.54.refs_1_, f32[2,1024,512]{2,1,0:T(8,128)S(1)} %get-tuple-element.46.b.refs_2_, bf16[1024,320]{1,0:T(8,128)(2,1)S(1)} %get-tuple-element.56.refs_3_, ...), custom_call_target="tpu_custom_call" | custom-call | flops 2000000000 | bytes 6291456 | tf_op jit(solution)/shard_map/leaf/pallas_call | solution.py:48
  20.0 0.0 collective-permute-done.1.g2
  20.1 4.8 %collective-permute-done.2.g1 = f32[448,128]{1,0:T(8,128)S(1)} collective-permute-done((f32[448,128]{1,0:T(8,128)S(1)}, f32[448,128]{1,0:T(8,128)S(1)}, u32[]{:S(2)}, u32[]{:S(2)}) %collective-permute-start.2) | collective-permute-done | bytes 229408 | tf_op jit(solution)/shard_map/ppermute | solution.py:257
  24.9 0.5 collective-permute-done.3.g3
  25.4 0.8 %levels32.1 = (f32[192,128]{1,0:T(8,128)S(1)}, f32[4,64,128]{2,1,0:T(8,128)S(1)}, f32[2,64,128]{2,1,0:T(8,128)S(1)}) custom-call(s32[1]{0:T(128)} %bitcast.me_ref.refs_0_, f32[448,128]{1,0:T(8,128)S(1)} %get-tuple-element.59.g0, f32[448,128]{1,0:T(8,128)S(1)} %collective-permute-done.1.g2, f32[448,128]{1,0:T(8,128)S(1)} %collective-permute-done.2.g1, ...), custom_call_target="tpu_custom_call" | custom-call | flops 100000000 | bytes 1048576 | tf_op jit(solution)/shard_map/levels32/pallas_call | solution.py:48
  26.2 3.8 %collective-permute-start.4 = (f32[192,128]{1,0:T(8,128)S(1)}, f32[192,128]{1,0:T(8,128)S(1)}, u32[]{:S(2)}, u32[]{:S(2)}) collective-permute-start(f32[192,128]{1,0:T(8,128)S(1)} %get-tuple-element.64.s0), channel_id=1, source_target_pairs={{0,64},{4,68},{8,72},{12,76},{16,80},{20,84},{24,88},{28,92},{32,9... | collective-permute-start | bytes 294920 | tf_op jit(solution)/shard_map/ppermute | solution.py:257
  30.0 0.7 %collective-permute-start.5 = (f32[192,128]{1,0:T(8,128)S(1)}, f32[192,128]{1,0:T(8,128)S(1)}, u32[]{:S(2)}, u32[]{:S(2)}) collective-permute-start(f32[192,128]{1,0:T(8,128)S(1)} %get-tuple-element.64.s0), channel_id=1, source_target_pairs={{0,32},{4,36},{8,40},{12,44},{16,48},{20,52},{24,56},{28,60},{32,0... | collective-permute-start | bytes 294920 | tf_op jit(solution)/shard_map/ppermute | solution.py:257
  30.7 0.0 collective-permute-start.6
  30.7 0.0 collective-permute-done.10.refs_5_
  30.7 2.0 %leaf.6.refs_1_ = f32[1024,256]{1,0:T(8,128)S(1)} custom-call(bf16[1024,1024]{1,0:T(8,128)(2,1)S(1)} %get-tuple-element.53.refs_0_, bf16[1024,1024]{1,0:T(8,128)(2,1)S(1)} %get-tuple-element.54.refs_1_, f32[2,1024,512]{2,1,0:T(8,128)S(1)} %get-tuple-element.46.b.refs_2_, bf16[1024,320]{1,0:T(8,128)(2,1)S(1)} %get-tuple-element.56.refs_3_, ...), custom_call_target="tpu_custom_call" | custom-call | flops 2000000000 | bytes 6291456 | tf_op jit(solution)/shard_map/leaf/pallas_call | solution.py:48
  32.7 0.0 collective-permute-done.4.s2
  32.7 2.0 %collective-permute-done.5.s1 = f32[192,128]{1,0:T(8,128)S(1)} collective-permute-done((f32[192,128]{1,0:T(8,128)S(1)}, f32[192,128]{1,0:T(8,128)S(1)}, u32[]{:S(2)}, u32[]{:S(2)}) %collective-permute-start.5) | collective-permute-done | bytes 98336 | tf_op jit(solution)/shard_map/ppermute | solution.py:257
  34.8 0.6 %collective-permute-done.6.s3 = f32[192,128]{1,0:T(8,128)S(1)} collective-permute-done((f32[192,128]{1,0:T(8,128)S(1)}, f32[192,128]{1,0:T(8,128)S(1)}, u32[]{:S(2)}, u32[]{:S(2)}) %collective-permute-start.6) | collective-permute-done | bytes 98336 | tf_op jit(solution)/shard_map/ppermute | solution.py:257
  35.4 0.6 %levels10.1 = (f32[256,128]{1,0:T(8,128)S(1)}, f32[256,128]{1,0:T(8,128)S(1)}, f32[256,128]{1,0:T(8,128)S(1)}, f32[256,128]{1,0:T(8,128)S(1)}) custom-call(s32[1]{0:T(128)} %bitcast.me_ref.refs_0_, f32[192,128]{1,0:T(8,128)S(1)} %get-tuple-element.64.s0, f32[192,128]{1,0:T(8,128)S(1)} %collective-permute-done.4.s2, ...), custom_call_target="tpu_custom_call" | custom-call | flops 100000000 | bytes 1048576 | tf_op jit(solution)/shard_map/levels10/pallas_call | solution.py:48
  36.0 2.8 %collective-permute-start.7 = (f32[256,128]{1,0:T(8,128)S(1)}, f32[256,128]{1,0:T(8,128)S(1)}, u32[]{:S(2)}, u32[]{:S(2)}) collective-permute-start(f32[256,128]{1,0:T(8,128)S(1)} %get-tuple-element.71), channel_id=1, source_target_pairs={{0,16},{4,20},{8,24},{12,28},{16,0},{20,4},{24,8},{28,12},{32,48},... | collective-permute-start | bytes 393224 | tf_op jit(solution)/shard_map/ppermute | solution.py:257
  38.8 0.3 collective-permute-start.8
  39.1 0.5 %collective-permute-start.9 = (f32[256,128]{1,0:T(8,128)S(1)}, f32[256,128]{1,0:T(8,128)S(1)}, u32[]{:S(2)}, u32[]{:S(2)}) collective-permute-start(f32[256,128]{1,0:T(8,128)S(1)} %get-tuple-element.73), channel_id=1, source_target_pairs={{0,24},{4,28},{8,16},{12,20},{16,8},{20,12},{24,0},{28,4},{32,56},... | collective-permute-start | bytes 393224 | tf_op jit(solution)/shard_map/ppermute | solution.py:257
  39.6 2.0 %leaf.7.refs_2_ = f32[1024,256]{1,0:T(8,128)S(1)} custom-call(bf16[1024,1024]{1,0:T(8,128)(2,1)S(1)} %get-tuple-element.53.refs_0_, bf16[1024,1024]{1,0:T(8,128)(2,1)S(1)} %get-tuple-element.54.refs_1_, f32[2,1024,512]{2,1,0:T(8,128)S(1)} %get-tuple-element.46.b.refs_2_, bf16[1024,320]{1,0:T(8,128)(2,1)S(1)} %get-tuple-element.56.refs_3_, ...), custom_call_target="tpu_custom_call" | custom-call | flops 2000000000 | bytes 6291456 | tf_op jit(solution)/shard_map/leaf/pallas_call | solution.py:48
  41.7 0.0 collective-permute-done.7.r2
  41.7 1.6 %collective-permute-done.8.r1 = f32[256,128]{1,0:T(8,128)S(1)} collective-permute-done((f32[256,128]{1,0:T(8,128)S(1)}, f32[256,128]{1,0:T(8,128)S(1)}, u32[]{:S(2)}, u32[]{:S(2)}) %collective-permute-start.8) | collective-permute-done | bytes 131104 | tf_op jit(solution)/shard_map/ppermute | solution.py:257
  43.2 2.3 %collective-permute-done.9.r3 = f32[256,128]{1,0:T(8,128)S(1)} collective-permute-done((f32[256,128]{1,0:T(8,128)S(1)}, f32[256,128]{1,0:T(8,128)S(1)}, u32[]{:S(2)}, u32[]{:S(2)}) %collective-permute-start.9) | collective-permute-done | bytes 131104 | tf_op jit(solution)/shard_map/ppermute | solution.py:257
  45.5 0.1 assemble.1.refs_5_
  45.6 2.6 %collective-permute-start.11 = (f32[256,512]{1,0:T(8,128)S(1)}, f32[256,512]{1,0:T(8,128)S(1)}, u32[]{:S(2)}, u32[]{:S(2)}) collective-permute-start(f32[256,512]{1,0:T(8,128)S(1)} %assemble.1.refs_5_), channel_id=1, source_target_pairs={{0,4},{4,0},{8,12},{12,8},{16,20},{20,16},{24,28},{28,24},{32,36},... | collective-permute-start | bytes 1572872 | tf_op jit(solution)/shard_map/ppermute | solution.py:253
  48.2 1.9 %finish.2.refs_6_ = f32[1024,1024]{1,0:T(8,128)} custom-call(s32[1]{0:T(128)} %bitcast.me_ref.refs_0_, f32[1024,256]{1,0:T(8,128)S(1)} %leaf.4.refs_1_, f32[1024,256]{1,0:T(8,128)S(1)} %leaf.5.refs_2_, bf16[1024,320]{1,0:T(8,128)(2,1)S(1)} %get-tuple-element.56.refs_3_, bf16[1024,320]{1,0:T(8,128)(2,1)S(1)} %get-tuple-element.57.refs_4_, ...), custom_call_target="tpu_custom_call" | custom-call | flops 1000000000 | bytes 5242880 | tf_op jit(solution)/shard_map/finish/pallas_call | solution.py:324
  50.1 0.0 collective-permute-done.11.refs_5_
  50.1 1.9 %finish.3 = f32[1024,1024]{1,0:T(8,128)} custom-call(s32[1]{0:T(128)} %bitcast.me_ref.refs_0_, f32[1024,256]{1,0:T(8,128)S(1)} %leaf.6.refs_1_, f32[1024,256]{1,0:T(8,128)S(1)} %leaf.7.refs_2_, bf16[1024,320]{1,0:T(8,128)(2,1)S(1)} %get-tuple-element.56.refs_3_, bf16[1024,320]{1,0:T(8,128)(2,1)S(1)} %get-tuple-element.57.refs_4_, ...), custom_call_target="tpu_custom_call", output_to_operand_aliasing={{}: (6, {})} | custom-call | flops 1000000000 | bytes 5242880 | tf_op jit(solution)/shard_map/finish/pallas_call | solution.py:324
Async XLA Ops:
  7.0 2.8 %copy-start = (f32[5,1024,64]{1,2,0:T(8,128)S(1)}, f32[5,1024,64]{1,2,0:T(8,128)}, u32[]{:S(2)}) copy-start(f32[5,1024,64]{1,2,0:T(8,128)} %param.7) | copy-start | bytes 3932164
  7.1 3.6 %collective-permute-start = (f32[448,512]{1,0:T(8,128)S(1)}, f32[448,512]{1,0:T(8,128)S(1)}, u32[]{:S(2)}, u32[]{:S(2)}) collective-permute-start(f32[448,512]{1,0:T(8,128)S(1)} %get-tuple-element.47.own), channel_id=1, source_target_pairs={{0,4},{4,0},{8,12},{12,8},{16,20},{20,16},{24,28},{28,24},{32,36},... | collective-permute-start | bytes 2752520 | tf_op jit(solution)/shard_map/ppermute | solution.py:253
  11.3 8.7 %collective-permute-start.1 = (f32[448,128]{1,0:T(8,128)S(1)}, f32[448,128]{1,0:T(8,128)S(1)}, u32[]{:S(2)}, u32[]{:S(2)}) collective-permute-start(f32[448,128]{1,0:T(8,128)S(1)} %get-tuple-element.50), channel_id=1, source_target_pairs={{0,16},{4,20},{8,24},{12,28},{16,0},{20,4},{24,8},{28,12},{32,48},... | collective-permute-start | bytes 688136 | tf_op jit(solution)/shard_map/ppermute | solution.py:257
  14.2 10.6 %collective-permute-start.2 = (f32[448,128]{1,0:T(8,128)S(1)}, f32[448,128]{1,0:T(8,128)S(1)}, u32[]{:S(2)}, u32[]{:S(2)}) collective-permute-start(f32[448,128]{1,0:T(8,128)S(1)} %get-tuple-element.51), channel_id=1, source_target_pairs={{0,8},{4,12},{8,0},{12,4},{16,24},{20,28},{24,16},{28,20},{32,40},... | collective-permute-start | bytes 688136 | tf_op jit(solution)/shard_map/ppermute | solution.py:257
  14.6 10.8 %collective-permute-start.3 = (f32[448,128]{1,0:T(8,128)S(1)}, f32[448,128]{1,0:T(8,128)S(1)}, u32[]{:S(2)}, u32[]{:S(2)}) collective-permute-start(f32[448,128]{1,0:T(8,128)S(1)} %get-tuple-element.52), channel_id=1, source_target_pairs={{0,24},{4,28},{8,16},{12,20},{16,8},{20,12},{24,0},{28,4},{32,56},... | collective-permute-start | bytes 688136 | tf_op jit(solution)/shard_map/ppermute | solution.py:257
  15.1 15.6 %collective-permute-start.10 = (f32[64,512]{1,0:T(8,128)S(1)}, f32[64,512]{1,0:T(8,128)S(1)}, u32[]{:S(2)}, u32[]{:S(2)}) collective-permute-start(f32[64,512]{1,0:T(8,128)S(1)} %get-tuple-element.74), channel_id=1, source_target_pairs={{0,4},{4,0},{8,12},{12,8},{16,20},{20,16},{24,28},{28,24},{32,36},... | collective-permute-start | bytes 393224 | tf_op jit(solution)/shard_map/ppermute | solution.py:253
  26.2 6.5 %collective-permute-start.4 = (f32[192,128]{1,0:T(8,128)S(1)}, f32[192,128]{1,0:T(8,128)S(1)}, u32[]{:S(2)}, u32[]{:S(2)}) collective-permute-start(f32[192,128]{1,0:T(8,128)S(1)} %get-tuple-element.64.s0), channel_id=1, source_target_pairs={{0,64},{4,68},{8,72},{12,76},{16,80},{20,84},{24,88},{28,92},{32,9... | collective-permute-start | bytes 294920 | tf_op jit(solution)/shard_map/ppermute | solution.py:257
  30.0 4.8 %collective-permute-start.5 = (f32[192,128]{1,0:T(8,128)S(1)}, f32[192,128]{1,0:T(8,128)S(1)}, u32[]{:S(2)}, u32[]{:S(2)}) collective-permute-start(f32[192,128]{1,0:T(8,128)S(1)} %get-tuple-element.64.s0), channel_id=1, source_target_pairs={{0,32},{4,36},{8,40},{12,44},{16,48},{20,52},{24,56},{28,60},{32,0... | collective-permute-start | bytes 294920 | tf_op jit(solution)/shard_map/ppermute | solution.py:257
  30.7 4.7 %collective-permute-start.6 = (f32[192,128]{1,0:T(8,128)S(1)}, f32[192,128]{1,0:T(8,128)S(1)}, u32[]{:S(2)}, u32[]{:S(2)}) collective-permute-start(f32[192,128]{1,0:T(8,128)S(1)} %get-tuple-element.64.s0), channel_id=1, source_target_pairs={{0,96},{4,100},{8,104},{12,108},{16,112},{20,116},{24,120},{28,124... | collective-permute-start | bytes 294920 | tf_op jit(solution)/shard_map/ppermute | solution.py:257
  36.0 5.7 %collective-permute-start.7 = (f32[256,128]{1,0:T(8,128)S(1)}, f32[256,128]{1,0:T(8,128)S(1)}, u32[]{:S(2)}, u32[]{:S(2)}) collective-permute-start(f32[256,128]{1,0:T(8,128)S(1)} %get-tuple-element.71), channel_id=1, source_target_pairs={{0,16},{4,20},{8,24},{12,28},{16,0},{20,4},{24,8},{28,12},{32,48},... | collective-permute-start | bytes 393224 | tf_op jit(solution)/shard_map/ppermute | solution.py:257
  38.8 4.4 %collective-permute-start.8 = (f32[256,128]{1,0:T(8,128)S(1)}, f32[256,128]{1,0:T(8,128)S(1)}, u32[]{:S(2)}, u32[]{:S(2)}) collective-permute-start(f32[256,128]{1,0:T(8,128)S(1)} %get-tuple-element.72), channel_id=1, source_target_pairs={{0,8},{4,12},{8,0},{12,4},{16,24},{20,28},{24,16},{28,20},{32,40},... | collective-permute-start | bytes 393224 | tf_op jit(solution)/shard_map/ppermute | solution.py:257
  39.1 6.4 %collective-permute-start.9 = (f32[256,128]{1,0:T(8,128)S(1)}, f32[256,128]{1,0:T(8,128)S(1)}, u32[]{:S(2)}, u32[]{:S(2)}) collective-permute-start(f32[256,128]{1,0:T(8,128)S(1)} %get-tuple-element.73), channel_id=1, source_target_pairs={{0,24},{4,28},{8,16},{12,20},{16,8},{20,12},{24,0},{28,4},{32,56},... | collective-permute-start | bytes 393224 | tf_op jit(solution)/shard_map/ppermute | solution.py:257
  45.6 4.5 %collective-permute-start.11 = (f32[256,512]{1,0:T(8,128)S(1)}, f32[256,512]{1,0:T(8,128)S(1)}, u32[]{:S(2)}, u32[]{:S(2)}) collective-permute-start(f32[256,512]{1,0:T(8,128)S(1)} %assemble.1.refs_5_), channel_id=1, source_target_pairs={{0,4},{4,0},{8,12},{12,8},{16,20},{20,16},{24,28},{28,24},{32,36},... | collective-permute-start | bytes 1572872 | tf_op jit(solution)/shard_map/ppermute | solution.py:253

commit v2 on v1

v2 whole, which is shorter than its diff:
```python
import jax
import jax.numpy as jnp
from jax import lax
from jax.experimental import pallas as pl
from jax.experimental.pallas import tpu as pltpu
from jax.sharding import PartitionSpec as P

R = 64
F32, BF16 = jnp.float32, jnp.bfloat16
MIB = 1 << 20


def split(a):
    high = a.astype(BF16)
    return high, (a - high.astype(F32)).astype(BF16)


def dot(a, b, dims=((1,), (0,))):
    return lax.dot_general(a, b, (dims, ((), ())), preferred_element_type=F32)


def mm3(a, b):
    (ah, al), (bh, bl) = a, b
    return dot(jnp.concatenate([ah, al, ah], 1), jnp.concatenate([bh, bh, bl], 0))


def mm(a, b):
    return mm3(split(a), split(b))


def bits(me_ref):
    me = me_ref[0]
    return me, [lax.rem(me >> b, 2) for b in range(5)]


VM = pl.BlockSpec(memory_space=pltpu.VMEM)
SM = pl.BlockSpec(memory_space=pltpu.SMEM)
HB = pl.BlockSpec(memory_space=pltpu.HBM)


def shape(*dims, dtype=F32):
    return jax.ShapeDtypeStruct(dims, dtype)


def call(kernel, ins, outs, specs, name, flops, moved, limit, scratch=(), grid=None, aliases=None):
    out_specs = [VM] * len(outs) if grid is None else grid[1]
    extra = {} if grid is None else dict(grid=grid[0])
    return pl.pallas_call(
        kernel,
        out_shape=tuple(outs),
        in_specs=specs,
        out_specs=tuple(out_specs),
        scratch_shapes=list(scratch),
        name=name,
        input_output_aliases=aliases or {},
        cost_estimate=pl.CostEstimate(flops=flops, bytes_accessed=1000, transcendentals=0),
        compiler_params=pltpu.CompilerParams(vmem_limit_bytes=limit * MIB),
        **extra,
    )(*ins)


def pack(w):
    low = jnp.concatenate([w[: 2 * R, R : 2 * R], w[:R, :R]], 0)
    return jnp.concatenate([w[: 3 * R, 2 * R : 3 * R], low], 1)


def k0(me_ref, vt_hbm, ut_hbm, cores_hbm, w_ref, packed, vh_ref, vl_ref, sel, vt, ut, sems):
    me, bit = bits(me_ref)
    where = [15 + (me >> 1), 7 + (me >> 2), 3 + (me >> 3), 1 + (me >> 4), 0]
    get_v = pltpu.make_async_copy(vt_hbm, vt, sems.at[0])
    get_u = pltpu.make_async_copy(ut_hbm, ut, sems.at[1])
    picks = [pltpu.make_async_copy(cores_hbm.at[i], sel.at[k], sems.at[2 + k]) for k, i in enumerate(where)]
    for copy in [get_v, get_u, *picks]:
        copy.start()
    get_v.wait()
    get_u.wait()
    vh, vl = split(vt[...])
    vh_ref[...] = vh
    vl_ref[...] = vl
    vh, vl = vh[: 4 * R], vl[: 4 * R]
    uh, ul = split(ut[R:, :])
    w = dot(jnp.concatenate([vh, vl, vh], 1), jnp.concatenate([uh, uh, ul], 1), ((1,), (1,)))
    w_ref[...] = w
    packed[...] = pack(w)
    for copy in picks:
        copy.wait()


def k1(vh, vl, l, yh, yl, lh_ref, ll_ref):
    lh, ll = split(l[...])
    lh_ref[...] = lh
    ll_ref[...] = ll
    yh[...], yl[...] = split(mm3((vh[...], vl[...]), (lh, ll)))


def k2(mine, me_ref, yh, yl, b, g):
    me, bit = bits(me_ref)
    half = g.shape[1]
    at = pl.ds(pl.multiple_of((bit[0] if mine else 1 - bit[0]) * half, half), half)
    g[...] = mm3((yh[...], yl[...]), split(b[:, at]))


def kw(w, w_got, far, far_got, packed, packed_got):
    packed[...] = pack(w[...]) + pack(w_got[...])
    packed_got[...] = far[...] + far_got[...]


def kn(packed, packed_got, out):
    both = packed[:, R:] + packed_got[:, R:]
    out[...] = jnp.concatenate([both[: 3 * R // 2], both[3 * R // 2 :]], 1)


def rows_of(q, bit, own):
    at = bit if own else 1 - bit
    return q[pl.ds(pl.multiple_of(at * R, R), R), :]


def stack(p, first, second, bit):
    p[pl.ds(pl.multiple_of((1 - bit) * R, R), R), :] = first
    p[pl.ds(pl.multiple_of(bit * R, R), R), :] = second


def own_share(core, bit, own, other):
    both = jnp.concatenate([rows_of(core, bit, True), rows_of(core, bit, False)], 0)
    full = mm(jnp.concatenate([own, other], 1), both)
    return jnp.where(bit == 0, full[:, R:], full[:, :R])


def k3(me_ref, g, got, w, w_got, packed, packed_got, sel, m0, m2, m1, m3, p3, q_mine, q_other, p, q, a):
    me, bit = bits(me_ref)
    x = lax.rem(me >> 1, 4)
    c = bit[0]
    share = own_share(sel.at[1], bit[1], packed[:, :R], packed_got[:, :R])
    stack(p, g[4 * R :, :], got[4 * R :, :], c)
    q[...] = mm(sel[0], p[...])
    mine, theirs = rows_of(q, c, True), rows_of(q, c, False)
    q_mine[...] = mine
    q_other[...] = theirs
    wide = jnp.concatenate([w[:, 3 * R :], w_got[:, 3 * R :]], 1)
    left = g[: 4 * R, :] + got[: 4 * R, :] - mm(wide, jnp.concatenate([mine, theirs], 0))
    third = left[3 * R :]
    p3[...] = third
    a[...] = left[: 3 * R] - mm(share, third)
    for d, out in ((2, m2), (1, m1), (3, m3), (0, m0)):
        out[...] = a[:, pl.ds(pl.multiple_of((x ^ d) * 2 * R, 2 * R), 2 * R)]


def unfold(w):
    return jnp.concatenate([w[:, :R], w[:, R:]], 0)


def k4(me_ref, m0, g2, g1, g3, w, w_got, sel, z, q2, p, q):
    me, bit = bits(me_ref)
    own, other = unfold(w), unfold(w_got)
    near = m0[...] + g1[...]
    far = g2[...] + g3[...]
    stack(p, near[2 * R :], far[2 * R :], bit[2])
    q[...] = mm(sel[2], p[...])
    mine, theirs = rows_of(q, bit[2], True), rows_of(q, bit[2], False)
    q2[0] = mine
    q2[1] = theirs
    wide = jnp.concatenate([own[: 2 * R], other[: 2 * R]], 1)
    z[: 2 * R, :] = near[: 2 * R] + far[: 2 * R] - mm(wide, jnp.concatenate([mine, theirs], 0))
    last = own[2 * R :] + other[2 * R :]
    z[2 * R :, :] = jnp.concatenate([last[: R // 2], last[R // 2 :]], 1)


def k5(me_ref, s, got, sel, q1, a0, p, q):
    me, bit = bits(me_ref)
    stack(p, s[R : 2 * R, :], got[R : 2 * R, :], bit[3])
    q[...] = mm(sel[3], p[...])
    mine, theirs = rows_of(q, bit[3], True), rows_of(q, bit[3], False)
    q1[...] = mine
    wide = jnp.concatenate([unfold(s[2 * R :, :]), unfold(got[2 * R :, :])], 1)
    a0[...] = s[:R, :] + got[:R, :] - mm(wide, jnp.concatenate([mine, theirs], 0))


def kr(me_ref, a0, got, sel, q1, q2, r0, r2, r1, r3, p):
    me, bit = bits(me_ref)
    stack(p, a0[...], got[...], bit[4])
    top = mm(rows_of(sel.at[4], bit[4], True), p[...])
    for k, out in ((1, r2), (0, r1), (1, r3), (0, r0)):
        out[:R, :] = top
        out[R : 2 * R, :] = q1[...]
        out[2 * R :, :] = q2[k]


def kq(me_ref, own, got, sel, q, p):
    me, bit = bits(me_ref)
    stack(p, own[...], got[...], bit[1])
    q[...] = mm(rows_of(sel.at[1], bit[1], True), p[...])


def k6(me_ref, r0, r2, r1, r3, q3, q_half):
    me, bit = bits(me_ref)
    x = lax.rem(me >> 1, 4)
    for d, r in ((0, r0), (1, r1), (2, r2), (3, r3)):
        q_half[: 3 * R, pl.ds(pl.multiple_of((x ^ d) * 2 * R, 2 * R), 2 * R)] = r[...]
    q_half[3 * R :, :] = q3[...]


def ku(ut, uh_ref, ul_ref):
    uh_ref[...], ul_ref[...] = split(ut[...].T)


def kl(piece, me_ref, lh, ll, b, uh, ul, q4, x):
    me, bit = bits(me_ref)
    n = x.shape[1]
    at = pl.multiple_of((bit[0] if piece < 2 else 1 - bit[0]) * 2 * n + piece % 2 * n, n)
    bh, bl = split(b[:, pl.ds(at, n)])
    qh, ql = split(q4[:, piece % 2 * n : piece % 2 * n + n])
    right = jnp.concatenate([bh, bh, bl], 0)
    below = jnp.concatenate([qh, qh, ql], 0)
    for k in range(4):
        r = slice(k * 256, k * 256 + 256)
        u4h, u4l = uh[r, 4 * R :], ul[r, 4 * R :]
        x[r, :] = dot(jnp.concatenate([lh[r, :], ll[r, :], lh[r, :]], 1), right) - dot(
            jnp.concatenate([u4h, u4l, u4h], 1), below
        )


def k7(mine, me_ref, xa, xb, uh, ul, q, *rest):
    out, buf, sems = rest[-3:]
    me, bit = bits(me_ref)
    half = q.shape[1]
    at = pl.multiple_of((bit[0] if mine else 1 - bit[0]) * half, half)
    qh, ql = split(q[...])
    right = jnp.concatenate([qh, qh, ql], 0)
    copies = []
    for k in range(4):
        r = slice(k * 256, k * 256 + 256)
        u3h, u3l = uh[r, : 4 * R], ul[r, : 4 * R]
        buf[r, :] = jnp.concatenate([xa[r, :], xb[r, :]], 1) - dot(jnp.concatenate([u3h, u3l, u3h], 1), right)
        copies.append(
            pltpu.make_async_copy(
                buf.at[pl.ds(k * 256, 256)], out.at[pl.ds(k * 256, 256), pl.ds(at, half)], sems.at[k]
            )
        )
        copies[-1].start()
    for copy in copies:
        copy.wait()


def to_other_core(value):
    return lax.ppermute(value, "rows", [(i, i ^ 1) for i in range(32)])


def along(value, shift, d):
    return lax.ppermute(value, "rows", [(i, i ^ (d << shift)) for i in range(32)])


def spread(values, shift):
    return [values[0]] + [along(values[k], shift, d) for k, d in ((1, 2), (2, 1), (3, 3))]


def local(right_side, leaf_inverse, left_factors, right_factors, cores):
    me = lax.axis_index("rows").astype(jnp.int32).reshape(1)
    rows, cols = right_side.shape
    half, eighth = cols // 2, cols // 8
    vt = right_factors.transpose(0, 2, 1).reshape(5 * R, rows)
    ut = left_factors.transpose(0, 2, 1).reshape(5 * R, rows)
    in_hbm = [pltpu.with_memory_space_constraint(v, pltpu.HBM) for v in (vt, ut, cores)]
    tall = shape(5 * R, rows, dtype=BF16)
    square = shape(rows, rows, dtype=BF16)
    after = lax.optimization_barrier

    w, packed, vh, vl, sel = call(
        k0, (me, *in_hbm), [shape(4 * R, 4 * R), shape(3 * R, 2 * R), tall, tall, shape(5, 2 * R, 2 * R)],
        [SM, HB, HB, HB], "couple", 1000, 3 * MIB, 12,
        scratch=[pltpu.VMEM((5 * R, rows), F32)] * 2 + [pltpu.SemaphoreType.DMA((8,))],
    )
    w_got = to_other_core(w)
    far = along(packed, 1, 1)
    yh, yl, lh, ll = call(
        k1, (vh, vl, leaf_inverse), [tall, tall, square, square], [VM] * 3, "project", 1000, 4 * MIB, 20,
    )

    def image(mine, yh_):
        return call(
            lambda *refs: k2(mine, *refs), (me, yh_, yl, right_side), [shape(5 * R, half)], [SM] + [VM] * 3,
            "columns", 10**10 if mine else 1000, 3 * MIB, 12,
        )[0]

    sent = image(False, yh)
    got = to_other_core(sent)
    far = after((far, sent))[0]
    far_got = to_other_core(far)
    g = image(True, after((yh, sent))[0])
    uh, ul = call(
        ku, (after((ut, g))[0],), [shape(rows, 5 * R, dtype=BF16)] * 2, [VM], "turn", 10, 3 * MIB, 8,
    )
    packed, packed_got = call(
        kw, (w, w_got, far, after((far_got, g))[0]), [shape(3 * R, 2 * R)] * 2, [VM] * 4, "chip", 10, MIB, 4,
    )
    *messages, p3, q4_mine, q4_other = call(
        k3, (me, g, got, w, w_got, packed, packed_got, sel),
        [shape(3 * R, eighth)] * 4 + [shape(R, half)] * 3,
        [SM] + [VM] * 7, "level4", 1000, 4 * MIB, 10,
        scratch=[pltpu.VMEM((2 * R, half), F32)] * 2 + [pltpu.VMEM((3 * R, half), F32)],
    )
    (w_next,) = call(
        kn, (packed, after((packed_got, p3))[0]), [shape(3 * R // 2, 2 * R)], [VM] * 2, "chips", 10, MIB, 4,
    )
    w_far = along(w_next, 1, 3)

    def leaf(piece, q4):
        return call(
            lambda *refs: kl(piece, *refs), (me, lh, ll, right_side, uh, ul, q4), [shape(rows, half // 2)],
            [SM] + [VM] * 6, "leaf", 1000, 6 * MIB, 12,
        )[0]

    x0 = leaf(0, q4_mine)
    q4_back = to_other_core(after((q4_other, x0))[0])
    got, x0 = after((spread(messages, 1), x0))
    small = [pltpu.VMEM((2 * R, eighth), F32)]
    z, q2 = call(
        k4, (me, *got, w_next, w_far, sel), [shape(5 * R // 2, eighth), shape(2, R, eighth)],
        [SM] + [VM] * 7, "level2", 1000, MIB, 8, scratch=small * 2,
    )
    got, x1 = after((along(z, 3, 1), leaf(1, after((q4_mine, q2))[0])))
    q1, a0 = call(
        k5, (me, z, got, sel), [shape(R, eighth)] * 2, [SM] + [VM] * 3, "level1", 1000, MIB, 8, scratch=small * 2,
    )
    p3_got = along(after((p3, q1))[0], 1, 1)
    got, x2 = after((along(a0, 3, 3), leaf(2, after((q4_back, q1))[0])))
    back = call(
        kr, (me, a0, got, sel, q1, q2), [shape(3 * R, eighth)] * 4, [SM] + [VM] * 5, "level0", 1000, MIB, 8,
        scratch=small,
    )
    (q3,) = call(
        kq, (me, p3, p3_got, sel), [shape(R, half)], [SM] + [VM] * 3, "level3", 1000, MIB, 8,
        scratch=[pltpu.VMEM((2 * R, half), F32)],
    )
    got, x3, q3 = after((spread(back, 1), leaf(3, after((q4_back, back[0]))[0]), q3))
    (q_half,) = call(k6, (me, *got, q3), [shape(4 * R, half)], [SM] + [VM] * 5, "assemble", 10, MIB, 8)
    q_rest = to_other_core(q_half)

    def finish(mine, xa, xb, q, *so_far):
        return pl.pallas_call(
            lambda *refs: k7(mine, *refs),
            out_shape=shape(rows, cols),
            in_specs=[SM] + [VM] * 5 + [HB] * len(so_far),
            out_specs=HB,
            scratch_shapes=[pltpu.VMEM((rows, half), F32), pltpu.SemaphoreType.DMA((4,))],
            name="finish",
            input_output_aliases={6: 0} if so_far else {},
            cost_estimate=pl.CostEstimate(flops=10**9, bytes_accessed=5 * MIB, transcendentals=0),
            compiler_params=pltpu.CompilerParams(vmem_limit_bytes=10 * MIB),
        )(me, xa, xb, uh, ul, q, *so_far)

    out = finish(True, x0, x1, q_half)
    return finish(False, x2, x3, q_rest, out)


def solution(mesh):
    in_specs = (
        P(("rep", "rows"), None),
        P(("rep", "rows"), None),
        P(None, ("rep", "rows"), None),
        P(None, ("rep", "rows"), None),
        P("rep", None, None),
    )
    out_specs = P(("rep", "rows"), None)
    return jax.shard_map(local, mesh=mesh, in_specs=in_specs, out_specs=out_specs, check_vma=False)
```

time: 52.2 us -> 48.4 us (0.927)
  waiting for transfers between devices: 12.2 us -> 3.83 us
  starting transfers between devices: 16.9 us -> 22.5 us
  Pallas kernels: 22.6 us -> 21.6 us
    ppermute x9 -> x11, waiting for transfers between devices: 11.8 us -> 3.3 us  [along(): return lax.ppermute(value, 'rows', [(i, i ^ d << shift) for i in range(32)])]
    ppermute x9 -> x11, starting transfers between devices: 11.9 us -> 16.7 us  [along(): return lax.ppermute(value, 'rows', [(i, i ^ d << shift) for i in range(32)])]
    pallas_call x11 -> x17, Pallas kernels: 18.9 us -> 17.9 us  [call(): pl.pallas_call(kernel, out_shape=tuple(outs), in_specs=specs, out_specs=t...]
    ppermute x3 -> x5, starting transfers between devices: 5.03 us -> 5.74 us  [to_other_core(): return lax.ppermute(value, 'rows', [(i, i ^ 1) for i in range(32)])]
  transfers between devices with their start and end apart: 12 -> 16, of which waited for: 7 -> 3; matrix products, arithmetic and copies ran while one was open for 0% -> 0% of each run, Pallas kernels for 24% -> 33%
where the time goes in v2:
time: 48.4 us; the launch traced here: 48.3 us
  starting transfers between devices  22.5 us (46%)
  Pallas kernels  21.6 us (45%)
  waiting for transfers between devices  3.83 us (8%)
    pallas_call x17, Pallas kernels, call(): pl.pallas_call(kernel, out_shape=tuple(outs), in_specs=specs, out_specs=t...  17.9 us
    ppermute x11, starting transfers between devices, along(): return lax.ppermute(value, 'rows', [(i, i ^ d << shift) for i in range(32)])  16.7 us
    ppermute x5, starting transfers between devices, to_other_core(): return lax.ppermute(value, 'rows', [(i, i ^ 1) for i in range(32)])  5.74 us
    pallas_call x2, Pallas kernels, finish(): pl.pallas_call(lambda *refs: k7(mine, *refs), out_shape=shape(rows, cols)...  3.75 us
    ppermute x11, waiting for transfers between devices, along(): return lax.ppermute(value, 'rows', [(i, i ^ d << shift) for i in range(32)])  3.3 us
  transfers between devices with their start and end apart: 16, of which 3 were waited for; matrix products, arithmetic and copies ran while one was open for 0% of the time, Pallas kernels for 33%

profile of v2, /device:TPU:1, one launch (start us, length us, event | category | flops | bytes accessed | tf_op | source)
XLA Modules:
  0.0 48.3 jit_solution(13767802962199186819)
XLA Ops:
  0.0 0.0 copy-start.2
  0.0 2.6 %couple.1 = (f32[256,256]{1,0:T(8,128)S(1)}, f32[192,128]{1,0:T(8,128)S(1)}, bf16[320,1024]{1,0:T(8,128)(2,1)S(1)}, bf16[320,1024]{1,0:T(8,128)(2,1)S(1)}, f32[5,128,128]{2,1,0:T(8,128)S(1)}) custom-call(s32[1]{0:T(128)} %bitcast.me_ref.refs_0_, f32[320,1024]{1,0:T(8,128)} %bitcast.9, f32[320,1024]{1,0:T(8,128)} %bitcast.7, f32[31,128,128]{2,1,0:T(8,128)} %cores_hbm.1), custom_call_target="tpu_custom_call" | custom-call | flops 1000 | bytes 1000 | tf_op jit(solution)/shard_map/couple/pallas_call | solution.py:48
  2.7 2.1 %collective-permute-start.2 = (f32[192,128]{1,0:T(8,128)S(1)}, f32[192,128]{1,0:T(8,128)S(1)}, u32[]{:S(2)}, u32[]{:S(2)}) collective-permute-start(f32[192,128]{1,0:T(8,128)S(1)} %get-tuple-element.64), channel_id=1, source_target_pairs={{0,8},{4,12},{8,0},{12,4},{16,24},{20,28},{24,16},{28,20},{32,40},... | collective-permute-start | bytes 294920 | tf_op jit(solution)/shard_map/ppermute | solution.py:249
  4.8 1.0 %collective-permute-start.1 = (f32[256,256]{1,0:T(8,128)S(1)}, f32[256,256]{1,0:T(8,128)S(1)}, u32[]{:S(2)}, u32[]{:S(2)}) collective-permute-start(f32[256,256]{1,0:T(8,128)S(1)} %get-tuple-element.63.w), channel_id=1, source_target_pairs={{0,4},{4,0},{8,12},{12,8},{16,20},{20,16},{24,28},{28,24},{32,36},... | collective-permute-start | bytes 786440 | tf_op jit(solution)/shard_map/ppermute | solution.py:245
  5.7 0.0 copy-done.2
  5.7 0.0 copy-start
  5.7 2.2 %project.1 = (bf16[320,1024]{1,0:T(8,128)(2,1)S(1)}, bf16[320,1024]{1,0:T(8,128)(2,1)S(1)}, bf16[1024,1024]{1,0:T(8,128)(2,1)S(1)}, bf16[1024,1024]{1,0:T(8,128)(2,1)S(1)}) custom-call(bf16[320,1024]{1,0:T(8,128)(2,1)S(1)} %get-tuple-element.58.vh, bf16[320,1024]{1,0:T(8,128)(2,1)S(1)} %get-tuple-element.59.vl, f32[1024,1024]{1,0:T(8,128)S(1)} %copy-done.2), custom_call_target="tpu_custom_call" | custom-call | flops 1000 | bytes 1000 | tf_op jit(solution)/shard_map/project/pallas_call | solution.py:48
  8.0 0.0 copy-done
  8.0 1.2 %columns.2 = f32[320,512]{1,0:T(8,128)S(1)} custom-call(s32[1]{0:T(128)} %bitcast.me_ref.refs_0_, bf16[320,1024]{1,0:T(8,128)(2,1)S(1)} %get-tuple-element.62.refs_1_, bf16[320,1024]{1,0:T(8,128)(2,1)S(1)} %get-tuple-element.61.refs_2_, f32[1024,1024]{1,0:T(8,128)S(1)} %copy-done), custom_call_target="tpu_custom_call" | custom-call | flops 1000 | bytes 1000 | tf_op jit(solution)/shard_map/columns/pallas_call | solution.py:48
  9.2 0.1 collective-permute-start
  9.3 0.0 collective-permute-done.2.far
  9.3 0.5 %collective-permute-start.3 = (f32[192,128]{1,0:T(8,128)S(1)}, f32[192,128]{1,0:T(8,128)S(1)}, u32[]{:S(2)}, u32[]{:S(2)}) collective-permute-start(f32[192,128]{1,0:T(8,128)S(1)} %collective-permute-done.2.far), channel_id=1, source_target_pairs={{0,4},{4,0},{8,12},{12,8},{16,20},{20,16},{24,28},{28,24},{32,36},... | collective-permute-start | bytes 294920 | tf_op jit(solution)/shard_map/ppermute | solution.py:245
  9.8 1.2 %columns.3.g = f32[320,512]{1,0:T(8,128)S(1)} custom-call(s32[1]{0:T(128)} %bitcast.me_ref.refs_0_, bf16[320,1024]{1,0:T(8,128)(2,1)S(1)} %get-tuple-element.62.refs_1_, bf16[320,1024]{1,0:T(8,128)(2,1)S(1)} %get-tuple-element.61.refs_2_, f32[1024,1024]{1,0:T(8,128)S(1)} %copy-done), custom_call_target="tpu_custom_call" | custom-call | flops 10000000000 | bytes 1000 | tf_op jit(solution)/shard_map/columns/pallas_call | solution.py:48
  10.9 0.0 copy-start.1
  11.0 0.5 %collective-permute-done.3.far_got = f32[192,128]{1,0:T(8,128)S(1)} collective-permute-done((f32[192,128]{1,0:T(8,128)S(1)}, f32[192,128]{1,0:T(8,128)S(1)}, u32[]{:S(2)}, u32[]{:S(2)}) %collective-permute-start.3) | collective-permute-done | bytes 98336 | tf_op jit(solution)/shard_map/ppermute | solution.py:245
  11.5 0.0 collective-permute-done.1.w_got
  11.5 0.1 chip.1
  11.6 0.0 collective-permute-done.got
  11.6 1.0 %level4.1 = (f32[192,128]{1,0:T(8,128)S(1)}, f32[192,128]{1,0:T(8,128)S(1)}, f32[192,128]{1,0:T(8,128)S(1)}, f32[192,128]{1,0:T(8,128)S(1)}, f32[64,512]{1,0:T(8...) custom-call(s32[1]{0:T(128)} %bitcast.me_ref.refs_0_, f32[320,512]{1,0:T(8,128)S(1)} %columns.3.g, ...), custom_call_target="tpu_custom_call" | custom-call | flops 1000 | bytes 1000 | tf_op jit(solution)/shard_map/level4/pallas_call | solution.py:48
  12.6 2.5 %collective-permute-start.4 = (f32[192,128]{1,0:T(8,128)S(1)}, f32[192,128]{1,0:T(8,128)S(1)}, u32[]{:S(2)}, u32[]{:S(2)}) collective-permute-start(f32[192,128]{1,0:T(8,128)S(1)} %get-tuple-element.71), channel_id=1, source_target_pairs={{0,16},{4,20},{8,24},{12,28},{16,0},{20,4},{24,8},{28,12},{32,48},... | collective-permute-start | bytes 294920 | tf_op jit(solution)/shard_map/ppermute | solution.py:249
  15.1 0.0 collective-permute-start.5
  15.1 0.8 %collective-permute-start.6 = (f32[192,128]{1,0:T(8,128)S(1)}, f32[192,128]{1,0:T(8,128)S(1)}, u32[]{:S(2)}, u32[]{:S(2)}) collective-permute-start(f32[192,128]{1,0:T(8,128)S(1)} %get-tuple-element.73), channel_id=1, source_target_pairs={{0,24},{4,28},{8,16},{12,20},{16,8},{20,12},{24,0},{28,4},{32,56},... | collective-permute-start | bytes 294920 | tf_op jit(solution)/shard_map/ppermute | solution.py:249
  15.9 0.1 chips.1.w
  16.0 2.0 %collective-permute-start.7 = (f32[96,128]{1,0:T(8,128)S(1)}, f32[96,128]{1,0:T(8,128)S(1)}, u32[]{:S(2)}, u32[]{:S(2)}) collective-permute-start(f32[96,128]{1,0:T(8,128)S(1)} %chips.1.w), channel_id=1, source_target_pairs={{0,24},{4,28},{8,16},{12,20},{16,8},{20,12},{24,0},{28,4},{32,56},... | collective-permute-start | bytes 147464 | tf_op jit(solution)/shard_map/ppermute | solution.py:249
  17.9 0.0 copy-done.1
  17.9 0.5 turn.1
  18.4 2.0 %leaf.4.refs_1_ = f32[1024,256]{1,0:T(8,128)S(1)} custom-call(s32[1]{0:T(128)} %bitcast.me_ref.refs_0_, bf16[1024,1024]{1,0:T(8,128)(2,1)S(1)} %get-tuple-element.74.refs_1_, bf16[1024,1024]{1,0:T(8,128)(2,1)S(1)} %get-tuple-element.75.refs_2_, f32[1024,1024]{1,0:T(8,128)S(1)} %copy-done, bf16[1024,320]{1,0:T(8,128)(2,1)S(1)} %get-tuple-element.77.refs_4_.refs_3_, ...), custom_call_target="tpu_custom_call" | custom-call | flops 1000 | bytes 1000 | tf_op jit(solution)/shard_map/leaf/pallas_call | solution.py:48
  20.4 1.3 %collective-permute-start.10 = (f32[64,512]{1,0:T(8,128)S(1)}, f32[64,512]{1,0:T(8,128)S(1)}, u32[]{:S(2)}, u32[]{:S(2)}) collective-permute-start(f32[64,512]{1,0:T(8,128)S(1)} %get-tuple-element.92), channel_id=1, source_target_pairs={{0,4},{4,0},{8,12},{12,8},{16,20},{20,16},{24,28},{28,24},{32,36},... | collective-permute-start | bytes 393224 | tf_op jit(solution)/shard_map/ppermute | solution.py:245
  21.7 0.0 collective-permute-done.4.g2
  21.7 0.0 collective-permute-done.5.g1
  21.7 0.0 collective-permute-done.6.g3
  21.7 0.0 collective-permute-done.7.w_got
  21.7 0.4 level2.1
  22.1 1.9 %collective-permute-start.8 = (f32[160,128]{1,0:T(8,128)S(1)}, f32[160,128]{1,0:T(8,128)S(1)}, u32[]{:S(2)}, u32[]{:S(2)}) collective-permute-start(f32[160,128]{1,0:T(8,128)S(1)} %get-tuple-element.86.s), channel_id=1, source_target_pairs={{0,32},{4,36},{8,40},{12,44},{16,48},{20,52},{24,56},{28,60},{32,0... | collective-permute-start | bytes 245768 | tf_op jit(solution)/shard_map/ppermute | solution.py:249
  24.0 2.0 %leaf.5.refs_2_ = f32[1024,256]{1,0:T(8,128)S(1)} custom-call(s32[1]{0:T(128)} %bitcast.me_ref.refs_0_, bf16[1024,1024]{1,0:T(8,128)(2,1)S(1)} %get-tuple-element.74.refs_1_, bf16[1024,1024]{1,0:T(8,128)(2,1)S(1)} %get-tuple-element.75.refs_2_, f32[1024,1024]{1,0:T(8,128)S(1)} %copy-done, bf16[1024,320]{1,0:T(8,128)(2,1)S(1)} %get-tuple-element.77.refs_4_.refs_3_, ...), custom_call_target="tpu_custom_call" | custom-call | flops 1000 | bytes 1000 | tf_op jit(solution)/shard_map/leaf/pallas_call | solution.py:48
  26.0 0.0 collective-permute-done.8.got
  26.0 0.4 level1.1
  26.3 3.5 %collective-permute-start.9 = (f32[64,128]{1,0:T(8,128)S(1)}, f32[64,128]{1,0:T(8,128)S(1)}, u32[]{:S(2)}, u32[]{:S(2)}) collective-permute-start(f32[64,128]{1,0:T(8,128)S(1)} %get-tuple-element.90.a0), channel_id=1, source_target_pairs={{0,96},{4,100},{8,104},{12,108},{16,112},{20,116},{24,120},{28,124... | collective-permute-start | bytes 98312 | tf_op jit(solution)/shard_map/ppermute | solution.py:249
  29.8 0.3 collective-permute-start.14
  30.1 0.0 collective-permute-done.10.refs_6_
  30.1 2.0 %leaf.6.refs_1_ = f32[1024,256]{1,0:T(8,128)S(1)} custom-call(s32[1]{0:T(128)} %bitcast.me_ref.refs_0_, bf16[1024,1024]{1,0:T(8,128)(2,1)S(1)} %get-tuple-element.74.refs_1_, bf16[1024,1024]{1,0:T(8,128)(2,1)S(1)} %get-tuple-element.75.refs_2_, f32[1024,1024]{1,0:T(8,128)S(1)} %copy-done, bf16[1024,320]{1,0:T(8,128)(2,1)S(1)} %get-tuple-element.77.refs_4_.refs_3_, ...), custom_call_target="tpu_custom_call" | custom-call | flops 1000 | bytes 1000 | tf_op jit(solution)/shard_map/leaf/pallas_call | solution.py:48
  32.1 0.0 collective-permute-done.9.got
  32.1 0.2 level0.1
  32.3 2.8 %collective-permute-start.11 = (f32[192,128]{1,0:T(8,128)S(1)}, f32[192,128]{1,0:T(8,128)S(1)}, u32[]{:S(2)}, u32[]{:S(2)}) collective-permute-start(f32[192,128]{1,0:T(8,128)S(1)} %get-tuple-element.98), channel_id=1, source_target_pairs={{0,16},{4,20},{8,24},{12,28},{16,0},{20,4},{24,8},{28,12},{32,48},... | collective-permute-start | bytes 294920 | tf_op jit(solution)/shard_map/ppermute | solution.py:249
  35.1 0.6 %collective-permute-start.12 = (f32[192,128]{1,0:T(8,128)S(1)}, f32[192,128]{1,0:T(8,128)S(1)}, u32[]{:S(2)}, u32[]{:S(2)}) collective-permute-start(f32[192,128]{1,0:T(8,128)S(1)} %get-tuple-element.99), channel_id=1, source_target_pairs={{0,8},{4,12},{8,0},{12,4},{16,24},{20,28},{24,16},{28,20},{32,40},... | collective-permute-start | bytes 294920 | tf_op jit(solution)/shard_map/ppermute | solution.py:249
  35.7 0.2 collective-permute-start.13
  35.9 2.0 %leaf.7.refs_2_ = f32[1024,256]{1,0:T(8,128)S(1)} custom-call(s32[1]{0:T(128)} %bitcast.me_ref.refs_0_, bf16[1024,1024]{1,0:T(8,128)(2,1)S(1)} %get-tuple-element.74.refs_1_, bf16[1024,1024]{1,0:T(8,128)(2,1)S(1)} %get-tuple-element.75.refs_2_, f32[1024,1024]{1,0:T(8,128)S(1)} %copy-done, bf16[1024,320]{1,0:T(8,128)(2,1)S(1)} %get-tuple-element.77.refs_4_.refs_3_, ...), custom_call_target="tpu_custom_call" | custom-call | flops 1000 | bytes 1000 | tf_op jit(solution)/shard_map/leaf/pallas_call | solution.py:48
  37.9 0.0 collective-permute-done.14.got
  37.9 0.2 level3.1.q3
  38.1 0.0 collective-permute-done.11.r2
  38.2 0.6 %collective-permute-done.12.r1 = f32[192,128]{1,0:T(8,128)S(1)} collective-permute-done((f32[192,128]{1,0:T(8,128)S(1)}, f32[192,128]{1,0:T(8,128)S(1)}, u32[]{:S(2)}, u32[]{:S(2)}) %collective-permute-start.12) | collective-permute-done | bytes 98336 | tf_op jit(solution)/shard_map/ppermute | solution.py:249
  38.7 2.7 %collective-permute-done.13.r3 = f32[192,128]{1,0:T(8,128)S(1)} collective-permute-done((f32[192,128]{1,0:T(8,128)S(1)}, f32[192,128]{1,0:T(8,128)S(1)}, u32[]{:S(2)}, u32[]{:S(2)}) %collective-permute-start.13) | collective-permute-done | bytes 98336 | tf_op jit(solution)/shard_map/ppermute | solution.py:249
  41.4 0.1 assemble.1.refs_5_
  41.5 2.9 %collective-permute-start.15 = (f32[256,512]{1,0:T(8,128)S(1)}, f32[256,512]{1,0:T(8,128)S(1)}, u32[]{:S(2)}, u32[]{:S(2)}) collective-permute-start(f32[256,512]{1,0:T(8,128)S(1)} %assemble.1.refs_5_), channel_id=1, source_target_pairs={{0,4},{4,0},{8,12},{12,8},{16,20},{20,16},{24,28},{28,24},{32,36},... | collective-permute-start | bytes 1572872 | tf_op jit(solution)/shard_map/ppermute | solution.py:245
  44.4 1.9 %finish.2.refs_6_ = f32[1024,1024]{1,0:T(8,128)} custom-call(s32[1]{0:T(128)} %bitcast.me_ref.refs_0_, f32[1024,256]{1,0:T(8,128)S(1)} %leaf.4.refs_1_, f32[1024,256]{1,0:T(8,128)S(1)} %leaf.5.refs_2_, bf16[1024,320]{1,0:T(8,128)(2,1)S(1)} %get-tuple-element.77.refs_4_.refs_3_, bf16[1024,320]{1,0:T(8,128)(2,1)S(1)} %get-tuple-element.78.refs_5_.refs_4_, ...), custom_call_target="tpu_custom_call" | custom-call | flops 1000000000 | bytes 5242880 | tf_op jit(solution)/shard_map/finish/pallas_call | solution.py:339
  46.3 0.0 collective-permute-done.15.refs_5_
  46.3 1.9 %finish.3 = f32[1024,1024]{1,0:T(8,128)} custom-call(s32[1]{0:T(128)} %bitcast.me_ref.refs_0_, f32[1024,256]{1,0:T(8,128)S(1)} %leaf.6.refs_1_, f32[1024,256]{1,0:T(8,128)S(1)} %leaf.7.refs_2_, bf16[1024,320]{1,0:T(8,128)(2,1)S(1)} %get-tuple-element.77.refs_4_.refs_3_, ...), custom_call_target="tpu_custom_call", output_to_operand_aliasing={{}: (6, {})} | custom-call | flops 1000000000 | bytes 5242880 | tf_op jit(solution)/shard_map/finish/pallas_call | solution.py:339
Async XLA Ops:
  0.0 5.7 %copy-start.2 = (f32[1024,1024]{1,0:T(8,128)S(1)}, f32[1024,1024]{1,0:T(8,128)}, u32[]{:S(2)}) copy-start(f32[1024,1024]{1,0:T(8,128)} %l.1) | copy-start | bytes 12582916
  2.7 6.6 %collective-permute-start.2 = (f32[192,128]{1,0:T(8,128)S(1)}, f32[192,128]{1,0:T(8,128)S(1)}, u32[]{:S(2)}, u32[]{:S(2)}) collective-permute-start(f32[192,128]{1,0:T(8,128)S(1)} %get-tuple-element.64), channel_id=1, source_target_pairs={{0,8},{4,12},{8,0},{12,4},{16,24},{20,28},{24,16},{28,20},{32,40},... | collective-permute-start | bytes 294920 | tf_op jit(solution)/shard_map/ppermute | solution.py:249
  4.8 6.7 %collective-permute-start.1 = (f32[256,256]{1,0:T(8,128)S(1)}, f32[256,256]{1,0:T(8,128)S(1)}, u32[]{:S(2)}, u32[]{:S(2)}) collective-permute-start(f32[256,256]{1,0:T(8,128)S(1)} %get-tuple-element.63.w), channel_id=1, source_target_pairs={{0,4},{4,0},{8,12},{12,8},{16,20},{20,16},{24,28},{28,24},{32,36},... | collective-permute-start | bytes 786440 | tf_op jit(solution)/shard_map/ppermute | solution.py:245
  5.7 2.2 %copy-start = (f32[1024,1024]{1,0:T(8,128)S(1)}, f32[1024,1024]{1,0:T(8,128)}, u32[]{:S(2)}) copy-start(f32[1024,1024]{1,0:T(8,128)} %refs_3_.11) | copy-start | bytes 12582916
  9.2 2.4 %collective-permute-start = (f32[320,512]{1,0:T(8,128)S(1)}, f32[320,512]{1,0:T(8,128)S(1)}, u32[]{:S(2)}, u32[]{:S(2)}) collective-permute-start(f32[320,512]{1,0:T(8,128)S(1)} %columns.2), channel_id=1, source_target_pairs={{0,4},{4,0},{8,12},{12,8},{16,20},{20,16},{24,28},{28,24},{32,36},... | collective-permute-start | bytes 1966088 | tf_op jit(solution)/shard_map/ppermute | solution.py:245
  9.3 2.2 %collective-permute-start.3 = (f32[192,128]{1,0:T(8,128)S(1)}, f32[192,128]{1,0:T(8,128)S(1)}, u32[]{:S(2)}, u32[]{:S(2)}) collective-permute-start(f32[192,128]{1,0:T(8,128)S(1)} %collective-permute-done.2.far), channel_id=1, source_target_pairs={{0,4},{4,0},{8,12},{12,8},{16,20},{20,16},{24,28},{28,24},{32,36},... | collective-permute-start | bytes 294920 | tf_op jit(solution)/shard_map/ppermute | solution.py:245
  10.9 7.0 %copy-start.1 = (f32[5,1024,64]{1,2,0:T(8,128)S(1)}, f32[5,1024,64]{1,2,0:T(8,128)}, u32[]{:S(2)}) copy-start(f32[5,1024,64]{1,2,0:T(8,128)} %param.7) | copy-start | bytes 3932164
  12.6 9.1 %collective-permute-start.4 = (f32[192,128]{1,0:T(8,128)S(1)}, f32[192,128]{1,0:T(8,128)S(1)}, u32[]{:S(2)}, u32[]{:S(2)}) collective-permute-start(f32[192,128]{1,0:T(8,128)S(1)} %get-tuple-element.71), channel_id=1, source_target_pairs={{0,16},{4,20},{8,24},{12,28},{16,0},{20,4},{24,8},{28,12},{32,48},... | collective-permute-start | bytes 294920 | tf_op jit(solution)/shard_map/ppermute | solution.py:249
  15.1 6.6 %collective-permute-start.5 = (f32[192,128]{1,0:T(8,128)S(1)}, f32[192,128]{1,0:T(8,128)S(1)}, u32[]{:S(2)}, u32[]{:S(2)}) collective-permute-start(f32[192,128]{1,0:T(8,128)S(1)} %get-tuple-element.72), channel_id=1, source_target_pairs={{0,8},{4,12},{8,0},{12,4},{16,24},{20,28},{24,16},{28,20},{32,40},... | collective-permute-start | bytes 294920 | tf_op jit(solution)/shard_map/ppermute | solution.py:249
  15.1 6.6 %collective-permute-start.6 = (f32[192,128]{1,0:T(8,128)S(1)}, f32[192,128]{1,0:T(8,128)S(1)}, u32[]{:S(2)}, u32[]{:S(2)}) collective-permute-start(f32[192,128]{1,0:T(8,128)S(1)} %get-tuple-element.73), channel_id=1, source_target_pairs={{0,24},{4,28},{8,16},{12,20},{16,8},{20,12},{24,0},{28,4},{32,56},... | collective-permute-start | bytes 294920 | tf_op jit(solution)/shard_map/ppermute | solution.py:249
  16.0 5.7 %collective-permute-start.7 = (f32[96,128]{1,0:T(8,128)S(1)}, f32[96,128]{1,0:T(8,128)S(1)}, u32[]{:S(2)}, u32[]{:S(2)}) collective-permute-start(f32[96,128]{1,0:T(8,128)S(1)} %chips.1.w), channel_id=1, source_target_pairs={{0,24},{4,28},{8,16},{12,20},{16,8},{20,12},{24,0},{28,4},{32,56},... | collective-permute-start | bytes 147464 | tf_op jit(solution)/shard_map/ppermute | solution.py:249
  20.4 9.7 %collective-permute-start.10 = (f32[64,512]{1,0:T(8,128)S(1)}, f32[64,512]{1,0:T(8,128)S(1)}, u32[]{:S(2)}, u32[]{:S(2)}) collective-permute-start(f32[64,512]{1,0:T(8,128)S(1)} %get-tuple-element.92), channel_id=1, source_target_pairs={{0,4},{4,0},{8,12},{12,8},{16,20},{20,16},{24,28},{28,24},{32,36},... | collective-permute-start | bytes 393224 | tf_op jit(solution)/shard_map/ppermute | solution.py:245
  22.1 3.9 %collective-permute-start.8 = (f32[160,128]{1,0:T(8,128)S(1)}, f32[160,128]{1,0:T(8,128)S(1)}, u32[]{:S(2)}, u32[]{:S(2)}) collective-permute-start(f32[160,128]{1,0:T(8,128)S(1)} %get-tuple-element.86.s), channel_id=1, source_target_pairs={{0,32},{4,36},{8,40},{12,44},{16,48},{20,52},{24,56},{28,60},{32,0... | collective-permute-start | bytes 245768 | tf_op jit(solution)/shard_map/ppermute | solution.py:249
  26.3 5.8 %collective-permute-start.9 = (f32[64,128]{1,0:T(8,128)S(1)}, f32[64,128]{1,0:T(8,128)S(1)}, u32[]{:S(2)}, u32[]{:S(2)}) collective-permute-start(f32[64,128]{1,0:T(8,128)S(1)} %get-tuple-element.90.a0), channel_id=1, source_target_pairs={{0,96},{4,100},{8,104},{12,108},{16,112},{20,116},{24,120},{28,124... | collective-permute-start | bytes 98312 | tf_op jit(solution)/shard_map/ppermute | solution.py:249
  29.8 8.1 %collective-permute-start.14 = (f32[64,512]{1,0:T(8,128)S(1)}, f32[64,512]{1,0:T(8,128)S(1)}, u32[]{:S(2)}, u32[]{:S(2)}) collective-permute-start(f32[64,512]{1,0:T(8,128)S(1)} %get-tuple-element.102.own), channel_id=1, source_target_pairs={{0,8},{4,12},{8,0},{12,4},{16,24},{20,28},{24,16},{28,20},{32,40},... | collective-permute-start | bytes 393224 | tf_op jit(solution)/shard_map/ppermute | solution.py:249
  32.3 5.9 %collective-permute-start.11 = (f32[192,128]{1,0:T(8,128)S(1)}, f32[192,128]{1,0:T(8,128)S(1)}, u32[]{:S(2)}, u32[]{:S(2)}) collective-permute-start(f32[192,128]{1,0:T(8,128)S(1)} %get-tuple-element.98), channel_id=1, source_target_pairs={{0,16},{4,20},{8,24},{12,28},{16,0},{20,4},{24,8},{28,12},{32,48},... | collective-permute-start | bytes 294920 | tf_op jit(solution)/shard_map/ppermute | solution.py:249
  35.1 3.7 %collective-permute-start.12 = (f32[192,128]{1,0:T(8,128)S(1)}, f32[192,128]{1,0:T(8,128)S(1)}, u32[]{:S(2)}, u32[]{:S(2)}) collective-permute-start(f32[192,128]{1,0:T(8,128)S(1)} %get-tuple-element.99), channel_id=1, source_target_pairs={{0,8},{4,12},{8,0},{12,4},{16,24},{20,28},{24,16},{28,20},{32,40},... | collective-permute-start | bytes 294920 | tf_op jit(solution)/shard_map/ppermute | solution.py:249
  35.7 5.7 %collective-permute-start.13 = (f32[192,128]{1,0:T(8,128)S(1)}, f32[192,128]{1,0:T(8,128)S(1)}, u32[]{:S(2)}, u32[]{:S(2)}) collective-permute-start(f32[192,128]{1,0:T(8,128)S(1)} %get-tuple-element.100), channel_id=1, source_target_pairs={{0,24},{4,28},{8,16},{12,20},{16,8},{20,12},{24,0},{28,4},{32,56},... | collective-permute-start | bytes 294920 | tf_op jit(solution)/shard_map/ppermute | solution.py:249
  41.5 4.8 %collective-permute-start.15 = (f32[256,512]{1,0:T(8,128)S(1)}, f32[256,512]{1,0:T(8,128)S(1)}, u32[]{:S(2)}, u32[]{:S(2)}) collective-permute-start(f32[256,512]{1,0:T(8,128)S(1)} %assemble.1.refs_5_), channel_id=1, source_target_pairs={{0,4},{4,0},{8,12},{12,8},{16,20},{20,16},{24,28},{28,24},{32,36},... | collective-permute-start | bytes 1572872 | tf_op jit(solution)/shard_map/ppermute | solution.py:245

commit v3 on v2

v3 whole, which is shorter than its diff:
```python
import jax
import jax.numpy as jnp
from jax import lax
from jax.experimental import pallas as pl
from jax.experimental.pallas import tpu as pltpu
from jax.sharding import PartitionSpec as P

R = 64
F32, BF16 = jnp.float32, jnp.bfloat16
MIB = 1 << 20


def split(a):
    high = a.astype(BF16)
    return high, (a - high.astype(F32)).astype(BF16)


def dot(a, b, dims=((1,), (0,))):
    return lax.dot_general(a, b, (dims, ((), ())), preferred_element_type=F32)


def mm3(a, b):
    (ah, al), (bh, bl) = a, b
    return dot(jnp.concatenate([ah, al, ah], 1), jnp.concatenate([bh, bh, bl], 0))


def mm(a, b):
    return mm3(split(a), split(b))


def bits(me_ref):
    me = me_ref[0]
    return me, [lax.rem(me >> b, 2) for b in range(5)]


VM = pl.BlockSpec(memory_space=pltpu.VMEM)
SM = pl.BlockSpec(memory_space=pltpu.SMEM)
HB = pl.BlockSpec(memory_space=pltpu.HBM)


def shape(*dims, dtype=F32):
    return jax.ShapeDtypeStruct(dims, dtype)


def call(kernel, ins, outs, specs, name, flops, moved, limit, scratch=(), grid=None, aliases=None):
    out_specs = [VM] * len(outs) if grid is None else grid[1]
    extra = {} if grid is None else dict(grid=grid[0])
    return pl.pallas_call(
        kernel,
        out_shape=tuple(outs),
        in_specs=specs,
        out_specs=tuple(out_specs),
        scratch_shapes=list(scratch),
        name=name,
        input_output_aliases=aliases or {},
        cost_estimate=pl.CostEstimate(flops=flops, bytes_accessed=1000, transcendentals=0),
        compiler_params=pltpu.CompilerParams(vmem_limit_bytes=limit * MIB),
        **extra,
    )(*ins)


def pack(w):
    low = jnp.concatenate([w[: 2 * R, R : 2 * R], w[:R, :R]], 0)
    return jnp.concatenate([w[: 3 * R, 2 * R : 3 * R], low], 1)


def k0(me_ref, vt_hbm, ut_hbm, cores_hbm, w_ref, packed, vh_ref, vl_ref, sel, vt, ut, sems):
    me, bit = bits(me_ref)
    where = [15 + (me >> 1), 7 + (me >> 2), 3 + (me >> 3), 1 + (me >> 4), 1 + ((me >> 4) ^ 1), 0]
    get_v = pltpu.make_async_copy(vt_hbm, vt, sems.at[0])
    get_u = pltpu.make_async_copy(ut_hbm, ut, sems.at[1])
    picks = [pltpu.make_async_copy(cores_hbm.at[i], sel.at[k], sems.at[2 + k]) for k, i in enumerate(where)]
    for copy in [get_v, get_u, *picks]:
        copy.start()
    get_v.wait()
    get_u.wait()
    vh, vl = split(vt[...])
    vh_ref[...] = vh
    vl_ref[...] = vl
    vh, vl = vh[: 4 * R], vl[: 4 * R]
    uh, ul = split(ut[R:, :])
    w = dot(jnp.concatenate([vh, vl, vh], 1), jnp.concatenate([uh, uh, ul], 1), ((1,), (1,)))
    w_ref[...] = w
    packed[...] = pack(w)
    for copy in picks:
        copy.wait()


def k1(vh, vl, l, yh, yl, lh_ref, ll_ref):
    lh, ll = split(l[...])
    lh_ref[...] = lh
    ll_ref[...] = ll
    yh[...], yl[...] = split(mm3((vh[...], vl[...]), (lh, ll)))


def k2(mine, me_ref, yh, yl, b, g):
    me, bit = bits(me_ref)
    half = g.shape[1]
    at = pl.ds(pl.multiple_of((bit[0] if mine else 1 - bit[0]) * half, half), half)
    g[...] = mm3((yh[...], yl[...]), split(b[:, at]))


def rows_of(q, bit, own):
    at = bit if own else 1 - bit
    return q[pl.ds(pl.multiple_of(at * R, R), R), :]


def stack(p, first, second, bit):
    p[pl.ds(pl.multiple_of((1 - bit) * R, R), R), :] = first
    p[pl.ds(pl.multiple_of(bit * R, R), R), :] = second


def own_share(core, bit, own, other):
    both = jnp.concatenate([rows_of(core, bit, True), rows_of(core, bit, False)], 0)
    full = mm(jnp.concatenate([own, other], 1), both)
    return jnp.where(bit == 0, full[:, R:], full[:, :R])


def kw(me_ref, w, w_got, far, far_got, sel, share, w_next):
    me, bit = bits(me_ref)
    own, other = pack(w[...]) + pack(w_got[...]), far[...] + far_got[...]
    share[...] = own_share(sel.at[1], bit[1], own[:, :R], other[:, :R])
    both = own[:, R:] + other[:, R:]
    w_next[...] = jnp.concatenate([both[: 3 * R // 2], both[3 * R // 2 :]], 1)


def k3(me_ref, g, got, w, w_got, share, w_next, sel, m0, m2, m1, m3, p3, q_mine, q_other, p, q, a):
    me, bit = bits(me_ref)
    x = lax.rem(me >> 1, 4)
    c = bit[0]
    stack(p, g[4 * R :, :], got[4 * R :, :], c)
    q[...] = mm(sel[0], p[...])
    mine, theirs = rows_of(q, c, True), rows_of(q, c, False)
    q_mine[...] = mine
    q_other[...] = theirs
    wide = jnp.concatenate([w[:, 3 * R :], w_got[:, 3 * R :]], 1)
    left = g[: 4 * R, :] + got[: 4 * R, :] - mm(wide, jnp.concatenate([mine, theirs], 0))
    third = left[3 * R :]
    p3[...] = third
    a[...] = left[: 3 * R] - mm(share[...], third)
    for d, out in ((2, m2), (1, m1), (3, m3), (0, m0)):
        out[: 3 * R, :] = a[:, pl.ds(pl.multiple_of((x ^ d) * 2 * R, 2 * R), 2 * R)]
    m2[3 * R :, :] = w_next[: 3 * R // 4, :]
    m3[3 * R :, :] = w_next[3 * R // 4 :, :]


def unfold(w):
    return jnp.concatenate([w[:, :R], w[:, R:]], 0)


def k4(me_ref, m0, g2, g1, g3, w, sel, z0, z2, z1, z3, q2, p, q):
    me, bit = bits(me_ref)
    own = unfold(w)
    other = unfold(jnp.concatenate([g2[3 * R :, :], g3[3 * R :, :]], 0))
    near = m0[...] + g1[...]
    far = g2[: 3 * R, :] + g3[: 3 * R, :]
    stack(p, near[2 * R :], far[2 * R :], bit[2])
    q[...] = mm(sel[2], p[...])
    mine, theirs = rows_of(q, bit[2], True), rows_of(q, bit[2], False)
    q2[0] = mine
    q2[1] = theirs
    wide = jnp.concatenate([own[: 2 * R], other[: 2 * R]], 1)
    t = near[: 2 * R] + far[: 2 * R] - mm(wide, jnp.concatenate([mine, theirs], 0))
    last = own[2 * R :] + other[2 * R :]
    last = jnp.concatenate([last[: R // 2], last[R // 2 :]], 1)
    for out in (z2, z1, z3, z0):
        out[: 2 * R, :] = t
        out[2 * R :, :] = last


def k5(me_ref, s0, s2, s1, s3, sel, q2, r0, r2, r1, r3, p, q):
    me, bit = bits(me_ref)
    sums = []
    for k, (a, b) in enumerate(((s0, s1), (s2, s3))):
        stack(p.at[k], a[R : 2 * R, :], b[R : 2 * R, :], bit[3])
        q[k] = mm(sel[3 + k], p[k])
    for k, (a, b) in enumerate(((s0, s1), (s2, s3))):
        both = jnp.concatenate([rows_of(q.at[k], bit[3], True), rows_of(q.at[k], bit[3], False)], 0)
        wide = jnp.concatenate([unfold(a[2 * R :, :]), unfold(b[2 * R :, :])], 1)
        sums.append(a[:R, :] + b[:R, :] - mm(wide, both))
    stack(p.at[2], sums[0], sums[1], bit[4])
    top = mm(rows_of(sel.at[5], bit[4], True), p[2])
    one = rows_of(q.at[0], bit[3], True)
    for k, out in ((1, r2), (0, r1), (1, r3), (0, r0)):
        out[:R, :] = top
        out[R : 2 * R, :] = one
        out[2 * R :, :] = q2[k]


def kq(me_ref, own, got, sel, q, p):
    me, bit = bits(me_ref)
    stack(p, own[...], got[...], bit[1])
    q[...] = mm(rows_of(sel.at[1], bit[1], True), p[...])


def k6(me_ref, r0, r2, r1, r3, q3, q4, q_half):
    me, bit = bits(me_ref)
    x = lax.rem(me >> 1, 4)
    for d, r in ((0, r0), (1, r1), (2, r2), (3, r3)):
        q_half[: 3 * R, pl.ds(pl.multiple_of((x ^ d) * 2 * R, 2 * R), 2 * R)] = r[...]
    q_half[3 * R : 4 * R, :] = q3[...]
    q_half[4 * R :, :] = q4[...]


def ku(ut, uh_ref, ul_ref, u4):
    h, l = split(ut[...].T)
    uh_ref[...] = h[:, : 4 * R]
    ul_ref[...] = l[:, : 4 * R]
    h, l = h[:, 4 * R :], l[:, 4 * R :]
    u4[...] = jnp.concatenate([h, l, h], 1)


def kl(first, me_ref, lh, ll, b, x):
    me, bit = bits(me_ref)
    n = b.shape[1] // 4
    at = pl.multiple_of((bit[0] if first < 2 else 1 - bit[0]) * 2 * n + first % 2 * n, n)
    x[...] = mm3((lh[...], ll[...]), split(b[:, pl.ds(at, x.shape[1])]))


PARTS = 4


def k7(mine, me_ref, xa, xb, uh, ul, u4, q, q4, *rest):
    out, buf, sem = rest[-3:]
    me, bit = bits(me_ref)
    half = q.shape[1]
    at = pl.multiple_of((bit[0] if mine else 1 - bit[0]) * half, half)
    fourth = split(q4[...] if mine else q[4 * R :, :])
    lower = jnp.concatenate([fourth[0], *fourth], 0)
    qh, ql = split(q[: 4 * R, :])
    upper = jnp.concatenate([qh, qh, ql], 0)
    n = buf.shape[0] // PARTS
    copies = []
    for k in range(PARTS):
        r = slice(k * n, k * n + n)
        left = jnp.concatenate([uh[r, :], ul[r, :], uh[r, :]], 1)
        x = xa[r, :] if mine else jnp.concatenate([xa[r, :], xb[r, :]], 1)
        buf[r, :] = x - dot(left, upper) - dot(u4[r, :], lower)
        copies.append(
            pltpu.make_async_copy(buf.at[pl.ds(k * n, n)], out.at[pl.ds(k * n, n), pl.ds(at, half)], sem.at[k])
        )
        copies[-1].start()
    for copy in copies:
        copy.wait()


def to_other_core(value):
    return lax.ppermute(value, "rows", [(i, i ^ 1) for i in range(32)])


def along(value, shift, d):
    return lax.ppermute(value, "rows", [(i, i ^ (d << shift)) for i in range(32)])


def spread(values, shift):
    return [values[0]] + [along(values[k], shift, d) for k, d in ((1, 2), (2, 1), (3, 3))]


def local(right_side, leaf_inverse, left_factors, right_factors, cores):
    me = lax.axis_index("rows").astype(jnp.int32).reshape(1)
    rows, cols = right_side.shape
    half, eighth = cols // 2, cols // 8
    vt = right_factors.transpose(0, 2, 1).reshape(5 * R, rows)
    ut = left_factors.transpose(0, 2, 1).reshape(5 * R, rows)
    in_hbm = [pltpu.with_memory_space_constraint(v, pltpu.HBM) for v in (vt, ut, cores)]
    tall = shape(5 * R, rows, dtype=BF16)
    square = shape(rows, rows, dtype=BF16)
    after = lax.optimization_barrier

    w, packed, vh, vl, sel = call(
        k0, (me, *in_hbm), [shape(4 * R, 4 * R), shape(3 * R, 2 * R), tall, tall, shape(6, 2 * R, 2 * R)],
        [SM, HB, HB, HB], "couple", 1000, 3 * MIB, 12,
        scratch=[pltpu.VMEM((5 * R, rows), F32)] * 2 + [pltpu.SemaphoreType.DMA((8,))],
    )
    w_got = to_other_core(w)
    far = along(packed, 1, 1)
    yh, yl, lh, ll = call(
        k1, (vh, vl, leaf_inverse), [tall, tall, square, square], [VM] * 3, "project", 1000, 4 * MIB, 20,
    )

    def image(mine, yh_):
        return call(
            lambda *refs: k2(mine, *refs), (me, yh_, yl, right_side), [shape(5 * R, half)], [SM] + [VM] * 3,
            "columns", 10**10 if mine else 1000, 3 * MIB, 12,
        )[0]

    sent = image(False, yh)
    got = to_other_core(sent)
    far = after((far, sent))[0]
    far_got = to_other_core(far)
    g = image(True, after((yh, sent))[0])
    far_got, g = after((far_got, g))
    share, w_next = call(
        kw, (me, w, w_got, far, far_got, sel), [shape(3 * R, R), shape(3 * R // 2, 2 * R)], [SM] + [VM] * 5,
        "chip", 10, MIB, 6,
    )
    *messages, p3, q4_mine, q4_other = call(
        k3, (me, g, got, w, w_got, share, w_next, sel),
        [shape(3 * R + k, eighth) for k in (0, 3 * R // 4, 0, 3 * R // 4)] + [shape(R, half)] * 3,
        [SM] + [VM] * 7, "level4", 1000, 4 * MIB, 10,
        scratch=[pltpu.VMEM((2 * R, half), F32)] * 2 + [pltpu.VMEM((3 * R, half), F32)],
    )

    def leaf(first, count, behind):
        return call(
            lambda *refs: kl(first, *refs), (me, after((lh, behind))[0], ll, right_side),
            [shape(rows, count * cols // 4)], [SM] + [VM] * 3, "leaf", 1000, 6 * MIB, 16,
        )[0]

    def turn(behind):
        return call(
            ku, (after((ut, behind))[0],), [shape(rows, k * R, dtype=BF16) for k in (4, 4, 3)], [VM], "turn",
            10, 3 * MIB, 8,
        )

    uh, ul, u4 = turn(q4_mine)
    got, x_mine, uh = after((spread(messages, 1), leaf(0, 2, q4_mine), uh))
    small = [pltpu.VMEM((2 * R, eighth), F32)]
    *z, q2 = call(
        k4, (me, *got, w_next, sel), [shape(5 * R // 2, eighth)] * 4 + [shape(2, R, eighth)],
        [SM] + [VM] * 6, "level2", 1000, MIB, 8, scratch=small * 2,
    )
    got, x2 = after((spread(z, 3), leaf(2, 1, q2)))
    p3_got = along(after((p3, q2))[0], 1, 1)
    back = call(
        k5, (me, *got, sel, q2), [shape(3 * R, eighth)] * 4, [SM] + [VM] * 6, "levels10", 1000, MIB, 8,
        scratch=[pltpu.VMEM((3, 2 * R, eighth), F32), pltpu.VMEM((2, 2 * R, eighth), F32)],
    )
    (q3,) = call(
        kq, (me, p3, p3_got, sel), [shape(R, half)], [SM] + [VM] * 3, "level3", 1000, MIB, 8,
        scratch=[pltpu.VMEM((2 * R, half), F32)],
    )
    got, x3, q3 = after((spread(back, 1), leaf(3, 1, back[0]), q3))
    (q_half,) = call(
        k6, (me, *got, q3, q4_other), [shape(5 * R, half)], [SM] + [VM] * 6, "assemble", 10, MIB, 8,
    )
    q_rest = to_other_core(q_half)

    def finish(mine, xa, xb, q, *so_far):
        return pl.pallas_call(
            lambda *refs: k7(mine, *refs),
            out_shape=shape(rows, cols),
            in_specs=[SM] + [VM] * 7 + [HB] * len(so_far),
            out_specs=HB,
            scratch_shapes=[pltpu.VMEM((rows, half), F32), pltpu.SemaphoreType.DMA((PARTS,))],
            name="finish",
            input_output_aliases={8: 0} if so_far else {},
            cost_estimate=pl.CostEstimate(flops=10**9, bytes_accessed=5 * MIB, transcendentals=0),
            compiler_params=pltpu.CompilerParams(vmem_limit_bytes=12 * MIB),
        )(me, xa, xb, uh, ul, u4, q, q4_mine, *so_far)

    out = finish(True, x_mine, x_mine, q_half)
    return finish(False, x2, x3, q_rest, out)


def solution(mesh):
    in_specs = (
        P(("rep", "rows"), None),
        P(("rep", "rows"), None),
        P(None, ("rep", "rows"), None),
        P(None, ("rep", "rows"), None),
        P("rep", None, None),
    )
    out_specs = P(("rep", "rows"), None)
    return jax.shard_map(local, mesh=mesh, in_specs=in_specs, out_specs=out_specs, check_vma=False)
```

time: 48.4 us -> 48 us (level)
  starting transfers between devices: 22.5 us -> 17.6 us
  waiting for transfers between devices: 3.83 us -> 8.21 us
    ppermute x11, waiting for transfers between devices: 3.3 us -> 7.68 us  [along(): return lax.ppermute(value, 'rows', [(i, i ^ d << shift) for i in range(32)])]
    ppermute x11, starting transfers between devices: 16.7 us -> 13.2 us  [along(): return lax.ppermute(value, 'rows', [(i, i ^ d << shift) for i in range(32)])]
    ppermute x5 -> x4, starting transfers between devices: 5.74 us -> 4.46 us  [to_other_core(): return lax.ppermute(value, 'rows', [(i, i ^ 1) for i in range(32)])]
    pallas_call x2, Pallas kernels: 3.75 us -> 4.38 us  [finish(): pl.pallas_call(lambda *refs: k7(mine, *refs), out_shape=shape(rows, cols)...]
    pallas_call x17 -> x14, Pallas kernels: 17.9 us -> 17.3 us  [call(): pl.pallas_call(kernel, out_shape=tuple(outs), in_specs=specs, out_specs=t...]
  transfers between devices with their start and end apart: 16 -> 15, of which waited for: 3 -> 7; matrix products, arithmetic and copies ran while one was open for 0% -> 0% of each run, Pallas kernels for 33% -> 32%
where the time goes in v3:
time: 48 us; the launch traced here: 47.9 us
  Pallas kernels  21.7 us (45%)
  starting transfers between devices  17.6 us (37%)
  waiting for transfers between devices  8.21 us (17%)
    pallas_call x14, Pallas kernels, call(): pl.pallas_call(kernel, out_shape=tuple(outs), in_specs=specs, out_specs=t...  17.3 us
    ppermute x11, starting transfers between devices, along(): return lax.ppermute(value, 'rows', [(i, i ^ d << shift) for i in range(32)])  13.2 us
    ppermute x11, waiting for transfers between devices, along(): return lax.ppermute(value, 'rows', [(i, i ^ d << shift) for i in range(32)])  7.68 us
    ppermute x4, starting transfers between devices, to_other_core(): return lax.ppermute(value, 'rows', [(i, i ^ 1) for i in range(32)])  4.46 us
    pallas_call x2, Pallas kernels, finish(): pl.pallas_call(lambda *refs: k7(mine, *refs), out_shape=shape(rows, cols)...  4.38 us
  transfers between devices with their start and end apart: 15, of which 7 were waited for; matrix products, arithmetic and copies ran while one was open for 0% of the time, Pallas kernels for 32%

profile of v3, /device:TPU:1, one launch (start us, length us, event | category | flops | bytes accessed | tf_op | source)
XLA Modules:
  0.0 47.9 jit_solution(16928814968871108968)
XLA Ops:
  0.0 0.0 copy-start.2
  0.0 2.6 %couple.1 = (f32[256,256]{1,0:T(8,128)S(1)}, f32[192,128]{1,0:T(8,128)S(1)}, bf16[320,1024]{1,0:T(8,128)(2,1)S(1)}, bf16[320,1024]{1,0:T(8,128)(2,1)S(1)}, f32[6,128,128]{2,1,0:T(8,128)S(1)}) custom-call(s32[1]{0:T(128)} %bitcast.me_ref.refs_0_, f32[320,1024]{1,0:T(8,128)} %bitcast.9, f32[320,1024]{1,0:T(8,128)} %bitcast.7, f32[31,128,128]{2,1,0:T(8,128)} %cores_hbm.1), custom_call_target="tpu_custom_call" | custom-call | flops 1000 | bytes 1000 | tf_op jit(solution)/shard_map/couple/pallas_call | solution.py:48
  2.7 2.1 %collective-permute-start = (f32[192,128]{1,0:T(8,128)S(1)}, f32[192,128]{1,0:T(8,128)S(1)}, u32[]{:S(2)}, u32[]{:S(2)}) collective-permute-start(f32[192,128]{1,0:T(8,128)S(1)} %get-tuple-element.61), channel_id=1, source_target_pairs={{0,8},{4,12},{8,0},{12,4},{16,24},{20,28},{24,16},{28,20},{32,40},... | collective-permute-start | bytes 294920 | tf_op jit(solution)/shard_map/ppermute | solution.py:252
  4.8 1.0 %collective-permute-start.3 = (f32[256,256]{1,0:T(8,128)S(1)}, f32[256,256]{1,0:T(8,128)S(1)}, u32[]{:S(2)}, u32[]{:S(2)}) collective-permute-start(f32[256,256]{1,0:T(8,128)S(1)} %get-tuple-element.69.w), channel_id=1, source_target_pairs={{0,4},{4,0},{8,12},{12,8},{16,20},{20,16},{24,28},{28,24},{32,36},... | collective-permute-start | bytes 786440 | tf_op jit(solution)/shard_map/ppermute | solution.py:248
  5.7 0.0 copy-done.2
  5.7 0.0 copy-start
  5.7 2.2 %project.1 = (bf16[320,1024]{1,0:T(8,128)(2,1)S(1)}, bf16[320,1024]{1,0:T(8,128)(2,1)S(1)}, bf16[1024,1024]{1,0:T(8,128)(2,1)S(1)}, bf16[1024,1024]{1,0:T(8,128)(2,1)S(1)}) custom-call(bf16[320,1024]{1,0:T(8,128)(2,1)S(1)} %get-tuple-element.62.vh, bf16[320,1024]{1,0:T(8,128)(2,1)S(1)} %get-tuple-element.63.vl, f32[1024,1024]{1,0:T(8,128)S(1)} %copy-done.2), custom_call_target="tpu_custom_call" | custom-call | flops 1000 | bytes 1000 | tf_op jit(solution)/shard_map/project/pallas_call | solution.py:48
  8.0 0.0 copy-done
  8.0 1.2 %columns.2 = f32[320,512]{1,0:T(8,128)S(1)} custom-call(s32[1]{0:T(128)} %bitcast.me_ref.refs_0_, bf16[320,1024]{1,0:T(8,128)(2,1)S(1)} %get-tuple-element.67.refs_1_, bf16[320,1024]{1,0:T(8,128)(2,1)S(1)} %get-tuple-element.65.refs_2_, f32[1024,1024]{1,0:T(8,128)S(1)} %copy-done), custom_call_target="tpu_custom_call" | custom-call | flops 1000 | bytes 1000 | tf_op jit(solution)/shard_map/columns/pallas_call | solution.py:48
  9.2 0.1 collective-permute-start.2
  9.3 0.0 collective-permute-done.far
  9.3 0.5 %collective-permute-start.1 = (f32[192,128]{1,0:T(8,128)S(1)}, f32[192,128]{1,0:T(8,128)S(1)}, u32[]{:S(2)}, u32[]{:S(2)}) collective-permute-start(f32[192,128]{1,0:T(8,128)S(1)} %collective-permute-done.far), channel_id=1, source_target_pairs={{0,4},{4,0},{8,12},{12,8},{16,20},{20,16},{24,28},{28,24},{32,36},... | collective-permute-start | bytes 294920 | tf_op jit(solution)/shard_map/ppermute | solution.py:248
  9.8 1.2 %columns.3.g = f32[320,512]{1,0:T(8,128)S(1)} custom-call(s32[1]{0:T(128)} %bitcast.me_ref.refs_0_, bf16[320,1024]{1,0:T(8,128)(2,1)S(1)} %get-tuple-element.67.refs_1_, bf16[320,1024]{1,0:T(8,128)(2,1)S(1)} %get-tuple-element.65.refs_2_, f32[1024,1024]{1,0:T(8,128)S(1)} %copy-done), custom_call_target="tpu_custom_call" | custom-call | flops 10000000000 | bytes 1000 | tf_op jit(solution)/shard_map/columns/pallas_call | solution.py:48
  11.0 0.0 copy-start.1
  11.0 0.5 %collective-permute-done.1.far_got = f32[192,128]{1,0:T(8,128)S(1)} collective-permute-done((f32[192,128]{1,0:T(8,128)S(1)}, f32[192,128]{1,0:T(8,128)S(1)}, u32[]{:S(2)}, u32[]{:S(2)}) %collective-permute-start.1) | collective-permute-done | bytes 98336 | tf_op jit(solution)/shard_map/ppermute | solution.py:248
  11.5 0.0 collective-permute-done.3.w_got
  11.5 0.4 chip.1
  11.9 0.0 collective-permute-done.2.got
  11.9 0.9 %level4.1 = (f32[192,128]{1,0:T(8,128)S(1)}, f32[240,128]{1,0:T(8,128)S(1)}, f32[192,128]{1,0:T(8,128)S(1)}, f32[240,128]{1,0:T(8,128)S(1)}, f32[64,512]{1,0:T(8...) custom-call(s32[1]{0:T(128)} %bitcast.me_ref.refs_0_, f32[320,512]{1,0:T(8,128)S(1)} %columns.3.g, ...), custom_call_target="tpu_custom_call" | custom-call | flops 1000 | bytes 1000 | tf_op jit(solution)/shard_map/level4/pallas_call | solution.py:48
  12.8 2.5 %collective-permute-start.4 = (f32[240,128]{1,0:T(8,128)S(1)}, f32[240,128]{1,0:T(8,128)S(1)}, u32[]{:S(2)}, u32[]{:S(2)}) collective-permute-start(f32[240,128]{1,0:T(8,128)S(1)} %get-tuple-element.75), channel_id=1, source_target_pairs={{0,16},{4,20},{8,24},{12,28},{16,0},{20,4},{24,8},{28,12},{32,48},... | collective-permute-start | bytes 368648 | tf_op jit(solution)/shard_map/ppermute | solution.py:252
  15.3 0.1 collective-permute-start.6
  15.4 0.1 collective-permute-start.5
  15.5 0.0 copy-done.1
  15.5 0.6 %turn.1 = (bf16[1024,256]{1,0:T(8,128)(2,1)S(1)}, bf16[1024,256]{1,0:T(8,128)(2,1)S(1)}, bf16[1024,192]{1,0:T(8,128)(2,1)S(1)}) custom-call(f32[320,1024]{1,0:T(8,128)S(1)} %bitcast.8), custom_call_target="tpu_custom_call" | custom-call | flops 10 | bytes 1000 | tf_op jit(solution)/shard_map/turn/pallas_call | solution.py:48
  16.1 3.4 %leaf.3.refs_1_.refs_2_ = f32[1024,512]{1,0:T(8,128)S(1)} custom-call(s32[1]{0:T(128)} %bitcast.me_ref.refs_0_, bf16[1024,1024]{1,0:T(8,128)(2,1)S(1)} %get-tuple-element.103.refs_1_, bf16[1024,1024]{1,0:T(8,128)(2,1)S(1)} %get-tuple-element.81.refs_2_, f32[1024,1024]{1,0:T(8,128)S(1)} %copy-done), custom_call_target="tpu_custom_call" | custom-call | flops 1000 | bytes 1000 | tf_op jit(solution)/shard_map/leaf/pallas_call | solution.py:48
  19.5 1.2 %collective-permute-done.5.g1 = f32[192,128]{1,0:T(8,128)S(1)} collective-permute-done((f32[192,128]{1,0:T(8,128)S(1)}, f32[192,128]{1,0:T(8,128)S(1)}, u32[]{:S(2)}, u32[]{:S(2)}) %collective-permute-start.5) | collective-permute-done | bytes 98336 | tf_op jit(solution)/shard_map/ppermute | solution.py:252
  20.7 0.0 collective-permute-done.4.g2
  20.7 1.2 %collective-permute-done.6.g3 = f32[240,128]{1,0:T(8,128)S(1)} collective-permute-done((f32[240,128]{1,0:T(8,128)S(1)}, f32[240,128]{1,0:T(8,128)S(1)}, u32[]{:S(2)}, u32[]{:S(2)}) %collective-permute-start.6) | collective-permute-done | bytes 122912 | tf_op jit(solution)/shard_map/ppermute | solution.py:252
  22.0 0.4 level2.1
  22.3 3.7 %collective-permute-start.7 = (f32[160,128]{1,0:T(8,128)S(1)}, f32[160,128]{1,0:T(8,128)S(1)}, u32[]{:S(2)}, u32[]{:S(2)}) collective-permute-start(f32[160,128]{1,0:T(8,128)S(1)} %get-tuple-element.89), channel_id=1, source_target_pairs={{0,64},{4,68},{8,72},{12,76},{16,80},{20,84},{24,88},{28,92},{32,9... | collective-permute-start | bytes 245768 | tf_op jit(solution)/shard_map/ppermute | solution.py:252
  26.0 0.7 %collective-permute-start.8 = (f32[160,128]{1,0:T(8,128)S(1)}, f32[160,128]{1,0:T(8,128)S(1)}, u32[]{:S(2)}, u32[]{:S(2)}) collective-permute-start(f32[160,128]{1,0:T(8,128)S(1)} %get-tuple-element.90), channel_id=1, source_target_pairs={{0,32},{4,36},{8,40},{12,44},{16,48},{20,52},{24,56},{28,60},{32,0... | collective-permute-start | bytes 245768 | tf_op jit(solution)/shard_map/ppermute | solution.py:252
  26.7 0.0 collective-permute-start.9
  26.8 0.6 %collective-permute-start.13 = (f32[64,512]{1,0:T(8,128)S(1)}, f32[64,512]{1,0:T(8,128)S(1)}, u32[]{:S(2)}, u32[]{:S(2)}) collective-permute-start(f32[64,512]{1,0:T(8,128)S(1)} %get-tuple-element.105.own), channel_id=1, source_target_pairs={{0,8},{4,12},{8,0},{12,4},{16,24},{20,28},{24,16},{28,20},{32,40},... | collective-permute-start | bytes 393224 | tf_op jit(solution)/shard_map/ppermute | solution.py:252
  27.3 1.8 %leaf.4.refs_1_ = f32[1024,256]{1,0:T(8,128)S(1)} custom-call(s32[1]{0:T(128)} %bitcast.me_ref.refs_0_, bf16[1024,1024]{1,0:T(8,128)(2,1)S(1)} %get-tuple-element.103.refs_1_, bf16[1024,1024]{1,0:T(8,128)(2,1)S(1)} %get-tuple-element.81.refs_2_, f32[1024,1024]{1,0:T(8,128)S(1)} %copy-done), custom_call_target="tpu_custom_call" | custom-call | flops 1000 | bytes 1000 | tf_op jit(solution)/shard_map/leaf/pallas_call | solution.py:48
  29.1 0.0 collective-permute-done.7.s2
  29.1 0.8 %collective-permute-done.8.s1 = f32[160,128]{1,0:T(8,128)S(1)} collective-permute-done((f32[160,128]{1,0:T(8,128)S(1)}, f32[160,128]{1,0:T(8,128)S(1)}, u32[]{:S(2)}, u32[]{:S(2)}) %collective-permute-start.8) | collective-permute-done | bytes 81952 | tf_op jit(solution)/shard_map/ppermute | solution.py:252
  29.9 1.3 %collective-permute-done.9.s3 = f32[160,128]{1,0:T(8,128)S(1)} collective-permute-done((f32[160,128]{1,0:T(8,128)S(1)}, f32[160,128]{1,0:T(8,128)S(1)}, u32[]{:S(2)}, u32[]{:S(2)}) %collective-permute-start.9) | collective-permute-done | bytes 81952 | tf_op jit(solution)/shard_map/ppermute | solution.py:252
  31.3 0.6 %levels10.1 = (f32[192,128]{1,0:T(8,128)S(1)}, f32[192,128]{1,0:T(8,128)S(1)}, f32[192,128]{1,0:T(8,128)S(1)}, f32[192,128]{1,0:T(8,128)S(1)}) custom-call(s32[1]{0:T(128)} %bitcast.me_ref.refs_0_, f32[160,128]{1,0:T(8,128)S(1)} %get-tuple-element.95.s0, f32[160,128]{1,0:T(8,128)S(1)} %collective-permute-done.7.s2, ...), custom_call_target="tpu_custom_call" | custom-call | flops 1000 | bytes 1000 | tf_op jit(solution)/shard_map/levels10/pallas_call | solution.py:48
  31.8 1.3 %collective-permute-start.10 = (f32[192,128]{1,0:T(8,128)S(1)}, f32[192,128]{1,0:T(8,128)S(1)}, u32[]{:S(2)}, u32[]{:S(2)}) collective-permute-start(f32[192,128]{1,0:T(8,128)S(1)} %get-tuple-element.100), channel_id=1, source_target_pairs={{0,16},{4,20},{8,24},{12,28},{16,0},{20,4},{24,8},{28,12},{32,48},... | collective-permute-start | bytes 294920 | tf_op jit(solution)/shard_map/ppermute | solution.py:252
  33.1 1.5 %collective-permute-start.11 = (f32[192,128]{1,0:T(8,128)S(1)}, f32[192,128]{1,0:T(8,128)S(1)}, u32[]{:S(2)}, u32[]{:S(2)}) collective-permute-start(f32[192,128]{1,0:T(8,128)S(1)} %get-tuple-element.101), channel_id=1, source_target_pairs={{0,8},{4,12},{8,0},{12,4},{16,24},{20,28},{24,16},{28,20},{32,40},... | collective-permute-start | bytes 294920 | tf_op jit(solution)/shard_map/ppermute | solution.py:252
  34.6 0.5 %collective-permute-start.12 = (f32[192,128]{1,0:T(8,128)S(1)}, f32[192,128]{1,0:T(8,128)S(1)}, u32[]{:S(2)}, u32[]{:S(2)}) collective-permute-start(f32[192,128]{1,0:T(8,128)S(1)} %get-tuple-element.102), channel_id=1, source_target_pairs={{0,24},{4,28},{8,16},{12,20},{16,8},{20,12},{24,0},{28,4},{32,56},... | collective-permute-start | bytes 294920 | tf_op jit(solution)/shard_map/ppermute | solution.py:252
  35.1 1.8 %leaf.5.refs_2_ = f32[1024,256]{1,0:T(8,128)S(1)} custom-call(s32[1]{0:T(128)} %bitcast.me_ref.refs_0_, bf16[1024,1024]{1,0:T(8,128)(2,1)S(1)} %get-tuple-element.103.refs_1_, bf16[1024,1024]{1,0:T(8,128)(2,1)S(1)} %get-tuple-element.81.refs_2_, f32[1024,1024]{1,0:T(8,128)S(1)} %copy-done), custom_call_target="tpu_custom_call" | custom-call | flops 1000 | bytes 1000 | tf_op jit(solution)/shard_map/leaf/pallas_call | solution.py:48
  37.0 0.0 collective-permute-done.13.got
  37.0 0.2 level3.1.q3
  37.2 0.0 collective-permute-done.10.r2
  37.2 0.4 collective-permute-done.11.r1
  37.7 2.7 %collective-permute-done.12.r3 = f32[192,128]{1,0:T(8,128)S(1)} collective-permute-done((f32[192,128]{1,0:T(8,128)S(1)}, f32[192,128]{1,0:T(8,128)S(1)}, u32[]{:S(2)}, u32[]{:S(2)}) %collective-permute-start.12) | collective-permute-done | bytes 98336 | tf_op jit(solution)/shard_map/ppermute | solution.py:252
  40.3 0.1 assemble.1.refs_6_
  40.4 2.9 %collective-permute-start.14 = (f32[320,512]{1,0:T(8,128)S(1)}, f32[320,512]{1,0:T(8,128)S(1)}, u32[]{:S(2)}, u32[]{:S(2)}) collective-permute-start(f32[320,512]{1,0:T(8,128)S(1)} %assemble.1.refs_6_), channel_id=1, source_target_pairs={{0,4},{4,0},{8,12},{12,8},{16,20},{20,16},{24,28},{28,24},{32,36},... | collective-permute-start | bytes 1966088 | tf_op jit(solution)/shard_map/ppermute | solution.py:248
  43.3 2.2 %finish.2.refs_8_ = f32[1024,1024]{1,0:T(8,128)} custom-call(s32[1]{0:T(128)} %bitcast.me_ref.refs_0_, f32[1024,512]{1,0:T(8,128)S(1)} %leaf.3.refs_1_.refs_2_, f32[1024,512]{1,0:T(8,128)S(1)} %leaf.3.refs_1_.refs_2_, bf16[1024,256]{1,0:T(8,128)(2,1)S(1)} %get-tuple-element.107.refs_3_, bf16[1024,256]{1,0:T(8,128)(2,1)S(1)} %get-tuple-element.108.refs_4_, ...), custom_call_target="tpu_custom_call" | custom-call | flops 1000000000 | bytes 5242880 | tf_op jit(solution)/shard_map/finish/pallas_call | solution.py:340
  45.5 0.0 collective-permute-done.14.refs_6_
  45.6 2.2 %finish.3 = f32[1024,1024]{1,0:T(8,128)} custom-call(s32[1]{0:T(128)} %bitcast.me_ref.refs_0_, f32[1024,256]{1,0:T(8,128)S(1)} %leaf.4.refs_1_, f32[1024,256]{1,0:T(8,128)S(1)} %leaf.5.refs_2_, bf16[1024,256]{1,0:T(8,128)(2,1)S(1)} %get-tuple-element.107.refs_3_, bf16[1024,256]{1,0:T(8,128)(2,1)S(1)} %get-tuple-element.108.refs_4_, ...), custom_call_target="tpu_custom_call", output_to_operand_aliasing={{}: (8, {})} | custom-call | flops 1000000000 | bytes 5242880 | tf_op jit(solution)/shard_map/finish/pallas_call | solution.py:340
Async XLA Ops:
  0.0 5.7 %copy-start.2 = (f32[1024,1024]{1,0:T(8,128)S(1)}, f32[1024,1024]{1,0:T(8,128)}, u32[]{:S(2)}) copy-start(f32[1024,1024]{1,0:T(8,128)} %l.1) | copy-start | bytes 12582916
  2.7 6.6 %collective-permute-start = (f32[192,128]{1,0:T(8,128)S(1)}, f32[192,128]{1,0:T(8,128)S(1)}, u32[]{:S(2)}, u32[]{:S(2)}) collective-permute-start(f32[192,128]{1,0:T(8,128)S(1)} %get-tuple-element.61), channel_id=1, source_target_pairs={{0,8},{4,12},{8,0},{12,4},{16,24},{20,28},{24,16},{28,20},{32,40},... | collective-permute-start | bytes 294920 | tf_op jit(solution)/shard_map/ppermute | solution.py:252
  4.8 6.7 %collective-permute-start.3 = (f32[256,256]{1,0:T(8,128)S(1)}, f32[256,256]{1,0:T(8,128)S(1)}, u32[]{:S(2)}, u32[]{:S(2)}) collective-permute-start(f32[256,256]{1,0:T(8,128)S(1)} %get-tuple-element.69.w), channel_id=1, source_target_pairs={{0,4},{4,0},{8,12},{12,8},{16,20},{20,16},{24,28},{28,24},{32,36},... | collective-permute-start | bytes 786440 | tf_op jit(solution)/shard_map/ppermute | solution.py:248
  5.7 2.2 %copy-start = (f32[1024,1024]{1,0:T(8,128)S(1)}, f32[1024,1024]{1,0:T(8,128)}, u32[]{:S(2)}) copy-start(f32[1024,1024]{1,0:T(8,128)} %refs_3_.9) | copy-start | bytes 12582916
  9.2 2.7 %collective-permute-start.2 = (f32[320,512]{1,0:T(8,128)S(1)}, f32[320,512]{1,0:T(8,128)S(1)}, u32[]{:S(2)}, u32[]{:S(2)}) collective-permute-start(f32[320,512]{1,0:T(8,128)S(1)} %columns.2), channel_id=1, source_target_pairs={{0,4},{4,0},{8,12},{12,8},{16,20},{20,16},{24,28},{28,24},{32,36},... | collective-permute-start | bytes 1966088 | tf_op jit(solution)/shard_map/ppermute | solution.py:248
  9.3 2.2 %collective-permute-start.1 = (f32[192,128]{1,0:T(8,128)S(1)}, f32[192,128]{1,0:T(8,128)S(1)}, u32[]{:S(2)}, u32[]{:S(2)}) collective-permute-start(f32[192,128]{1,0:T(8,128)S(1)} %collective-permute-done.far), channel_id=1, source_target_pairs={{0,4},{4,0},{8,12},{12,8},{16,20},{20,16},{24,28},{28,24},{32,36},... | collective-permute-start | bytes 294920 | tf_op jit(solution)/shard_map/ppermute | solution.py:248
  11.0 4.6 %copy-start.1 = (f32[5,1024,64]{1,2,0:T(8,128)S(1)}, f32[5,1024,64]{1,2,0:T(8,128)}, u32[]{:S(2)}) copy-start(f32[5,1024,64]{1,2,0:T(8,128)} %param.7) | copy-start | bytes 3932164
  12.8 7.9 %collective-permute-start.4 = (f32[240,128]{1,0:T(8,128)S(1)}, f32[240,128]{1,0:T(8,128)S(1)}, u32[]{:S(2)}, u32[]{:S(2)}) collective-permute-start(f32[240,128]{1,0:T(8,128)S(1)} %get-tuple-element.75), channel_id=1, source_target_pairs={{0,16},{4,20},{8,24},{12,28},{16,0},{20,4},{24,8},{28,12},{32,48},... | collective-permute-start | bytes 368648 | tf_op jit(solution)/shard_map/ppermute | solution.py:252
  15.3 6.6 %collective-permute-start.6 = (f32[240,128]{1,0:T(8,128)S(1)}, f32[240,128]{1,0:T(8,128)S(1)}, u32[]{:S(2)}, u32[]{:S(2)}) collective-permute-start(f32[240,128]{1,0:T(8,128)S(1)} %get-tuple-element.77), channel_id=1, source_target_pairs={{0,24},{4,28},{8,16},{12,20},{16,8},{20,12},{24,0},{28,4},{32,56},... | collective-permute-start | bytes 368648 | tf_op jit(solution)/shard_map/ppermute | solution.py:252
  15.4 5.3 %collective-permute-start.5 = (f32[192,128]{1,0:T(8,128)S(1)}, f32[192,128]{1,0:T(8,128)S(1)}, u32[]{:S(2)}, u32[]{:S(2)}) collective-permute-start(f32[192,128]{1,0:T(8,128)S(1)} %get-tuple-element.76), channel_id=1, source_target_pairs={{0,8},{4,12},{8,0},{12,4},{16,24},{20,28},{24,16},{28,20},{32,40},... | collective-permute-start | bytes 294920 | tf_op jit(solution)/shard_map/ppermute | solution.py:252
  22.3 6.8 %collective-permute-start.7 = (f32[160,128]{1,0:T(8,128)S(1)}, f32[160,128]{1,0:T(8,128)S(1)}, u32[]{:S(2)}, u32[]{:S(2)}) collective-permute-start(f32[160,128]{1,0:T(8,128)S(1)} %get-tuple-element.89), channel_id=1, source_target_pairs={{0,64},{4,68},{8,72},{12,76},{16,80},{20,84},{24,88},{28,92},{32,9... | collective-permute-start | bytes 245768 | tf_op jit(solution)/shard_map/ppermute | solution.py:252
  26.0 3.9 %collective-permute-start.8 = (f32[160,128]{1,0:T(8,128)S(1)}, f32[160,128]{1,0:T(8,128)S(1)}, u32[]{:S(2)}, u32[]{:S(2)}) collective-permute-start(f32[160,128]{1,0:T(8,128)S(1)} %get-tuple-element.90), channel_id=1, source_target_pairs={{0,32},{4,36},{8,40},{12,44},{16,48},{20,52},{24,56},{28,60},{32,0... | collective-permute-start | bytes 245768 | tf_op jit(solution)/shard_map/ppermute | solution.py:252
  26.7 4.5 %collective-permute-start.9 = (f32[160,128]{1,0:T(8,128)S(1)}, f32[160,128]{1,0:T(8,128)S(1)}, u32[]{:S(2)}, u32[]{:S(2)}) collective-permute-start(f32[160,128]{1,0:T(8,128)S(1)} %get-tuple-element.91), channel_id=1, source_target_pairs={{0,96},{4,100},{8,104},{12,108},{16,112},{20,116},{24,120},{28,124... | collective-permute-start | bytes 245768 | tf_op jit(solution)/shard_map/ppermute | solution.py:252
  26.8 10.2 %collective-permute-start.13 = (f32[64,512]{1,0:T(8,128)S(1)}, f32[64,512]{1,0:T(8,128)S(1)}, u32[]{:S(2)}, u32[]{:S(2)}) collective-permute-start(f32[64,512]{1,0:T(8,128)S(1)} %get-tuple-element.105.own), channel_id=1, source_target_pairs={{0,8},{4,12},{8,0},{12,4},{16,24},{20,28},{24,16},{28,20},{32,40},... | collective-permute-start | bytes 393224 | tf_op jit(solution)/shard_map/ppermute | solution.py:252
  31.8 5.4 %collective-permute-start.10 = (f32[192,128]{1,0:T(8,128)S(1)}, f32[192,128]{1,0:T(8,128)S(1)}, u32[]{:S(2)}, u32[]{:S(2)}) collective-permute-start(f32[192,128]{1,0:T(8,128)S(1)} %get-tuple-element.100), channel_id=1, source_target_pairs={{0,16},{4,20},{8,24},{12,28},{16,0},{20,4},{24,8},{28,12},{32,48},... | collective-permute-start | bytes 294920 | tf_op jit(solution)/shard_map/ppermute | solution.py:252
  33.1 4.5 %collective-permute-start.11 = (f32[192,128]{1,0:T(8,128)S(1)}, f32[192,128]{1,0:T(8,128)S(1)}, u32[]{:S(2)}, u32[]{:S(2)}) collective-permute-start(f32[192,128]{1,0:T(8,128)S(1)} %get-tuple-element.101), channel_id=1, source_target_pairs={{0,8},{4,12},{8,0},{12,4},{16,24},{20,28},{24,16},{28,20},{32,40},... | collective-permute-start | bytes 294920 | tf_op jit(solution)/shard_map/ppermute | solution.py:252
  34.6 5.7 %collective-permute-start.12 = (f32[192,128]{1,0:T(8,128)S(1)}, f32[192,128]{1,0:T(8,128)S(1)}, u32[]{:S(2)}, u32[]{:S(2)}) collective-permute-start(f32[192,128]{1,0:T(8,128)S(1)} %get-tuple-element.102), channel_id=1, source_target_pairs={{0,24},{4,28},{8,16},{12,20},{16,8},{20,12},{24,0},{28,4},{32,56},... | collective-permute-start | bytes 294920 | tf_op jit(solution)/shard_map/ppermute | solution.py:252
  40.4 5.1 %collective-permute-start.14 = (f32[320,512]{1,0:T(8,128)S(1)}, f32[320,512]{1,0:T(8,128)S(1)}, u32[]{:S(2)}, u32[]{:S(2)}) collective-permute-start(f32[320,512]{1,0:T(8,128)S(1)} %assemble.1.refs_6_), channel_id=1, source_target_pairs={{0,4},{4,0},{8,12},{12,8},{16,20},{20,16},{24,28},{28,24},{32,36},... | collective-permute-start | bytes 1966088 | tf_op jit(solution)/shard_map/ppermute | solution.py:248

commit v4 on v3

--- a/solution.py
+++ b/solution.py
@@ -116,18 +116,16 @@
     return jnp.where(bit == 0, full[:, R:], full[:, :R])
 
 
-def kw(me_ref, w, w_got, far, far_got, sel, share, w_next):
-    me, bit = bits(me_ref)
-    own, other = pack(w[...]) + pack(w_got[...]), far[...] + far_got[...]
-    share[...] = own_share(sel.at[1], bit[1], own[:, :R], other[:, :R])
-    both = own[:, R:] + other[:, R:]
-    w_next[...] = jnp.concatenate([both[: 3 * R // 2], both[3 * R // 2 :]], 1)
-
-
-def k3(me_ref, g, got, w, w_got, share, w_next, sel, m0, m2, m1, m3, p3, q_mine, q_other, p, q, a):
+def kw(w, w_got, far, far_got, packed, packed_got):
+    packed[...] = pack(w[...]) + pack(w_got[...])
+    packed_got[...] = far[...] + far_got[...]
+
+
+def k3(me_ref, g, got, w, w_got, packed, packed_got, sel, m0, m2, m1, m3, p3, q_mine, q_other, w_next, p, q, a):
     me, bit = bits(me_ref)
     x = lax.rem(me >> 1, 4)
     c = bit[0]
+    share = own_share(sel.at[1], bit[1], packed[:, :R], packed_got[:, :R])
     stack(p, g[4 * R :, :], got[4 * R :, :], c)
     q[...] = mm(sel[0], p[...])
     mine, theirs = rows_of(q, c, True), rows_of(q, c, False)
@@ -137,11 +135,14 @@
     left = g[: 4 * R, :] + got[: 4 * R, :] - mm(wide, jnp.concatenate([mine, theirs], 0))
     third = left[3 * R :]
     p3[...] = third
-    a[...] = left[: 3 * R] - mm(share[...], third)
+    a[...] = left[: 3 * R] - mm(share, third)
     for d, out in ((2, m2), (1, m1), (3, m3), (0, m0)):
         out[: 3 * R, :] = a[:, pl.ds(pl.multiple_of((x ^ d) * 2 * R, 2 * R), 2 * R)]
-    m2[3 * R :, :] = w_next[: 3 * R // 4, :]
-    m3[3 * R :, :] = w_next[3 * R // 4 :, :]
+    both = packed[:, R:] + packed_got[:, R:]
+    both = jnp.concatenate([both[: 3 * R // 2], both[3 * R // 2 :]], 1)
+    w_next[...] = both
+    m2[3 * R :, :] = both[: 3 * R // 4]
+    m3[3 * R :, :] = both[3 * R // 4 :]
 
 
 def unfold(w):
@@ -193,13 +194,12 @@
     q[...] = mm(rows_of(sel.at[1], bit[1], True), p[...])
 
 
-def k6(me_ref, r0, r2, r1, r3, q3, q4, q_half):
+def k6(me_ref, r0, r2, r1, r3, q3, q_half):
     me, bit = bits(me_ref)
     x = lax.rem(me >> 1, 4)
     for d, r in ((0, r0), (1, r1), (2, r2), (3, r3)):
         q_half[: 3 * R, pl.ds(pl.multiple_of((x ^ d) * 2 * R, 2 * R), 2 * R)] = r[...]
-    q_half[3 * R : 4 * R, :] = q3[...]
-    q_half[4 * R :, :] = q4[...]
+    q_half[3 * R :, :] = q3[...]
 
 
 def ku(ut, uh_ref, ul_ref, u4):
@@ -210,32 +210,36 @@
     u4[...] = jnp.concatenate([h, l, h], 1)
 
 
-def kl(first, me_ref, lh, ll, b, x):
+def below(q):
+    h, l = split(q)
+    return jnp.concatenate([h, h, l], 0)
+
+
+def kl(first, me_ref, lh, ll, b, u4, q4, x):
     me, bit = bits(me_ref)
     n = b.shape[1] // 4
-    at = pl.multiple_of((bit[0] if first < 2 else 1 - bit[0]) * 2 * n + first % 2 * n, n)
-    x[...] = mm3((lh[...], ll[...]), split(b[:, pl.ds(at, x.shape[1])]))
+    within = first % 2 * n
+    at = pl.multiple_of((bit[0] if first < 2 else 1 - bit[0]) * 2 * n + within, n)
+    leaf = mm3((lh[...], ll[...]), split(b[:, pl.ds(at, x.shape[1])]))
+    x[...] = leaf - dot(u4[...], below(q4[:, within : within + x.shape[1]]))
 
 
 PARTS = 4
 
 
-def k7(mine, me_ref, xa, xb, uh, ul, u4, q, q4, *rest):
+def k7(mine, me_ref, xa, xb, uh, ul, q, *rest):
     out, buf, sem = rest[-3:]
     me, bit = bits(me_ref)
     half = q.shape[1]
     at = pl.multiple_of((bit[0] if mine else 1 - bit[0]) * half, half)
-    fourth = split(q4[...] if mine else q[4 * R :, :])
-    lower = jnp.concatenate([fourth[0], *fourth], 0)
-    qh, ql = split(q[: 4 * R, :])
-    upper = jnp.concatenate([qh, qh, ql], 0)
+    right = below(q[...])
     n = buf.shape[0] // PARTS
     copies = []
     for k in range(PARTS):
         r = slice(k * n, k * n + n)
         left = jnp.concatenate([uh[r, :], ul[r, :], uh[r, :]], 1)
         x = xa[r, :] if mine else jnp.concatenate([xa[r, :], xb[r, :]], 1)
-        buf[r, :] = x - dot(left, upper) - dot(u4[r, :], lower)
+        buf[r, :] = x - dot(left, right)
         copies.append(
             pltpu.make_async_copy(buf.at[pl.ds(k * n, n)], out.at[pl.ds(k * n, n), pl.ds(at, half)], sem.at[k])
         )
@@ -290,21 +294,21 @@
     far_got = to_other_core(far)
     g = image(True, after((yh, sent))[0])
     far_got, g = after((far_got, g))
-    share, w_next = call(
-        kw, (me, w, w_got, far, far_got, sel), [shape(3 * R, R), shape(3 * R // 2, 2 * R)], [SM] + [VM] * 5,
-        "chip", 10, MIB, 6,
-    )
-    *messages, p3, q4_mine, q4_other = call(
-        k3, (me, g, got, w, w_got, share, w_next, sel),
-        [shape(3 * R + k, eighth) for k in (0, 3 * R // 4, 0, 3 * R // 4)] + [shape(R, half)] * 3,
+    packed, packed_got = call(
+        kw, (w, w_got, far, far_got), [shape(3 * R, 2 * R)] * 2, [VM] * 4, "chip", 10, MIB, 4,
+    )
+    *messages, p3, q4_mine, q4_other, w_next = call(
+        k3, (me, g, got, w, w_got, packed, packed_got, sel),
+        [shape(3 * R + k, eighth) for k in (0, 3 * R // 4, 0, 3 * R // 4)] + [shape(R, half)] * 3
+        + [shape(3 * R // 2, 2 * R)],
         [SM] + [VM] * 7, "level4", 1000, 4 * MIB, 10,
         scratch=[pltpu.VMEM((2 * R, half), F32)] * 2 + [pltpu.VMEM((3 * R, half), F32)],
     )
 
-    def leaf(first, count, behind):
+    def leaf(first, count, q4, behind):
         return call(
-            lambda *refs: kl(first, *refs), (me, after((lh, behind))[0], ll, right_side),
-            [shape(rows, count * cols // 4)], [SM] + [VM] * 3, "leaf", 1000, 6 * MIB, 16,
+            lambda *refs: kl(first, *refs), (me, after((lh, behind))[0], ll, right_side, u4, q4),
+            [shape(rows, count * cols // 4)], [SM] + [VM] * 5, "leaf", 1000, 6 * MIB, 16,
         )[0]
 
     def turn(behind):
@@ -314,13 +318,15 @@
         )
 
     uh, ul, u4 = turn(q4_mine)
-    got, x_mine, uh = after((spread(messages, 1), leaf(0, 2, q4_mine), uh))
+    x_mine = leaf(0, 2, q4_mine, q4_mine)
+    q4_back = to_other_core(after((q4_other, x_mine))[0])
+    got, x_mine = after((spread(messages, 1), x_mine))
     small = [pltpu.VMEM((2 * R, eighth), F32)]
     *z, q2 = call(
         k4, (me, *got, w_next, sel), [shape(5 * R // 2, eighth)] * 4 + [shape(2, R, eighth)],
         [SM] + [VM] * 6, "level2", 1000, MIB, 8, scratch=small * 2,
     )
-    got, x2 = after((spread(z, 3), leaf(2, 1, q2)))
+    got, x2 = after((spread(z, 3), leaf(2, 1, q4_back, q2)))
     p3_got = along(after((p3, q2))[0], 1, 1)
     back = call(
         k5, (me, *got, sel, q2), [shape(3 * R, eighth)] * 4, [SM] + [VM] * 6, "levels10", 1000, MIB, 8,
@@ -330,9 +336,9 @@
         kq, (me, p3, p3_got, sel), [shape(R, half)], [SM] + [VM] * 3, "level3", 1000, MIB, 8,
         scratch=[pltpu.VMEM((2 * R, half), F32)],
     )
-    got, x3, q3 = after((spread(back, 1), leaf(3, 1, back[0]), q3))
+    got, x3, q3 = after((spread(back, 1), leaf(3, 1, q4_back, back[0]), q3))
     (q_half,) = call(
-        k6, (me, *got, q3, q4_other), [shape(5 * R, half)], [SM] + [VM] * 6, "assemble", 10, MIB, 8,
+        k6, (me, *got, q3), [shape(4 * R, half)], [SM] + [VM] * 5, "assemble", 10, MIB, 8,
     )
     q_rest = to_other_core(q_half)
 
@@ -340,14 +346,14 @@
         return pl.pallas_call(
             lambda *refs: k7(mine, *refs),
             out_shape=shape(rows, cols),
-            in_specs=[SM] + [VM] * 7 + [HB] * len(so_far),
+            in_specs=[SM] + [VM] * 5 + [HB] * len(so_far),
             out_specs=HB,
             scratch_shapes=[pltpu.VMEM((rows, half), F32), pltpu.SemaphoreType.DMA((PARTS,))],
             name="finish",
-            input_output_aliases={8: 0} if so_far else {},
+            input_output_aliases={6: 0} if so_far else {},
             cost_estimate=pl.CostEstimate(flops=10**9, bytes_accessed=5 * MIB, transcendentals=0),
             compiler_params=pltpu.CompilerParams(vmem_limit_bytes=12 * MIB),
-        )(me, xa, xb, uh, ul, u4, q, q4_mine, *so_far)
+        )(me, xa, xb, uh, ul, q, *so_far)
 
     out = finish(True, x_mine, x_mine, q_half)
     return finish(False, x2, x3, q_rest, out)

time: 48 us -> 47.1 us (0.981)
  waiting for transfers between devices: 8.21 us -> 6.52 us
  starting transfers between devices: 17.6 us -> 18.7 us
    ppermute x11, waiting for transfers between devices: 7.68 us -> 5.99 us  [along(): return lax.ppermute(value, 'rows', [(i, i ^ d << shift) for i in range(32)])]
    ppermute x4 -> x5, starting transfers between devices: 4.46 us -> 5.53 us  [to_other_core(): return lax.ppermute(value, 'rows', [(i, i ^ 1) for i in range(32)])]
    pallas_call x2, Pallas kernels: 4.38 us -> 3.72 us  [finish(): pl.pallas_call(lambda *refs: k7(mine, *refs), out_shape=shape(rows, cols)...]
  transfers between devices with their start and end apart: 15 -> 16, of which waited for: 7 -> 6; matrix products, arithmetic and copies ran while one was open for 0% -> 0% of each run, Pallas kernels for 32% -> 34%
where the time goes in v4:
time: 47.1 us; the launch traced here: 47 us
  Pallas kernels  21.4 us (45%)
  starting transfers between devices  18.7 us (40%)
  waiting for transfers between devices  6.52 us (14%)
    pallas_call x14, Pallas kernels, call(): pl.pallas_call(kernel, out_shape=tuple(outs), in_specs=specs, out_specs=t...  17.7 us
    ppermute x11, starting transfers between devices, along(): return lax.ppermute(value, 'rows', [(i, i ^ d << shift) for i in range(32)])  13.2 us
    ppermute x11, waiting for transfers between devices, along(): return lax.ppermute(value, 'rows', [(i, i ^ d << shift) for i in range(32)])  5.99 us
    ppermute x5, starting transfers between devices, to_other_core(): return lax.ppermute(value, 'rows', [(i, i ^ 1) for i in range(32)])  5.53 us
    pallas_call x2, Pallas kernels, finish(): pl.pallas_call(lambda *refs: k7(mine, *refs), out_shape=shape(rows, cols)...  3.72 us
  transfers between devices with their start and end apart: 16, of which 6 were waited for; matrix products, arithmetic and copies ran while one was open for 0% of the time, Pallas kernels for 34%

profile of v4, /device:TPU:1, one launch (start us, length us, event | category | flops | bytes accessed | tf_op | source)
XLA Modules:
  0.0 47.0 jit_solution(566795913437669518)
XLA Ops:
  0.0 0.0 copy-start.2
  0.0 2.6 %couple.1 = (f32[256,256]{1,0:T(8,128)S(1)}, f32[192,128]{1,0:T(8,128)S(1)}, bf16[320,1024]{1,0:T(8,128)(2,1)S(1)}, bf16[320,1024]{1,0:T(8,128)(2,1)S(1)}, f32[6,128,128]{2,1,0:T(8,128)S(1)}) custom-call(s32[1]{0:T(128)} %bitcast.me_ref.refs_0_, f32[320,1024]{1,0:T(8,128)} %bitcast.9, f32[320,1024]{1,0:T(8,128)} %bitcast.7, f32[31,128,128]{2,1,0:T(8,128)} %cores_hbm.1), custom_call_target="tpu_custom_call" | custom-call | flops 1000 | bytes 1000 | tf_op jit(solution)/shard_map/couple/pallas_call | solution.py:48
  2.7 2.1 %collective-permute-start = (f32[192,128]{1,0:T(8,128)S(1)}, f32[192,128]{1,0:T(8,128)S(1)}, u32[]{:S(2)}, u32[]{:S(2)}) collective-permute-start(f32[192,128]{1,0:T(8,128)S(1)} %get-tuple-element.62), channel_id=1, source_target_pairs={{0,8},{4,12},{8,0},{12,4},{16,24},{20,28},{24,16},{28,20},{32,40},... | collective-permute-start | bytes 294920 | tf_op jit(solution)/shard_map/ppermute | solution.py:256
  4.8 1.0 %collective-permute-start.3 = (f32[256,256]{1,0:T(8,128)S(1)}, f32[256,256]{1,0:T(8,128)S(1)}, u32[]{:S(2)}, u32[]{:S(2)}) collective-permute-start(f32[256,256]{1,0:T(8,128)S(1)} %get-tuple-element.70.w), channel_id=1, source_target_pairs={{0,4},{4,0},{8,12},{12,8},{16,20},{20,16},{24,28},{28,24},{32,36},... | collective-permute-start | bytes 786440 | tf_op jit(solution)/shard_map/ppermute | solution.py:252
  5.7 0.0 copy-done.2
  5.7 0.0 copy-start
  5.7 2.2 %project.1 = (bf16[320,1024]{1,0:T(8,128)(2,1)S(1)}, bf16[320,1024]{1,0:T(8,128)(2,1)S(1)}, bf16[1024,1024]{1,0:T(8,128)(2,1)S(1)}, bf16[1024,1024]{1,0:T(8,128)(2,1)S(1)}) custom-call(bf16[320,1024]{1,0:T(8,128)(2,1)S(1)} %get-tuple-element.63.vh, bf16[320,1024]{1,0:T(8,128)(2,1)S(1)} %get-tuple-element.64.vl, f32[1024,1024]{1,0:T(8,128)S(1)} %copy-done.2), custom_call_target="tpu_custom_call" | custom-call | flops 1000 | bytes 1000 | tf_op jit(solution)/shard_map/project/pallas_call | solution.py:48
  8.0 0.0 copy-done
  8.0 1.2 %columns.2 = f32[320,512]{1,0:T(8,128)S(1)} custom-call(s32[1]{0:T(128)} %bitcast.me_ref.refs_0_, bf16[320,1024]{1,0:T(8,128)(2,1)S(1)} %get-tuple-element.68.refs_1_, bf16[320,1024]{1,0:T(8,128)(2,1)S(1)} %get-tuple-element.66.refs_2_, f32[1024,1024]{1,0:T(8,128)S(1)} %copy-done), custom_call_target="tpu_custom_call" | custom-call | flops 1000 | bytes 1000 | tf_op jit(solution)/shard_map/columns/pallas_call | solution.py:48
  9.2 0.1 collective-permute-start.2
  9.3 0.0 collective-permute-done.far
  9.3 0.5 %collective-permute-start.1 = (f32[192,128]{1,0:T(8,128)S(1)}, f32[192,128]{1,0:T(8,128)S(1)}, u32[]{:S(2)}, u32[]{:S(2)}) collective-permute-start(f32[192,128]{1,0:T(8,128)S(1)} %collective-permute-done.far), channel_id=1, source_target_pairs={{0,4},{4,0},{8,12},{12,8},{16,20},{20,16},{24,28},{28,24},{32,36},... | collective-permute-start | bytes 294920 | tf_op jit(solution)/shard_map/ppermute | solution.py:252
  9.8 1.2 %columns.3.g = f32[320,512]{1,0:T(8,128)S(1)} custom-call(s32[1]{0:T(128)} %bitcast.me_ref.refs_0_, bf16[320,1024]{1,0:T(8,128)(2,1)S(1)} %get-tuple-element.68.refs_1_, bf16[320,1024]{1,0:T(8,128)(2,1)S(1)} %get-tuple-element.66.refs_2_, f32[1024,1024]{1,0:T(8,128)S(1)} %copy-done), custom_call_target="tpu_custom_call" | custom-call | flops 10000000000 | bytes 1000 | tf_op jit(solution)/shard_map/columns/pallas_call | solution.py:48
  11.0 0.0 copy-start.1
  11.0 0.5 %collective-permute-done.1.far_got = f32[192,128]{1,0:T(8,128)S(1)} collective-permute-done((f32[192,128]{1,0:T(8,128)S(1)}, f32[192,128]{1,0:T(8,128)S(1)}, u32[]{:S(2)}, u32[]{:S(2)}) %collective-permute-start.1) | collective-permute-done | bytes 98336 | tf_op jit(solution)/shard_map/ppermute | solution.py:252
  11.5 0.0 collective-permute-done.3.w_got
  11.5 0.1 chip.1
  11.6 0.0 collective-permute-done.2.got
  11.6 1.0 %level4.1 = (f32[192,128]{1,0:T(8,128)S(1)}, f32[240,128]{1,0:T(8,128)S(1)}, f32[192,128]{1,0:T(8,128)S(1)}, f32[240,128]{1,0:T(8,128)S(1)}, f32[64,512]{1,0:T(8...) custom-call(s32[1]{0:T(128)} %bitcast.me_ref.refs_0_, f32[320,512]{1,0:T(8,128)S(1)} %columns.3.g, ...), custom_call_target="tpu_custom_call" | custom-call | flops 1000 | bytes 1000 | tf_op jit(solution)/shard_map/level4/pallas_call | solution.py:48
  12.6 2.5 %collective-permute-start.4 = (f32[240,128]{1,0:T(8,128)S(1)}, f32[240,128]{1,0:T(8,128)S(1)}, u32[]{:S(2)}, u32[]{:S(2)}) collective-permute-start(f32[240,128]{1,0:T(8,128)S(1)} %get-tuple-element.76), channel_id=1, source_target_pairs={{0,16},{4,20},{8,24},{12,28},{16,0},{20,4},{24,8},{28,12},{32,48},... | collective-permute-start | bytes 368648 | tf_op jit(solution)/shard_map/ppermute | solution.py:256
  15.1 0.1 collective-permute-start.6
  15.2 0.1 collective-permute-start.5
  15.3 0.0 copy-done.1
  15.3 0.6 %turn.1 = (bf16[1024,256]{1,0:T(8,128)(2,1)S(1)}, bf16[1024,256]{1,0:T(8,128)(2,1)S(1)}, bf16[1024,192]{1,0:T(8,128)(2,1)S(1)}) custom-call(f32[320,1024]{1,0:T(8,128)S(1)} %bitcast.8), custom_call_target="tpu_custom_call" | custom-call | flops 10 | bytes 1000 | tf_op jit(solution)/shard_map/turn/pallas_call | solution.py:48
  15.9 3.7 %leaf.3.refs_1_.refs_2_ = f32[1024,512]{1,0:T(8,128)S(1)} custom-call(s32[1]{0:T(128)} %bitcast.me_ref.refs_0_, bf16[1024,1024]{1,0:T(8,128)(2,1)S(1)} %get-tuple-element.107.refs_1_, bf16[1024,1024]{1,0:T(8,128)(2,1)S(1)} %get-tuple-element.82.refs_2_, f32[1024,1024]{1,0:T(8,128)S(1)} %copy-done, bf16[1024,192]{1,0:T(8,128)(2,1)S(1)} %get-tuple-element.84.refs_4_, ...), custom_call_target="tpu_custom_call" | custom-call | flops 1000 | bytes 1000 | tf_op jit(solution)/shard_map/leaf/pallas_call | solution.py:48
  19.6 1.1 %collective-permute-start.10 = (f32[64,512]{1,0:T(8,128)S(1)}, f32[64,512]{1,0:T(8,128)S(1)}, u32[]{:S(2)}, u32[]{:S(2)}) collective-permute-start(f32[64,512]{1,0:T(8,128)S(1)} %get-tuple-element.97), channel_id=1, source_target_pairs={{0,4},{4,0},{8,12},{12,8},{16,20},{20,16},{24,28},{28,24},{32,36},... | collective-permute-start | bytes 393224 | tf_op jit(solution)/shard_map/ppermute | solution.py:252
  20.6 0.0 collective-permute-done.5.g1
  20.6 0.0 collective-permute-done.4.g2
  20.6 1.1 %collective-permute-done.6.g3 = f32[240,128]{1,0:T(8,128)S(1)} collective-permute-done((f32[240,128]{1,0:T(8,128)S(1)}, f32[240,128]{1,0:T(8,128)S(1)}, u32[]{:S(2)}, u32[]{:S(2)}) %collective-permute-start.6) | collective-permute-done | bytes 122912 | tf_op jit(solution)/shard_map/ppermute | solution.py:256
  21.7 0.4 level2.1
  22.1 3.7 %collective-permute-start.7 = (f32[160,128]{1,0:T(8,128)S(1)}, f32[160,128]{1,0:T(8,128)S(1)}, u32[]{:S(2)}, u32[]{:S(2)}) collective-permute-start(f32[160,128]{1,0:T(8,128)S(1)} %get-tuple-element.91), channel_id=1, source_target_pairs={{0,64},{4,68},{8,72},{12,76},{16,80},{20,84},{24,88},{28,92},{32,9... | collective-permute-start | bytes 245768 | tf_op jit(solution)/shard_map/ppermute | solution.py:256
  25.8 0.7 %collective-permute-start.8 = (f32[160,128]{1,0:T(8,128)S(1)}, f32[160,128]{1,0:T(8,128)S(1)}, u32[]{:S(2)}, u32[]{:S(2)}) collective-permute-start(f32[160,128]{1,0:T(8,128)S(1)} %get-tuple-element.92), channel_id=1, source_target_pairs={{0,32},{4,36},{8,40},{12,44},{16,48},{20,52},{24,56},{28,60},{32,0... | collective-permute-start | bytes 245768 | tf_op jit(solution)/shard_map/ppermute | solution.py:256
  26.5 0.0 collective-permute-start.9
  26.5 0.6 %collective-permute-start.14 = (f32[64,512]{1,0:T(8,128)S(1)}, f32[64,512]{1,0:T(8,128)S(1)}, u32[]{:S(2)}, u32[]{:S(2)}) collective-permute-start(f32[64,512]{1,0:T(8,128)S(1)} %get-tuple-element.109.own), channel_id=1, source_target_pairs={{0,8},{4,12},{8,0},{12,4},{16,24},{20,28},{24,16},{28,20},{32,40},... | collective-permute-start | bytes 393224 | tf_op jit(solution)/shard_map/ppermute | solution.py:256
  27.1 0.0 collective-permute-done.10.refs_5_
  27.1 2.0 %leaf.4.refs_1_ = f32[1024,256]{1,0:T(8,128)S(1)} custom-call(s32[1]{0:T(128)} %bitcast.me_ref.refs_0_, bf16[1024,1024]{1,0:T(8,128)(2,1)S(1)} %get-tuple-element.107.refs_1_, bf16[1024,1024]{1,0:T(8,128)(2,1)S(1)} %get-tuple-element.82.refs_2_, f32[1024,1024]{1,0:T(8,128)S(1)} %copy-done, bf16[1024,192]{1,0:T(8,128)(2,1)S(1)} %get-tuple-element.84.refs_4_, ...), custom_call_target="tpu_custom_call" | custom-call | flops 1000 | bytes 1000 | tf_op jit(solution)/shard_map/leaf/pallas_call | solution.py:48
  29.1 0.0 collective-permute-done.7.s2
  29.1 0.6 %collective-permute-done.8.s1 = f32[160,128]{1,0:T(8,128)S(1)} collective-permute-done((f32[160,128]{1,0:T(8,128)S(1)}, f32[160,128]{1,0:T(8,128)S(1)}, u32[]{:S(2)}, u32[]{:S(2)}) %collective-permute-start.8) | collective-permute-done | bytes 81952 | tf_op jit(solution)/shard_map/ppermute | solution.py:256
  29.7 1.3 %collective-permute-done.9.s3 = f32[160,128]{1,0:T(8,128)S(1)} collective-permute-done((f32[160,128]{1,0:T(8,128)S(1)}, f32[160,128]{1,0:T(8,128)S(1)}, u32[]{:S(2)}, u32[]{:S(2)}) %collective-permute-start.9) | collective-permute-done | bytes 81952 | tf_op jit(solution)/shard_map/ppermute | solution.py:256
  31.0 0.6 %levels10.1 = (f32[192,128]{1,0:T(8,128)S(1)}, f32[192,128]{1,0:T(8,128)S(1)}, f32[192,128]{1,0:T(8,128)S(1)}, f32[192,128]{1,0:T(8,128)S(1)}) custom-call(s32[1]{0:T(128)} %bitcast.me_ref.refs_0_, f32[160,128]{1,0:T(8,128)S(1)} %get-tuple-element.99.s0, f32[160,128]{1,0:T(8,128)S(1)} %collective-permute-done.7.s2, ...), custom_call_target="tpu_custom_call" | custom-call | flops 1000 | bytes 1000 | tf_op jit(solution)/shard_map/levels10/pallas_call | solution.py:48
  31.6 2.7 %collective-permute-start.11 = (f32[192,128]{1,0:T(8,128)S(1)}, f32[192,128]{1,0:T(8,128)S(1)}, u32[]{:S(2)}, u32[]{:S(2)}) collective-permute-start(f32[192,128]{1,0:T(8,128)S(1)} %get-tuple-element.104), channel_id=1, source_target_pairs={{0,16},{4,20},{8,24},{12,28},{16,0},{20,4},{24,8},{28,12},{32,48},... | collective-permute-start | bytes 294920 | tf_op jit(solution)/shard_map/ppermute | solution.py:256
  34.3 0.1 collective-permute-start.12
  34.4 0.5 %collective-permute-start.13 = (f32[192,128]{1,0:T(8,128)S(1)}, f32[192,128]{1,0:T(8,128)S(1)}, u32[]{:S(2)}, u32[]{:S(2)}) collective-permute-start(f32[192,128]{1,0:T(8,128)S(1)} %get-tuple-element.106), channel_id=1, source_target_pairs={{0,24},{4,28},{8,16},{12,20},{16,8},{20,12},{24,0},{28,4},{32,56},... | collective-permute-start | bytes 294920 | tf_op jit(solution)/shard_map/ppermute | solution.py:256
  34.9 2.0 %leaf.5.refs_2_ = f32[1024,256]{1,0:T(8,128)S(1)} custom-call(s32[1]{0:T(128)} %bitcast.me_ref.refs_0_, bf16[1024,1024]{1,0:T(8,128)(2,1)S(1)} %get-tuple-element.107.refs_1_, bf16[1024,1024]{1,0:T(8,128)(2,1)S(1)} %get-tuple-element.82.refs_2_, f32[1024,1024]{1,0:T(8,128)S(1)} %copy-done, bf16[1024,192]{1,0:T(8,128)(2,1)S(1)} %get-tuple-element.84.refs_4_, ...), custom_call_target="tpu_custom_call" | custom-call | flops 1000 | bytes 1000 | tf_op jit(solution)/shard_map/leaf/pallas_call | solution.py:48
  36.9 0.0 collective-permute-done.14.got
  36.9 0.2 level3.1.q3
  37.1 0.0 collective-permute-done.11.r2
  37.1 0.6 %collective-permute-done.12.r1 = f32[192,128]{1,0:T(8,128)S(1)} collective-permute-done((f32[192,128]{1,0:T(8,128)S(1)}, f32[192,128]{1,0:T(8,128)S(1)}, u32[]{:S(2)}, u32[]{:S(2)}) %collective-permute-start.12) | collective-permute-done | bytes 98336 | tf_op jit(solution)/shard_map/ppermute | solution.py:256
  37.7 2.4 %collective-permute-done.13.r3 = f32[192,128]{1,0:T(8,128)S(1)} collective-permute-done((f32[192,128]{1,0:T(8,128)S(1)}, f32[192,128]{1,0:T(8,128)S(1)}, u32[]{:S(2)}, u32[]{:S(2)}) %collective-permute-start.13) | collective-permute-done | bytes 98336 | tf_op jit(solution)/shard_map/ppermute | solution.py:256
  40.1 0.1 assemble.1.refs_5_
  40.2 2.9 %collective-permute-start.15 = (f32[256,512]{1,0:T(8,128)S(1)}, f32[256,512]{1,0:T(8,128)S(1)}, u32[]{:S(2)}, u32[]{:S(2)}) collective-permute-start(f32[256,512]{1,0:T(8,128)S(1)} %assemble.1.refs_5_), channel_id=1, source_target_pairs={{0,4},{4,0},{8,12},{12,8},{16,20},{20,16},{24,28},{28,24},{32,36},... | collective-permute-start | bytes 1572872 | tf_op jit(solution)/shard_map/ppermute | solution.py:252
  43.1 1.8 %finish.2.refs_6_ = f32[1024,1024]{1,0:T(8,128)} custom-call(s32[1]{0:T(128)} %bitcast.me_ref.refs_0_, f32[1024,512]{1,0:T(8,128)S(1)} %leaf.3.refs_1_.refs_2_, f32[1024,512]{1,0:T(8,128)S(1)} %leaf.3.refs_1_.refs_2_, bf16[1024,256]{1,0:T(8,128)(2,1)S(1)} %get-tuple-element.111.refs_3_, bf16[1024,256]{1,0:T(8,128)(2,1)S(1)} %get-tuple-element.112.refs_4_, ...), custom_call_target="tpu_custom_call" | custom-call | flops 1000000000 | bytes 5242880 | tf_op jit(solution)/shard_map/finish/pallas_call | solution.py:346
  45.0 0.0 collective-permute-done.15.refs_5_
  45.0 1.9 %finish.3 = f32[1024,1024]{1,0:T(8,128)} custom-call(s32[1]{0:T(128)} %bitcast.me_ref.refs_0_, f32[1024,256]{1,0:T(8,128)S(1)} %leaf.4.refs_1_, f32[1024,256]{1,0:T(8,128)S(1)} %leaf.5.refs_2_, bf16[1024,256]{1,0:T(8,128)(2,1)S(1)} %get-tuple-element.111.refs_3_, bf16[1024,256]{1,0:T(8,128)(2,1)S(1)} %get-tuple-element.112.refs_4_, ...), custom_call_target="tpu_custom_call", output_to_operand_aliasing={{}: (6, {})} | custom-call | flops 1000000000 | bytes 5242880 | tf_op jit(solution)/shard_map/finish/pallas_call | solution.py:346
Async XLA Ops:
  0.0 5.7 %copy-start.2 = (f32[1024,1024]{1,0:T(8,128)S(1)}, f32[1024,1024]{1,0:T(8,128)}, u32[]{:S(2)}) copy-start(f32[1024,1024]{1,0:T(8,128)} %l.1) | copy-start | bytes 12582916
  2.7 6.6 %collective-permute-start = (f32[192,128]{1,0:T(8,128)S(1)}, f32[192,128]{1,0:T(8,128)S(1)}, u32[]{:S(2)}, u32[]{:S(2)}) collective-permute-start(f32[192,128]{1,0:T(8,128)S(1)} %get-tuple-element.62), channel_id=1, source_target_pairs={{0,8},{4,12},{8,0},{12,4},{16,24},{20,28},{24,16},{28,20},{32,40},... | collective-permute-start | bytes 294920 | tf_op jit(solution)/shard_map/ppermute | solution.py:256
  4.8 6.7 %collective-permute-start.3 = (f32[256,256]{1,0:T(8,128)S(1)}, f32[256,256]{1,0:T(8,128)S(1)}, u32[]{:S(2)}, u32[]{:S(2)}) collective-permute-start(f32[256,256]{1,0:T(8,128)S(1)} %get-tuple-element.70.w), channel_id=1, source_target_pairs={{0,4},{4,0},{8,12},{12,8},{16,20},{20,16},{24,28},{28,24},{32,36},... | collective-permute-start | bytes 786440 | tf_op jit(solution)/shard_map/ppermute | solution.py:252
  5.7 2.2 %copy-start = (f32[1024,1024]{1,0:T(8,128)S(1)}, f32[1024,1024]{1,0:T(8,128)}, u32[]{:S(2)}) copy-start(f32[1024,1024]{1,0:T(8,128)} %refs_3_.9) | copy-start | bytes 12582916
  9.2 2.4 %collective-permute-start.2 = (f32[320,512]{1,0:T(8,128)S(1)}, f32[320,512]{1,0:T(8,128)S(1)}, u32[]{:S(2)}, u32[]{:S(2)}) collective-permute-start(f32[320,512]{1,0:T(8,128)S(1)} %columns.2), channel_id=1, source_target_pairs={{0,4},{4,0},{8,12},{12,8},{16,20},{20,16},{24,28},{28,24},{32,36},... | collective-permute-start | bytes 1966088 | tf_op jit(solution)/shard_map/ppermute | solution.py:252
  9.3 2.2 %collective-permute-start.1 = (f32[192,128]{1,0:T(8,128)S(1)}, f32[192,128]{1,0:T(8,128)S(1)}, u32[]{:S(2)}, u32[]{:S(2)}) collective-permute-start(f32[192,128]{1,0:T(8,128)S(1)} %collective-permute-done.far), channel_id=1, source_target_pairs={{0,4},{4,0},{8,12},{12,8},{16,20},{20,16},{24,28},{28,24},{32,36},... | collective-permute-start | bytes 294920 | tf_op jit(solution)/shard_map/ppermute | solution.py:252
  11.0 4.3 %copy-start.1 = (f32[5,1024,64]{1,2,0:T(8,128)S(1)}, f32[5,1024,64]{1,2,0:T(8,128)}, u32[]{:S(2)}) copy-start(f32[5,1024,64]{1,2,0:T(8,128)} %param.7) | copy-start | bytes 3932164
  12.6 8.1 %collective-permute-start.4 = (f32[240,128]{1,0:T(8,128)S(1)}, f32[240,128]{1,0:T(8,128)S(1)}, u32[]{:S(2)}, u32[]{:S(2)}) collective-permute-start(f32[240,128]{1,0:T(8,128)S(1)} %get-tuple-element.76), channel_id=1, source_target_pairs={{0,16},{4,20},{8,24},{12,28},{16,0},{20,4},{24,8},{28,12},{32,48},... | collective-permute-start | bytes 368648 | tf_op jit(solution)/shard_map/ppermute | solution.py:256
  15.1 6.6 %collective-permute-start.6 = (f32[240,128]{1,0:T(8,128)S(1)}, f32[240,128]{1,0:T(8,128)S(1)}, u32[]{:S(2)}, u32[]{:S(2)}) collective-permute-start(f32[240,128]{1,0:T(8,128)S(1)} %get-tuple-element.78), channel_id=1, source_target_pairs={{0,24},{4,28},{8,16},{12,20},{16,8},{20,12},{24,0},{28,4},{32,56},... | collective-permute-start | bytes 368648 | tf_op jit(solution)/shard_map/ppermute | solution.py:256
  15.2 5.4 %collective-permute-start.5 = (f32[192,128]{1,0:T(8,128)S(1)}, f32[192,128]{1,0:T(8,128)S(1)}, u32[]{:S(2)}, u32[]{:S(2)}) collective-permute-start(f32[192,128]{1,0:T(8,128)S(1)} %get-tuple-element.77), channel_id=1, source_target_pairs={{0,8},{4,12},{8,0},{12,4},{16,24},{20,28},{24,16},{28,20},{32,40},... | collective-permute-start | bytes 294920 | tf_op jit(solution)/shard_map/ppermute | solution.py:256
  19.6 7.5 %collective-permute-start.10 = (f32[64,512]{1,0:T(8,128)S(1)}, f32[64,512]{1,0:T(8,128)S(1)}, u32[]{:S(2)}, u32[]{:S(2)}) collective-permute-start(f32[64,512]{1,0:T(8,128)S(1)} %get-tuple-element.97), channel_id=1, source_target_pairs={{0,4},{4,0},{8,12},{12,8},{16,20},{20,16},{24,28},{28,24},{32,36},... | collective-permute-start | bytes 393224 | tf_op jit(solution)/shard_map/ppermute | solution.py:252
  22.1 7.0 %collective-permute-start.7 = (f32[160,128]{1,0:T(8,128)S(1)}, f32[160,128]{1,0:T(8,128)S(1)}, u32[]{:S(2)}, u32[]{:S(2)}) collective-permute-start(f32[160,128]{1,0:T(8,128)S(1)} %get-tuple-element.91), channel_id=1, source_target_pairs={{0,64},{4,68},{8,72},{12,76},{16,80},{20,84},{24,88},{28,92},{32,9... | collective-permute-start | bytes 245768 | tf_op jit(solution)/shard_map/ppermute | solution.py:256
  25.8 3.9 %collective-permute-start.8 = (f32[160,128]{1,0:T(8,128)S(1)}, f32[160,128]{1,0:T(8,128)S(1)}, u32[]{:S(2)}, u32[]{:S(2)}) collective-permute-start(f32[160,128]{1,0:T(8,128)S(1)} %get-tuple-element.92), channel_id=1, source_target_pairs={{0,32},{4,36},{8,40},{12,44},{16,48},{20,52},{24,56},{28,60},{32,0... | collective-permute-start | bytes 245768 | tf_op jit(solution)/shard_map/ppermute | solution.py:256
  26.5 4.5 %collective-permute-start.9 = (f32[160,128]{1,0:T(8,128)S(1)}, f32[160,128]{1,0:T(8,128)S(1)}, u32[]{:S(2)}, u32[]{:S(2)}) collective-permute-start(f32[160,128]{1,0:T(8,128)S(1)} %get-tuple-element.93), channel_id=1, source_target_pairs={{0,96},{4,100},{8,104},{12,108},{16,112},{20,116},{24,120},{28,124... | collective-permute-start | bytes 245768 | tf_op jit(solution)/shard_map/ppermute | solution.py:256
  26.5 10.4 %collective-permute-start.14 = (f32[64,512]{1,0:T(8,128)S(1)}, f32[64,512]{1,0:T(8,128)S(1)}, u32[]{:S(2)}, u32[]{:S(2)}) collective-permute-start(f32[64,512]{1,0:T(8,128)S(1)} %get-tuple-element.109.own), channel_id=1, source_target_pairs={{0,8},{4,12},{8,0},{12,4},{16,24},{20,28},{24,16},{28,20},{32,40},... | collective-permute-start | bytes 393224 | tf_op jit(solution)/shard_map/ppermute | solution.py:256
  31.6 5.6 %collective-permute-start.11 = (f32[192,128]{1,0:T(8,128)S(1)}, f32[192,128]{1,0:T(8,128)S(1)}, u32[]{:S(2)}, u32[]{:S(2)}) collective-permute-start(f32[192,128]{1,0:T(8,128)S(1)} %get-tuple-element.104), channel_id=1, source_target_pairs={{0,16},{4,20},{8,24},{12,28},{16,0},{20,4},{24,8},{28,12},{32,48},... | collective-permute-start | bytes 294920 | tf_op jit(solution)/shard_map/ppermute | solution.py:256
  34.3 3.5 %collective-permute-start.12 = (f32[192,128]{1,0:T(8,128)S(1)}, f32[192,128]{1,0:T(8,128)S(1)}, u32[]{:S(2)}, u32[]{:S(2)}) collective-permute-start(f32[192,128]{1,0:T(8,128)S(1)} %get-tuple-element.105), channel_id=1, source_target_pairs={{0,8},{4,12},{8,0},{12,4},{16,24},{20,28},{24,16},{28,20},{32,40},... | collective-permute-start | bytes 294920 | tf_op jit(solution)/shard_map/ppermute | solution.py:256
  34.4 5.7 %collective-permute-start.13 = (f32[192,128]{1,0:T(8,128)S(1)}, f32[192,128]{1,0:T(8,128)S(1)}, u32[]{:S(2)}, u32[]{:S(2)}) collective-permute-start(f32[192,128]{1,0:T(8,128)S(1)} %get-tuple-element.106), channel_id=1, source_target_pairs={{0,24},{4,28},{8,16},{12,20},{16,8},{20,12},{24,0},{28,4},{32,56},... | collective-permute-start | bytes 294920 | tf_op jit(solution)/shard_map/ppermute | solution.py:256
  40.2 4.8 %collective-permute-start.15 = (f32[256,512]{1,0:T(8,128)S(1)}, f32[256,512]{1,0:T(8,128)S(1)}, u32[]{:S(2)}, u32[]{:S(2)}) collective-permute-start(f32[256,512]{1,0:T(8,128)S(1)} %assemble.1.refs_5_), channel_id=1, source_target_pairs={{0,4},{4,0},{8,12},{12,8},{16,20},{20,16},{24,28},{28,24},{32,36},... | collective-permute-start | bytes 1572872 | tf_op jit(solution)/shard_map/ppermute | solution.py:252

commit v5 on v4

--- a/solution.py
+++ b/solution.py
@@ -141,8 +141,7 @@
     both = packed[:, R:] + packed_got[:, R:]
     both = jnp.concatenate([both[: 3 * R // 2], both[3 * R // 2 :]], 1)
     w_next[...] = both
-    m2[3 * R :, :] = both[: 3 * R // 4]
-    m3[3 * R :, :] = both[3 * R // 4 :]
+    m3[3 * R :, :] = both
 
 
 def unfold(w):
@@ -152,9 +151,9 @@
 def k4(me_ref, m0, g2, g1, g3, w, sel, z0, z2, z1, z3, q2, p, q):
     me, bit = bits(me_ref)
     own = unfold(w)
-    other = unfold(jnp.concatenate([g2[3 * R :, :], g3[3 * R :, :]], 0))
+    other = unfold(g3[3 * R :, :])
     near = m0[...] + g1[...]
-    far = g2[: 3 * R, :] + g3[: 3 * R, :]
+    far = g2[...] + g3[: 3 * R, :]
     stack(p, near[2 * R :], far[2 * R :], bit[2])
     q[...] = mm(sel[2], p[...])
     mine, theirs = rows_of(q, bit[2], True), rows_of(q, bit[2], False)
@@ -299,7 +298,7 @@
     )
     *messages, p3, q4_mine, q4_other, w_next = call(
         k3, (me, g, got, w, w_got, packed, packed_got, sel),
-        [shape(3 * R + k, eighth) for k in (0, 3 * R // 4, 0, 3 * R // 4)] + [shape(R, half)] * 3
+        [shape(3 * R + k, eighth) for k in (0, 0, 0, 3 * R // 2)] + [shape(R, half)] * 3
         + [shape(3 * R // 2, 2 * R)],
         [SM] + [VM] * 7, "level4", 1000, 4 * MIB, 10,
         scratch=[pltpu.VMEM((2 * R, half), F32)] * 2 + [pltpu.VMEM((3 * R, half), F32)],

time: 47.1 us -> 46.8 us (level)
  waiting for transfers between devices: 6.52 us -> 4.55 us
  starting transfers between devices: 18.7 us -> 20.4 us
    ppermute x11, waiting for transfers between devices: 5.99 us -> 4.01 us  [along(): return lax.ppermute(value, 'rows', [(i, i ^ d << shift) for i in range(32)])]
    ppermute x5, starting transfers between devices: 5.53 us -> 6.69 us  [to_other_core(): return lax.ppermute(value, 'rows', [(i, i ^ 1) for i in range(32)])]
    ppermute x11, starting transfers between devices: 13.2 us -> 13.7 us  [along(): return lax.ppermute(value, 'rows', [(i, i ^ d << shift) for i in range(32)])]
  transfers between devices with their start and end apart: 16 -> 16, of which waited for: 6 -> 5; matrix products, arithmetic and copies ran while one was open for 0% -> 0% of each run, Pallas kernels for 34% -> 34%
where the time goes in v5:
time: 46.8 us; the launch traced here: 46.7 us
  Pallas kernels  21.4 us (46%)
  starting transfers between devices  20.4 us (44%)
  waiting for transfers between devices  4.55 us (10%)
    pallas_call x14, Pallas kernels, call(): pl.pallas_call(kernel, out_shape=tuple(outs), in_specs=specs, out_specs=t...  17.7 us
    ppermute x11, starting transfers between devices, along(): return lax.ppermute(value, 'rows', [(i, i ^ d << shift) for i in range(32)])  13.7 us
    ppermute x5, starting transfers between devices, to_other_core(): return lax.ppermute(value, 'rows', [(i, i ^ 1) for i in range(32)])  6.69 us
    ppermute x11, waiting for transfers between devices, along(): return lax.ppermute(value, 'rows', [(i, i ^ d << shift) for i in range(32)])  4.01 us
    pallas_call x2, Pallas kernels, finish(): pl.pallas_call(lambda *refs: k7(mine, *refs), out_shape=shape(rows, cols)...  3.72 us
  transfers between devices with their start and end apart: 16, of which 5 were waited for; matrix products, arithmetic and copies ran while one was open for 0% of the time, Pallas kernels for 34%

profile of v5, /device:TPU:1, one launch (start us, length us, event | category | flops | bytes accessed | tf_op | source)
XLA Modules:
  0.0 46.7 jit_solution(18054100131140746778)
XLA Ops:
  0.0 0.0 copy-start.2
  0.0 2.6 %couple.1 = (f32[256,256]{1,0:T(8,128)S(1)}, f32[192,128]{1,0:T(8,128)S(1)}, bf16[320,1024]{1,0:T(8,128)(2,1)S(1)}, bf16[320,1024]{1,0:T(8,128)(2,1)S(1)}, f32[6,128,128]{2,1,0:T(8,128)S(1)}) custom-call(s32[1]{0:T(128)} %bitcast.me_ref.refs_0_, f32[320,1024]{1,0:T(8,128)} %bitcast.9, f32[320,1024]{1,0:T(8,128)} %bitcast.7, f32[31,128,128]{2,1,0:T(8,128)} %cores_hbm.1), custom_call_target="tpu_custom_call" | custom-call | flops 1000 | bytes 1000 | tf_op jit(solution)/shard_map/couple/pallas_call | solution.py:48
  2.7 2.1 %collective-permute-start = (f32[192,128]{1,0:T(8,128)S(1)}, f32[192,128]{1,0:T(8,128)S(1)}, u32[]{:S(2)}, u32[]{:S(2)}) collective-permute-start(f32[192,128]{1,0:T(8,128)S(1)} %get-tuple-element.62), channel_id=1, source_target_pairs={{0,8},{4,12},{8,0},{12,4},{16,24},{20,28},{24,16},{28,20},{32,40},... | collective-permute-start | bytes 294920 | tf_op jit(solution)/shard_map/ppermute | solution.py:255
  4.8 1.0 %collective-permute-start.3 = (f32[256,256]{1,0:T(8,128)S(1)}, f32[256,256]{1,0:T(8,128)S(1)}, u32[]{:S(2)}, u32[]{:S(2)}) collective-permute-start(f32[256,256]{1,0:T(8,128)S(1)} %get-tuple-element.70.w), channel_id=1, source_target_pairs={{0,4},{4,0},{8,12},{12,8},{16,20},{20,16},{24,28},{28,24},{32,36},... | collective-permute-start | bytes 786440 | tf_op jit(solution)/shard_map/ppermute | solution.py:251
  5.7 0.0 copy-done.2
  5.7 0.0 copy-start
  5.7 2.2 %project.1 = (bf16[320,1024]{1,0:T(8,128)(2,1)S(1)}, bf16[320,1024]{1,0:T(8,128)(2,1)S(1)}, bf16[1024,1024]{1,0:T(8,128)(2,1)S(1)}, bf16[1024,1024]{1,0:T(8,128)(2,1)S(1)}) custom-call(bf16[320,1024]{1,0:T(8,128)(2,1)S(1)} %get-tuple-element.63.vh, bf16[320,1024]{1,0:T(8,128)(2,1)S(1)} %get-tuple-element.64.vl, f32[1024,1024]{1,0:T(8,128)S(1)} %copy-done.2), custom_call_target="tpu_custom_call" | custom-call | flops 1000 | bytes 1000 | tf_op jit(solution)/shard_map/project/pallas_call | solution.py:48
  8.0 0.0 copy-done
  8.0 1.2 %columns.2 = f32[320,512]{1,0:T(8,128)S(1)} custom-call(s32[1]{0:T(128)} %bitcast.me_ref.refs_0_, bf16[320,1024]{1,0:T(8,128)(2,1)S(1)} %get-tuple-element.68.refs_1_, bf16[320,1024]{1,0:T(8,128)(2,1)S(1)} %get-tuple-element.66.refs_2_, f32[1024,1024]{1,0:T(8,128)S(1)} %copy-done), custom_call_target="tpu_custom_call" | custom-call | flops 1000 | bytes 1000 | tf_op jit(solution)/shard_map/columns/pallas_call | solution.py:48
  9.2 0.1 collective-permute-start.2
  9.3 0.0 collective-permute-done.far
  9.3 0.5 %collective-permute-start.1 = (f32[192,128]{1,0:T(8,128)S(1)}, f32[192,128]{1,0:T(8,128)S(1)}, u32[]{:S(2)}, u32[]{:S(2)}) collective-permute-start(f32[192,128]{1,0:T(8,128)S(1)} %collective-permute-done.far), channel_id=1, source_target_pairs={{0,4},{4,0},{8,12},{12,8},{16,20},{20,16},{24,28},{28,24},{32,36},... | collective-permute-start | bytes 294920 | tf_op jit(solution)/shard_map/ppermute | solution.py:251
  9.8 1.2 %columns.3.g = f32[320,512]{1,0:T(8,128)S(1)} custom-call(s32[1]{0:T(128)} %bitcast.me_ref.refs_0_, bf16[320,1024]{1,0:T(8,128)(2,1)S(1)} %get-tuple-element.68.refs_1_, bf16[320,1024]{1,0:T(8,128)(2,1)S(1)} %get-tuple-element.66.refs_2_, f32[1024,1024]{1,0:T(8,128)S(1)} %copy-done), custom_call_target="tpu_custom_call" | custom-call | flops 10000000000 | bytes 1000 | tf_op jit(solution)/shard_map/columns/pallas_call | solution.py:48
  11.0 0.0 copy-start.1
  11.0 0.5 %collective-permute-done.1.far_got = f32[192,128]{1,0:T(8,128)S(1)} collective-permute-done((f32[192,128]{1,0:T(8,128)S(1)}, f32[192,128]{1,0:T(8,128)S(1)}, u32[]{:S(2)}, u32[]{:S(2)}) %collective-permute-start.1) | collective-permute-done | bytes 98336 | tf_op jit(solution)/shard_map/ppermute | solution.py:251
  11.5 0.0 collective-permute-done.3.w_got
  11.5 0.1 chip.1
  11.6 0.0 collective-permute-done.2.got
  11.6 1.0 %level4.1 = (f32[192,128]{1,0:T(8,128)S(1)}, f32[192,128]{1,0:T(8,128)S(1)}, f32[192,128]{1,0:T(8,128)S(1)}, f32[288,128]{1,0:T(8,128)S(1)}, f32[64,512]{1,0:T(8...) custom-call(s32[1]{0:T(128)} %bitcast.me_ref.refs_0_, f32[320,512]{1,0:T(8,128)S(1)} %columns.3.g, ...), custom_call_target="tpu_custom_call" | custom-call | flops 1000 | bytes 1000 | tf_op jit(solution)/shard_map/level4/pallas_call | solution.py:48
  12.6 1.9 %collective-permute-start.6 = (f32[288,128]{1,0:T(8,128)S(1)}, f32[288,128]{1,0:T(8,128)S(1)}, u32[]{:S(2)}, u32[]{:S(2)}) collective-permute-start(f32[288,128]{1,0:T(8,128)S(1)} %get-tuple-element.78), channel_id=1, source_target_pairs={{0,24},{4,28},{8,16},{12,20},{16,8},{20,12},{24,0},{28,4},{32,56},... | collective-permute-start | bytes 442376 | tf_op jit(solution)/shard_map/ppermute | solution.py:255
  14.5 0.7 %collective-permute-start.4 = (f32[192,128]{1,0:T(8,128)S(1)}, f32[192,128]{1,0:T(8,128)S(1)}, u32[]{:S(2)}, u32[]{:S(2)}) collective-permute-start(f32[192,128]{1,0:T(8,128)S(1)} %get-tuple-element.76), channel_id=1, source_target_pairs={{0,16},{4,20},{8,24},{12,28},{16,0},{20,4},{24,8},{28,12},{32,48},... | collective-permute-start | bytes 294920 | tf_op jit(solution)/shard_map/ppermute | solution.py:255
  15.2 0.7 %collective-permute-start.5 = (f32[192,128]{1,0:T(8,128)S(1)}, f32[192,128]{1,0:T(8,128)S(1)}, u32[]{:S(2)}, u32[]{:S(2)}) collective-permute-start(f32[192,128]{1,0:T(8,128)S(1)} %get-tuple-element.77), channel_id=1, source_target_pairs={{0,8},{4,12},{8,0},{12,4},{16,24},{20,28},{24,16},{28,20},{32,40},... | collective-permute-start | bytes 294920 | tf_op jit(solution)/shard_map/ppermute | solution.py:255
  15.9 0.0 copy-done.1
  15.9 0.6 %turn.1 = (bf16[1024,256]{1,0:T(8,128)(2,1)S(1)}, bf16[1024,256]{1,0:T(8,128)(2,1)S(1)}, bf16[1024,192]{1,0:T(8,128)(2,1)S(1)}) custom-call(f32[320,1024]{1,0:T(8,128)S(1)} %bitcast.8), custom_call_target="tpu_custom_call" | custom-call | flops 10 | bytes 1000 | tf_op jit(solution)/shard_map/turn/pallas_call | solution.py:48
  16.5 3.7 %leaf.3.refs_1_.refs_2_ = f32[1024,512]{1,0:T(8,128)S(1)} custom-call(s32[1]{0:T(128)} %bitcast.me_ref.refs_0_, bf16[1024,1024]{1,0:T(8,128)(2,1)S(1)} %get-tuple-element.107.refs_1_, bf16[1024,1024]{1,0:T(8,128)(2,1)S(1)} %get-tuple-element.82.refs_2_, f32[1024,1024]{1,0:T(8,128)S(1)} %copy-done, bf16[1024,192]{1,0:T(8,128)(2,1)S(1)} %get-tuple-element.84.refs_4_, ...), custom_call_target="tpu_custom_call" | custom-call | flops 1000 | bytes 1000 | tf_op jit(solution)/shard_map/leaf/pallas_call | solution.py:48
  20.2 1.1 %collective-permute-start.10 = (f32[64,512]{1,0:T(8,128)S(1)}, f32[64,512]{1,0:T(8,128)S(1)}, u32[]{:S(2)}, u32[]{:S(2)}) collective-permute-start(f32[64,512]{1,0:T(8,128)S(1)} %get-tuple-element.97), channel_id=1, source_target_pairs={{0,4},{4,0},{8,12},{12,8},{16,20},{20,16},{24,28},{28,24},{32,36},... | collective-permute-start | bytes 393224 | tf_op jit(solution)/shard_map/ppermute | solution.py:251
  21.2 0.0 collective-permute-done.4.g2
  21.3 0.0 collective-permute-done.5.g1
  21.3 0.0 collective-permute-done.6.g3
  21.3 0.4 level2.1
  21.6 3.7 %collective-permute-start.7 = (f32[160,128]{1,0:T(8,128)S(1)}, f32[160,128]{1,0:T(8,128)S(1)}, u32[]{:S(2)}, u32[]{:S(2)}) collective-permute-start(f32[160,128]{1,0:T(8,128)S(1)} %get-tuple-element.91), channel_id=1, source_target_pairs={{0,64},{4,68},{8,72},{12,76},{16,80},{20,84},{24,88},{28,92},{32,9... | collective-permute-start | bytes 245768 | tf_op jit(solution)/shard_map/ppermute | solution.py:255
  25.3 0.7 %collective-permute-start.8 = (f32[160,128]{1,0:T(8,128)S(1)}, f32[160,128]{1,0:T(8,128)S(1)}, u32[]{:S(2)}, u32[]{:S(2)}) collective-permute-start(f32[160,128]{1,0:T(8,128)S(1)} %get-tuple-element.92), channel_id=1, source_target_pairs={{0,32},{4,36},{8,40},{12,44},{16,48},{20,52},{24,56},{28,60},{32,0... | collective-permute-start | bytes 245768 | tf_op jit(solution)/shard_map/ppermute | solution.py:255
  26.1 0.0 collective-permute-start.9
  26.1 0.5 %collective-permute-start.14 = (f32[64,512]{1,0:T(8,128)S(1)}, f32[64,512]{1,0:T(8,128)S(1)}, u32[]{:S(2)}, u32[]{:S(2)}) collective-permute-start(f32[64,512]{1,0:T(8,128)S(1)} %get-tuple-element.109.own), channel_id=1, source_target_pairs={{0,8},{4,12},{8,0},{12,4},{16,24},{20,28},{24,16},{28,20},{32,40},... | collective-permute-start | bytes 393224 | tf_op jit(solution)/shard_map/ppermute | solution.py:255
  26.5 0.0 collective-permute-done.10.refs_5_
  26.5 1.9 %leaf.4.refs_1_ = f32[1024,256]{1,0:T(8,128)S(1)} custom-call(s32[1]{0:T(128)} %bitcast.me_ref.refs_0_, bf16[1024,1024]{1,0:T(8,128)(2,1)S(1)} %get-tuple-element.107.refs_1_, bf16[1024,1024]{1,0:T(8,128)(2,1)S(1)} %get-tuple-element.82.refs_2_, f32[1024,1024]{1,0:T(8,128)S(1)} %copy-done, bf16[1024,192]{1,0:T(8,128)(2,1)S(1)} %get-tuple-element.84.refs_4_, ...), custom_call_target="tpu_custom_call" | custom-call | flops 1000 | bytes 1000 | tf_op jit(solution)/shard_map/leaf/pallas_call | solution.py:48
  28.5 0.0 collective-permute-done.7.s2
  28.5 0.6 %collective-permute-done.8.s1 = f32[160,128]{1,0:T(8,128)S(1)} collective-permute-done((f32[160,128]{1,0:T(8,128)S(1)}, f32[160,128]{1,0:T(8,128)S(1)}, u32[]{:S(2)}, u32[]{:S(2)}) %collective-permute-start.8) | collective-permute-done | bytes 81952 | tf_op jit(solution)/shard_map/ppermute | solution.py:255
  29.1 1.5 %collective-permute-done.9.s3 = f32[160,128]{1,0:T(8,128)S(1)} collective-permute-done((f32[160,128]{1,0:T(8,128)S(1)}, f32[160,128]{1,0:T(8,128)S(1)}, u32[]{:S(2)}, u32[]{:S(2)}) %collective-permute-start.9) | collective-permute-done | bytes 81952 | tf_op jit(solution)/shard_map/ppermute | solution.py:255
  30.6 0.6 %levels10.1 = (f32[192,128]{1,0:T(8,128)S(1)}, f32[192,128]{1,0:T(8,128)S(1)}, f32[192,128]{1,0:T(8,128)S(1)}, f32[192,128]{1,0:T(8,128)S(1)}) custom-call(s32[1]{0:T(128)} %bitcast.me_ref.refs_0_, f32[160,128]{1,0:T(8,128)S(1)} %get-tuple-element.99.s0, f32[160,128]{1,0:T(8,128)S(1)} %collective-permute-done.7.s2, ...), custom_call_target="tpu_custom_call" | custom-call | flops 1000 | bytes 1000 | tf_op jit(solution)/shard_map/levels10/pallas_call | solution.py:48
  31.1 2.5 %collective-permute-start.11 = (f32[192,128]{1,0:T(8,128)S(1)}, f32[192,128]{1,0:T(8,128)S(1)}, u32[]{:S(2)}, u32[]{:S(2)}) collective-permute-start(f32[192,128]{1,0:T(8,128)S(1)} %get-tuple-element.104), channel_id=1, source_target_pairs={{0,16},{4,20},{8,24},{12,28},{16,0},{20,4},{24,8},{28,12},{32,48},... | collective-permute-start | bytes 294920 | tf_op jit(solution)/shard_map/ppermute | solution.py:255
  33.7 0.0 collective-permute-start.12
  33.7 0.8 %collective-permute-start.13 = (f32[192,128]{1,0:T(8,128)S(1)}, f32[192,128]{1,0:T(8,128)S(1)}, u32[]{:S(2)}, u32[]{:S(2)}) collective-permute-start(f32[192,128]{1,0:T(8,128)S(1)} %get-tuple-element.106), channel_id=1, source_target_pairs={{0,24},{4,28},{8,16},{12,20},{16,8},{20,12},{24,0},{28,4},{32,56},... | collective-permute-start | bytes 294920 | tf_op jit(solution)/shard_map/ppermute | solution.py:255
  34.5 2.0 %leaf.5.refs_2_ = f32[1024,256]{1,0:T(8,128)S(1)} custom-call(s32[1]{0:T(128)} %bitcast.me_ref.refs_0_, bf16[1024,1024]{1,0:T(8,128)(2,1)S(1)} %get-tuple-element.107.refs_1_, bf16[1024,1024]{1,0:T(8,128)(2,1)S(1)} %get-tuple-element.82.refs_2_, f32[1024,1024]{1,0:T(8,128)S(1)} %copy-done, bf16[1024,192]{1,0:T(8,128)(2,1)S(1)} %get-tuple-element.84.refs_4_, ...), custom_call_target="tpu_custom_call" | custom-call | flops 1000 | bytes 1000 | tf_op jit(solution)/shard_map/leaf/pallas_call | solution.py:48
  36.4 0.0 collective-permute-done.14.got
  36.4 0.2 level3.1.q3
  36.7 0.0 collective-permute-done.11.r2
  36.7 0.4 collective-permute-done.12.r1
  37.1 1.5 %collective-permute-done.13.r3 = f32[192,128]{1,0:T(8,128)S(1)} collective-permute-done((f32[192,128]{1,0:T(8,128)S(1)}, f32[192,128]{1,0:T(8,128)S(1)}, u32[]{:S(2)}, u32[]{:S(2)}) %collective-permute-start.13) | collective-permute-done | bytes 98336 | tf_op jit(solution)/shard_map/ppermute | solution.py:255
  38.6 0.1 assemble.1.refs_5_
  38.7 4.1 %collective-permute-start.15 = (f32[256,512]{1,0:T(8,128)S(1)}, f32[256,512]{1,0:T(8,128)S(1)}, u32[]{:S(2)}, u32[]{:S(2)}) collective-permute-start(f32[256,512]{1,0:T(8,128)S(1)} %assemble.1.refs_5_), channel_id=1, source_target_pairs={{0,4},{4,0},{8,12},{12,8},{16,20},{20,16},{24,28},{28,24},{32,36},... | collective-permute-start | bytes 1572872 | tf_op jit(solution)/shard_map/ppermute | solution.py:251
  42.8 1.9 %finish.2.refs_6_ = f32[1024,1024]{1,0:T(8,128)} custom-call(s32[1]{0:T(128)} %bitcast.me_ref.refs_0_, f32[1024,512]{1,0:T(8,128)S(1)} %leaf.3.refs_1_.refs_2_, f32[1024,512]{1,0:T(8,128)S(1)} %leaf.3.refs_1_.refs_2_, bf16[1024,256]{1,0:T(8,128)(2,1)S(1)} %get-tuple-element.111.refs_3_, bf16[1024,256]{1,0:T(8,128)(2,1)S(1)} %get-tuple-element.112.refs_4_, ...), custom_call_target="tpu_custom_call" | custom-call | flops 1000000000 | bytes 5242880 | tf_op jit(solution)/shard_map/finish/pallas_call | solution.py:345
  44.7 0.0 collective-permute-done.15.refs_5_
  44.7 1.9 %finish.3 = f32[1024,1024]{1,0:T(8,128)} custom-call(s32[1]{0:T(128)} %bitcast.me_ref.refs_0_, f32[1024,256]{1,0:T(8,128)S(1)} %leaf.4.refs_1_, f32[1024,256]{1,0:T(8,128)S(1)} %leaf.5.refs_2_, bf16[1024,256]{1,0:T(8,128)(2,1)S(1)} %get-tuple-element.111.refs_3_, bf16[1024,256]{1,0:T(8,128)(2,1)S(1)} %get-tuple-element.112.refs_4_, ...), custom_call_target="tpu_custom_call", output_to_operand_aliasing={{}: (6, {})} | custom-call | flops 1000000000 | bytes 5242880 | tf_op jit(solution)/shard_map/finish/pallas_call | solution.py:345
Async XLA Ops:
  0.0 5.7 %copy-start.2 = (f32[1024,1024]{1,0:T(8,128)S(1)}, f32[1024,1024]{1,0:T(8,128)}, u32[]{:S(2)}) copy-start(f32[1024,1024]{1,0:T(8,128)} %l.1) | copy-start | bytes 12582916
  2.7 6.6 %collective-permute-start = (f32[192,128]{1,0:T(8,128)S(1)}, f32[192,128]{1,0:T(8,128)S(1)}, u32[]{:S(2)}, u32[]{:S(2)}) collective-permute-start(f32[192,128]{1,0:T(8,128)S(1)} %get-tuple-element.62), channel_id=1, source_target_pairs={{0,8},{4,12},{8,0},{12,4},{16,24},{20,28},{24,16},{28,20},{32,40},... | collective-permute-start | bytes 294920 | tf_op jit(solution)/shard_map/ppermute | solution.py:255
  4.8 6.7 %collective-permute-start.3 = (f32[256,256]{1,0:T(8,128)S(1)}, f32[256,256]{1,0:T(8,128)S(1)}, u32[]{:S(2)}, u32[]{:S(2)}) collective-permute-start(f32[256,256]{1,0:T(8,128)S(1)} %get-tuple-element.70.w), channel_id=1, source_target_pairs={{0,4},{4,0},{8,12},{12,8},{16,20},{20,16},{24,28},{28,24},{32,36},... | collective-permute-start | bytes 786440 | tf_op jit(solution)/shard_map/ppermute | solution.py:251
  5.7 2.2 %copy-start = (f32[1024,1024]{1,0:T(8,128)S(1)}, f32[1024,1024]{1,0:T(8,128)}, u32[]{:S(2)}) copy-start(f32[1024,1024]{1,0:T(8,128)} %refs_3_.9) | copy-start | bytes 12582916
  9.2 2.4 %collective-permute-start.2 = (f32[320,512]{1,0:T(8,128)S(1)}, f32[320,512]{1,0:T(8,128)S(1)}, u32[]{:S(2)}, u32[]{:S(2)}) collective-permute-start(f32[320,512]{1,0:T(8,128)S(1)} %columns.2), channel_id=1, source_target_pairs={{0,4},{4,0},{8,12},{12,8},{16,20},{20,16},{24,28},{28,24},{32,36},... | collective-permute-start | bytes 1966088 | tf_op jit(solution)/shard_map/ppermute | solution.py:251
  9.3 2.2 %collective-permute-start.1 = (f32[192,128]{1,0:T(8,128)S(1)}, f32[192,128]{1,0:T(8,128)S(1)}, u32[]{:S(2)}, u32[]{:S(2)}) collective-permute-start(f32[192,128]{1,0:T(8,128)S(1)} %collective-permute-done.far), channel_id=1, source_target_pairs={{0,4},{4,0},{8,12},{12,8},{16,20},{20,16},{24,28},{28,24},{32,36},... | collective-permute-start | bytes 294920 | tf_op jit(solution)/shard_map/ppermute | solution.py:251
  11.0 5.0 %copy-start.1 = (f32[5,1024,64]{1,2,0:T(8,128)S(1)}, f32[5,1024,64]{1,2,0:T(8,128)}, u32[]{:S(2)}) copy-start(f32[5,1024,64]{1,2,0:T(8,128)} %param.7) | copy-start | bytes 3932164
  12.6 8.7 %collective-permute-start.6 = (f32[288,128]{1,0:T(8,128)S(1)}, f32[288,128]{1,0:T(8,128)S(1)}, u32[]{:S(2)}, u32[]{:S(2)}) collective-permute-start(f32[288,128]{1,0:T(8,128)S(1)} %get-tuple-element.78), channel_id=1, source_target_pairs={{0,24},{4,28},{8,16},{12,20},{16,8},{20,12},{24,0},{28,4},{32,56},... | collective-permute-start | bytes 442376 | tf_op jit(solution)/shard_map/ppermute | solution.py:255
  14.5 6.8 %collective-permute-start.4 = (f32[192,128]{1,0:T(8,128)S(1)}, f32[192,128]{1,0:T(8,128)S(1)}, u32[]{:S(2)}, u32[]{:S(2)}) collective-permute-start(f32[192,128]{1,0:T(8,128)S(1)} %get-tuple-element.76), channel_id=1, source_target_pairs={{0,16},{4,20},{8,24},{12,28},{16,0},{20,4},{24,8},{28,12},{32,48},... | collective-permute-start | bytes 294920 | tf_op jit(solution)/shard_map/ppermute | solution.py:255
  15.2 6.1 %collective-permute-start.5 = (f32[192,128]{1,0:T(8,128)S(1)}, f32[192,128]{1,0:T(8,128)S(1)}, u32[]{:S(2)}, u32[]{:S(2)}) collective-permute-start(f32[192,128]{1,0:T(8,128)S(1)} %get-tuple-element.77), channel_id=1, source_target_pairs={{0,8},{4,12},{8,0},{12,4},{16,24},{20,28},{24,16},{28,20},{32,40},... | collective-permute-start | bytes 294920 | tf_op jit(solution)/shard_map/ppermute | solution.py:255
  20.2 6.4 %collective-permute-start.10 = (f32[64,512]{1,0:T(8,128)S(1)}, f32[64,512]{1,0:T(8,128)S(1)}, u32[]{:S(2)}, u32[]{:S(2)}) collective-permute-start(f32[64,512]{1,0:T(8,128)S(1)} %get-tuple-element.97), channel_id=1, source_target_pairs={{0,4},{4,0},{8,12},{12,8},{16,20},{20,16},{24,28},{28,24},{32,36},... | collective-permute-start | bytes 393224 | tf_op jit(solution)/shard_map/ppermute | solution.py:251
  21.6 6.9 %collective-permute-start.7 = (f32[160,128]{1,0:T(8,128)S(1)}, f32[160,128]{1,0:T(8,128)S(1)}, u32[]{:S(2)}, u32[]{:S(2)}) collective-permute-start(f32[160,128]{1,0:T(8,128)S(1)} %get-tuple-element.91), channel_id=1, source_target_pairs={{0,64},{4,68},{8,72},{12,76},{16,80},{20,84},{24,88},{28,92},{32,9... | collective-permute-start | bytes 245768 | tf_op jit(solution)/shard_map/ppermute | solution.py:255
  25.3 3.7 %collective-permute-start.8 = (f32[160,128]{1,0:T(8,128)S(1)}, f32[160,128]{1,0:T(8,128)S(1)}, u32[]{:S(2)}, u32[]{:S(2)}) collective-permute-start(f32[160,128]{1,0:T(8,128)S(1)} %get-tuple-element.92), channel_id=1, source_target_pairs={{0,32},{4,36},{8,40},{12,44},{16,48},{20,52},{24,56},{28,60},{32,0... | collective-permute-start | bytes 245768 | tf_op jit(solution)/shard_map/ppermute | solution.py:255
  26.1 4.5 %collective-permute-start.9 = (f32[160,128]{1,0:T(8,128)S(1)}, f32[160,128]{1,0:T(8,128)S(1)}, u32[]{:S(2)}, u32[]{:S(2)}) collective-permute-start(f32[160,128]{1,0:T(8,128)S(1)} %get-tuple-element.93), channel_id=1, source_target_pairs={{0,96},{4,100},{8,104},{12,108},{16,112},{20,116},{24,120},{28,124... | collective-permute-start | bytes 245768 | tf_op jit(solution)/shard_map/ppermute | solution.py:255
  26.1 10.4 %collective-permute-start.14 = (f32[64,512]{1,0:T(8,128)S(1)}, f32[64,512]{1,0:T(8,128)S(1)}, u32[]{:S(2)}, u32[]{:S(2)}) collective-permute-start(f32[64,512]{1,0:T(8,128)S(1)} %get-tuple-element.109.own), channel_id=1, source_target_pairs={{0,8},{4,12},{8,0},{12,4},{16,24},{20,28},{24,16},{28,20},{32,40},... | collective-permute-start | bytes 393224 | tf_op jit(solution)/shard_map/ppermute | solution.py:255
  31.1 5.6 %collective-permute-start.11 = (f32[192,128]{1,0:T(8,128)S(1)}, f32[192,128]{1,0:T(8,128)S(1)}, u32[]{:S(2)}, u32[]{:S(2)}) collective-permute-start(f32[192,128]{1,0:T(8,128)S(1)} %get-tuple-element.104), channel_id=1, source_target_pairs={{0,16},{4,20},{8,24},{12,28},{16,0},{20,4},{24,8},{28,12},{32,48},... | collective-permute-start | bytes 294920 | tf_op jit(solution)/shard_map/ppermute | solution.py:255
  33.7 3.5 %collective-permute-start.12 = (f32[192,128]{1,0:T(8,128)S(1)}, f32[192,128]{1,0:T(8,128)S(1)}, u32[]{:S(2)}, u32[]{:S(2)}) collective-permute-start(f32[192,128]{1,0:T(8,128)S(1)} %get-tuple-element.105), channel_id=1, source_target_pairs={{0,8},{4,12},{8,0},{12,4},{16,24},{20,28},{24,16},{28,20},{32,40},... | collective-permute-start | bytes 294920 | tf_op jit(solution)/shard_map/ppermute | solution.py:255
  33.7 5.0 %collective-permute-start.13 = (f32[192,128]{1,0:T(8,128)S(1)}, f32[192,128]{1,0:T(8,128)S(1)}, u32[]{:S(2)}, u32[]{:S(2)}) collective-permute-start(f32[192,128]{1,0:T(8,128)S(1)} %get-tuple-element.106), channel_id=1, source_target_pairs={{0,24},{4,28},{8,16},{12,20},{16,8},{20,12},{24,0},{28,4},{32,56},... | collective-permute-start | bytes 294920 | tf_op jit(solution)/shard_map/ppermute | solution.py:255
  38.7 6.0 %collective-permute-start.15 = (f32[256,512]{1,0:T(8,128)S(1)}, f32[256,512]{1,0:T(8,128)S(1)}, u32[]{:S(2)}, u32[]{:S(2)}) collective-permute-start(f32[256,512]{1,0:T(8,128)S(1)} %assemble.1.refs_5_), channel_id=1, source_target_pairs={{0,4},{4,0},{8,12},{12,8},{16,20},{20,16},{24,28},{28,24},{32,36},... | collective-permute-start | bytes 1572872 | tf_op jit(solution)/shard_map/ppermute | solution.py:251

commit v6 on v5

--- a/solution.py
+++ b/solution.py
@@ -148,7 +148,7 @@
     return jnp.concatenate([w[:, :R], w[:, R:]], 0)
 
 
-def k4(me_ref, m0, g2, g1, g3, w, sel, z0, z2, z1, z3, q2, p, q):
+def k4(me_ref, m0, g2, g1, g3, w, sel, z0, z3, z2, z1, q2, p, q):
     me, bit = bits(me_ref)
     own = unfold(w)
     other = unfold(g3[3 * R :, :])
@@ -168,7 +168,7 @@
         out[2 * R :, :] = last
 
 
-def k5(me_ref, s0, s2, s1, s3, sel, q2, r0, r2, r1, r3, p, q):
+def k5(me_ref, s0, s3, s2, s1, sel, q2, r0, r3, r2, r1, p, q):
     me, bit = bits(me_ref)
     sums = []
     for k, (a, b) in enumerate(((s0, s1), (s2, s3))):
@@ -193,7 +193,7 @@
     q[...] = mm(rows_of(sel.at[1], bit[1], True), p[...])
 
 
-def k6(me_ref, r0, r2, r1, r3, q3, q_half):
+def k6(me_ref, r0, r3, r2, r1, q3, q_half):
     me, bit = bits(me_ref)
     x = lax.rem(me >> 1, 4)
     for d, r in ((0, r0), (1, r1), (2, r2), (3, r3)):
@@ -255,8 +255,8 @@
     return lax.ppermute(value, "rows", [(i, i ^ (d << shift)) for i in range(32)])
 
 
-def spread(values, shift):
-    return [values[0]] + [along(values[k], shift, d) for k, d in ((1, 2), (2, 1), (3, 3))]
+def spread(values, shift, order=(2, 1, 3)):
+    return [values[0]] + [along(values[k + 1], shift, d) for k, d in enumerate(order)]
 
 
 def local(right_side, leaf_inverse, left_factors, right_factors, cores):
@@ -325,7 +325,7 @@
         k4, (me, *got, w_next, sel), [shape(5 * R // 2, eighth)] * 4 + [shape(2, R, eighth)],
         [SM] + [VM] * 6, "level2", 1000, MIB, 8, scratch=small * 2,
     )
-    got, x2 = after((spread(z, 3), leaf(2, 1, q4_back, q2)))
+    got, x2 = after((spread(z, 3, (3, 2, 1)), leaf(2, 1, q4_back, q2)))
     p3_got = along(after((p3, q2))[0], 1, 1)
     back = call(
         k5, (me, *got, sel, q2), [shape(3 * R, eighth)] * 4, [SM] + [VM] * 6, "levels10", 1000, MIB, 8,
@@ -335,7 +335,7 @@
         kq, (me, p3, p3_got, sel), [shape(R, half)], [SM] + [VM] * 3, "level3", 1000, MIB, 8,
         scratch=[pltpu.VMEM((2 * R, half), F32)],
     )
-    got, x3, q3 = after((spread(back, 1), leaf(3, 1, q4_back, back[0]), q3))
+    got, x3, q3 = after((spread(back, 1, (3, 2, 1)), leaf(3, 1, q4_back, back[0]), q3))
     (q_half,) = call(
         k6, (me, *got, q3), [shape(4 * R, half)], [SM] + [VM] * 5, "assemble", 10, MIB, 8,
     )

time: 46.8 us -> 45.8 us (0.979)
  waiting for transfers between devices: 4.55 us -> 3.57 us
    ppermute x11, waiting for transfers between devices: 4.01 us -> 3.04 us  [along(): return lax.ppermute(value, 'rows', [(i, i ^ d << shift) for i in range(32)])]
  transfers between devices with their start and end apart: 16 -> 16, of which waited for: 5 -> 3; matrix products, arithmetic and copies ran while one was open for 0% -> 0% of each run, Pallas kernels for 34% -> 35%
where the time goes in v6:
time: 45.8 us; the launch traced here: 45.7 us
  Pallas kernels  21.4 us (47%)
  starting transfers between devices  20.3 us (44%)
  waiting for transfers between devices  3.57 us (8%)
    pallas_call x14, Pallas kernels, call(): pl.pallas_call(kernel, out_shape=tuple(outs), in_specs=specs, out_specs=t...  17.7 us
    ppermute x11, starting transfers between devices, along(): return lax.ppermute(value, 'rows', [(i, i ^ d << shift) for i in range(32)])  13.8 us
    ppermute x5, starting transfers between devices, to_other_core(): return lax.ppermute(value, 'rows', [(i, i ^ 1) for i in range(32)])  6.52 us
    pallas_call x2, Pallas kernels, finish(): pl.pallas_call(lambda *refs: k7(mine, *refs), out_shape=shape(rows, cols)...  3.72 us
    ppermute x11, waiting for transfers between devices, along(): return lax.ppermute(value, 'rows', [(i, i ^ d << shift) for i in range(32)])  3.04 us
  transfers between devices with their start and end apart: 16, of which 3 were waited for; matrix products, arithmetic and copies ran while one was open for 0% of the time, Pallas kernels for 35%

profile of v6, /device:TPU:1, one launch (start us, length us, event | category | flops | bytes accessed | tf_op | source)
XLA Modules:
  0.0 45.7 jit_solution(4795446128739943817)
XLA Ops:
  0.0 0.0 copy-start.2
  0.0 2.6 %couple.1 = (f32[256,256]{1,0:T(8,128)S(1)}, f32[192,128]{1,0:T(8,128)S(1)}, bf16[320,1024]{1,0:T(8,128)(2,1)S(1)}, bf16[320,1024]{1,0:T(8,128)(2,1)S(1)}, f32[6,128,128]{2,1,0:T(8,128)S(1)}) custom-call(s32[1]{0:T(128)} %bitcast.me_ref.refs_0_, f32[320,1024]{1,0:T(8,128)} %bitcast.9, f32[320,1024]{1,0:T(8,128)} %bitcast.7, f32[31,128,128]{2,1,0:T(8,128)} %cores_hbm.1), custom_call_target="tpu_custom_call" | custom-call | flops 1000 | bytes 1000 | tf_op jit(solution)/shard_map/couple/pallas_call | solution.py:48
  2.7 2.1 %collective-permute-start = (f32[192,128]{1,0:T(8,128)S(1)}, f32[192,128]{1,0:T(8,128)S(1)}, u32[]{:S(2)}, u32[]{:S(2)}) collective-permute-start(f32[192,128]{1,0:T(8,128)S(1)} %get-tuple-element.62), channel_id=1, source_target_pairs={{0,8},{4,12},{8,0},{12,4},{16,24},{20,28},{24,16},{28,20},{32,40},... | collective-permute-start | bytes 294920 | tf_op jit(solution)/shard_map/ppermute | solution.py:255
  4.8 1.0 %collective-permute-start.3 = (f32[256,256]{1,0:T(8,128)S(1)}, f32[256,256]{1,0:T(8,128)S(1)}, u32[]{:S(2)}, u32[]{:S(2)}) collective-permute-start(f32[256,256]{1,0:T(8,128)S(1)} %get-tuple-element.70.w), channel_id=1, source_target_pairs={{0,4},{4,0},{8,12},{12,8},{16,20},{20,16},{24,28},{28,24},{32,36},... | collective-permute-start | bytes 786440 | tf_op jit(solution)/shard_map/ppermute | solution.py:251
  5.7 0.0 copy-done.2
  5.7 0.0 copy-start
  5.7 2.2 %project.1 = (bf16[320,1024]{1,0:T(8,128)(2,1)S(1)}, bf16[320,1024]{1,0:T(8,128)(2,1)S(1)}, bf16[1024,1024]{1,0:T(8,128)(2,1)S(1)}, bf16[1024,1024]{1,0:T(8,128)(2,1)S(1)}) custom-call(bf16[320,1024]{1,0:T(8,128)(2,1)S(1)} %get-tuple-element.63.vh, bf16[320,1024]{1,0:T(8,128)(2,1)S(1)} %get-tuple-element.64.vl, f32[1024,1024]{1,0:T(8,128)S(1)} %copy-done.2), custom_call_target="tpu_custom_call" | custom-call | flops 1000 | bytes 1000 | tf_op jit(solution)/shard_map/project/pallas_call | solution.py:48
  8.0 0.0 copy-done
  8.0 1.2 %columns.2 = f32[320,512]{1,0:T(8,128)S(1)} custom-call(s32[1]{0:T(128)} %bitcast.me_ref.refs_0_, bf16[320,1024]{1,0:T(8,128)(2,1)S(1)} %get-tuple-element.68.refs_1_, bf16[320,1024]{1,0:T(8,128)(2,1)S(1)} %get-tuple-element.66.refs_2_, f32[1024,1024]{1,0:T(8,128)S(1)} %copy-done), custom_call_target="tpu_custom_call" | custom-call | flops 1000 | bytes 1000 | tf_op jit(solution)/shard_map/columns/pallas_call | solution.py:48
  9.2 0.1 collective-permute-start.2
  9.3 0.0 collective-permute-done.far
  9.3 0.5 %collective-permute-start.1 = (f32[192,128]{1,0:T(8,128)S(1)}, f32[192,128]{1,0:T(8,128)S(1)}, u32[]{:S(2)}, u32[]{:S(2)}) collective-permute-start(f32[192,128]{1,0:T(8,128)S(1)} %collective-permute-done.far), channel_id=1, source_target_pairs={{0,4},{4,0},{8,12},{12,8},{16,20},{20,16},{24,28},{28,24},{32,36},... | collective-permute-start | bytes 294920 | tf_op jit(solution)/shard_map/ppermute | solution.py:251
  9.8 1.2 %columns.3.g = f32[320,512]{1,0:T(8,128)S(1)} custom-call(s32[1]{0:T(128)} %bitcast.me_ref.refs_0_, bf16[320,1024]{1,0:T(8,128)(2,1)S(1)} %get-tuple-element.68.refs_1_, bf16[320,1024]{1,0:T(8,128)(2,1)S(1)} %get-tuple-element.66.refs_2_, f32[1024,1024]{1,0:T(8,128)S(1)} %copy-done), custom_call_target="tpu_custom_call" | custom-call | flops 10000000000 | bytes 1000 | tf_op jit(solution)/shard_map/columns/pallas_call | solution.py:48
  11.0 0.0 copy-start.1
  11.0 0.5 %collective-permute-done.1.far_got = f32[192,128]{1,0:T(8,128)S(1)} collective-permute-done((f32[192,128]{1,0:T(8,128)S(1)}, f32[192,128]{1,0:T(8,128)S(1)}, u32[]{:S(2)}, u32[]{:S(2)}) %collective-permute-start.1) | collective-permute-done | bytes 98336 | tf_op jit(solution)/shard_map/ppermute | solution.py:251
  11.5 0.0 collective-permute-done.3.w_got
  11.5 0.1 chip.1
  11.6 0.0 collective-permute-done.2.got
  11.6 1.0 %level4.1 = (f32[192,128]{1,0:T(8,128)S(1)}, f32[192,128]{1,0:T(8,128)S(1)}, f32[192,128]{1,0:T(8,128)S(1)}, f32[288,128]{1,0:T(8,128)S(1)}, f32[64,512]{1,0:T(8...) custom-call(s32[1]{0:T(128)} %bitcast.me_ref.refs_0_, f32[320,512]{1,0:T(8,128)S(1)} %columns.3.g, ...), custom_call_target="tpu_custom_call" | custom-call | flops 1000 | bytes 1000 | tf_op jit(solution)/shard_map/level4/pallas_call | solution.py:48
  12.6 1.9 %collective-permute-start.6 = (f32[288,128]{1,0:T(8,128)S(1)}, f32[288,128]{1,0:T(8,128)S(1)}, u32[]{:S(2)}, u32[]{:S(2)}) collective-permute-start(f32[288,128]{1,0:T(8,128)S(1)} %get-tuple-element.78), channel_id=1, source_target_pairs={{0,24},{4,28},{8,16},{12,20},{16,8},{20,12},{24,0},{28,4},{32,56},... | collective-permute-start | bytes 442376 | tf_op jit(solution)/shard_map/ppermute | solution.py:255
  14.5 0.7 %collective-permute-start.4 = (f32[192,128]{1,0:T(8,128)S(1)}, f32[192,128]{1,0:T(8,128)S(1)}, u32[]{:S(2)}, u32[]{:S(2)}) collective-permute-start(f32[192,128]{1,0:T(8,128)S(1)} %get-tuple-element.76), channel_id=1, source_target_pairs={{0,16},{4,20},{8,24},{12,28},{16,0},{20,4},{24,8},{28,12},{32,48},... | collective-permute-start | bytes 294920 | tf_op jit(solution)/shard_map/ppermute | solution.py:255
  15.2 0.7 %collective-permute-start.5 = (f32[192,128]{1,0:T(8,128)S(1)}, f32[192,128]{1,0:T(8,128)S(1)}, u32[]{:S(2)}, u32[]{:S(2)}) collective-permute-start(f32[192,128]{1,0:T(8,128)S(1)} %get-tuple-element.77), channel_id=1, source_target_pairs={{0,8},{4,12},{8,0},{12,4},{16,24},{20,28},{24,16},{28,20},{32,40},... | collective-permute-start | bytes 294920 | tf_op jit(solution)/shard_map/ppermute | solution.py:255
  15.9 0.0 copy-done.1
  15.9 0.6 %turn.1 = (bf16[1024,256]{1,0:T(8,128)(2,1)S(1)}, bf16[1024,256]{1,0:T(8,128)(2,1)S(1)}, bf16[1024,192]{1,0:T(8,128)(2,1)S(1)}) custom-call(f32[320,1024]{1,0:T(8,128)S(1)} %bitcast.8), custom_call_target="tpu_custom_call" | custom-call | flops 10 | bytes 1000 | tf_op jit(solution)/shard_map/turn/pallas_call | solution.py:48
  16.5 3.7 %leaf.3.refs_1_.refs_2_ = f32[1024,512]{1,0:T(8,128)S(1)} custom-call(s32[1]{0:T(128)} %bitcast.me_ref.refs_0_, bf16[1024,1024]{1,0:T(8,128)(2,1)S(1)} %get-tuple-element.107.refs_1_, bf16[1024,1024]{1,0:T(8,128)(2,1)S(1)} %get-tuple-element.82.refs_2_, f32[1024,1024]{1,0:T(8,128)S(1)} %copy-done, bf16[1024,192]{1,0:T(8,128)(2,1)S(1)} %get-tuple-element.84.refs_4_, ...), custom_call_target="tpu_custom_call" | custom-call | flops 1000 | bytes 1000 | tf_op jit(solution)/shard_map/leaf/pallas_call | solution.py:48
  20.2 1.1 %collective-permute-start.10 = (f32[64,512]{1,0:T(8,128)S(1)}, f32[64,512]{1,0:T(8,128)S(1)}, u32[]{:S(2)}, u32[]{:S(2)}) collective-permute-start(f32[64,512]{1,0:T(8,128)S(1)} %get-tuple-element.97), channel_id=1, source_target_pairs={{0,4},{4,0},{8,12},{12,8},{16,20},{20,16},{24,28},{28,24},{32,36},... | collective-permute-start | bytes 393224 | tf_op jit(solution)/shard_map/ppermute | solution.py:251
  21.2 0.0 collective-permute-done.4.g2
  21.3 0.0 collective-permute-done.5.g1
  21.3 0.0 collective-permute-done.6.g3
  21.3 0.4 level2.1
  21.6 3.8 %collective-permute-start.7 = (f32[160,128]{1,0:T(8,128)S(1)}, f32[160,128]{1,0:T(8,128)S(1)}, u32[]{:S(2)}, u32[]{:S(2)}) collective-permute-start(f32[160,128]{1,0:T(8,128)S(1)} %get-tuple-element.91), channel_id=1, source_target_pairs={{0,96},{4,100},{8,104},{12,108},{16,112},{20,116},{24,120},{28,124... | collective-permute-start | bytes 245768 | tf_op jit(solution)/shard_map/ppermute | solution.py:255
  25.5 0.0 collective-permute-start.8
  25.5 0.7 %collective-permute-start.9 = (f32[160,128]{1,0:T(8,128)S(1)}, f32[160,128]{1,0:T(8,128)S(1)}, u32[]{:S(2)}, u32[]{:S(2)}) collective-permute-start(f32[160,128]{1,0:T(8,128)S(1)} %get-tuple-element.93), channel_id=1, source_target_pairs={{0,32},{4,36},{8,40},{12,44},{16,48},{20,52},{24,56},{28,60},{32,0... | collective-permute-start | bytes 245768 | tf_op jit(solution)/shard_map/ppermute | solution.py:255
  26.1 0.5 %collective-permute-start.14 = (f32[64,512]{1,0:T(8,128)S(1)}, f32[64,512]{1,0:T(8,128)S(1)}, u32[]{:S(2)}, u32[]{:S(2)}) collective-permute-start(f32[64,512]{1,0:T(8,128)S(1)} %get-tuple-element.109.own), channel_id=1, source_target_pairs={{0,8},{4,12},{8,0},{12,4},{16,24},{20,28},{24,16},{28,20},{32,40},... | collective-permute-start | bytes 393224 | tf_op jit(solution)/shard_map/ppermute | solution.py:255
  26.6 0.0 collective-permute-done.10.refs_5_
  26.6 2.0 %leaf.4.refs_1_ = f32[1024,256]{1,0:T(8,128)S(1)} custom-call(s32[1]{0:T(128)} %bitcast.me_ref.refs_0_, bf16[1024,1024]{1,0:T(8,128)(2,1)S(1)} %get-tuple-element.107.refs_1_, bf16[1024,1024]{1,0:T(8,128)(2,1)S(1)} %get-tuple-element.82.refs_2_, f32[1024,1024]{1,0:T(8,128)S(1)} %copy-done, bf16[1024,192]{1,0:T(8,128)(2,1)S(1)} %get-tuple-element.84.refs_4_, ...), custom_call_target="tpu_custom_call" | custom-call | flops 1000 | bytes 1000 | tf_op jit(solution)/shard_map/leaf/pallas_call | solution.py:48
  28.6 0.0 collective-permute-done.7.s3
  28.6 1.7 %collective-permute-done.8.s2 = f32[160,128]{1,0:T(8,128)S(1)} collective-permute-done((f32[160,128]{1,0:T(8,128)S(1)}, f32[160,128]{1,0:T(8,128)S(1)}, u32[]{:S(2)}, u32[]{:S(2)}) %collective-permute-start.8) | collective-permute-done | bytes 81952 | tf_op jit(solution)/shard_map/ppermute | solution.py:255
  30.3 0.0 collective-permute-done.9.s1
  30.3 0.6 %levels10.1 = (f32[192,128]{1,0:T(8,128)S(1)}, f32[192,128]{1,0:T(8,128)S(1)}, f32[192,128]{1,0:T(8,128)S(1)}, f32[192,128]{1,0:T(8,128)S(1)}) custom-call(s32[1]{0:T(128)} %bitcast.me_ref.refs_0_, f32[160,128]{1,0:T(8,128)S(1)} %get-tuple-element.99.s0, f32[160,128]{1,0:T(8,128)S(1)} %collective-permute-done.7.s3, ...), custom_call_target="tpu_custom_call" | custom-call | flops 1000 | bytes 1000 | tf_op jit(solution)/shard_map/levels10/pallas_call | solution.py:48
  30.8 1.9 %collective-permute-start.11 = (f32[192,128]{1,0:T(8,128)S(1)}, f32[192,128]{1,0:T(8,128)S(1)}, u32[]{:S(2)}, u32[]{:S(2)}) collective-permute-start(f32[192,128]{1,0:T(8,128)S(1)} %get-tuple-element.104), channel_id=1, source_target_pairs={{0,24},{4,28},{8,16},{12,20},{16,8},{20,12},{24,0},{28,4},{32,56},... | collective-permute-start | bytes 294920 | tf_op jit(solution)/shard_map/ppermute | solution.py:255
  32.8 0.7 %collective-permute-start.12 = (f32[192,128]{1,0:T(8,128)S(1)}, f32[192,128]{1,0:T(8,128)S(1)}, u32[]{:S(2)}, u32[]{:S(2)}) collective-permute-start(f32[192,128]{1,0:T(8,128)S(1)} %get-tuple-element.105), channel_id=1, source_target_pairs={{0,16},{4,20},{8,24},{12,28},{16,0},{20,4},{24,8},{28,12},{32,48},... | collective-permute-start | bytes 294920 | tf_op jit(solution)/shard_map/ppermute | solution.py:255
  33.5 0.7 %collective-permute-start.13 = (f32[192,128]{1,0:T(8,128)S(1)}, f32[192,128]{1,0:T(8,128)S(1)}, u32[]{:S(2)}, u32[]{:S(2)}) collective-permute-start(f32[192,128]{1,0:T(8,128)S(1)} %get-tuple-element.106), channel_id=1, source_target_pairs={{0,8},{4,12},{8,0},{12,4},{16,24},{20,28},{24,16},{28,20},{32,40},... | collective-permute-start | bytes 294920 | tf_op jit(solution)/shard_map/ppermute | solution.py:255
  34.2 2.0 %leaf.5.refs_2_ = f32[1024,256]{1,0:T(8,128)S(1)} custom-call(s32[1]{0:T(128)} %bitcast.me_ref.refs_0_, bf16[1024,1024]{1,0:T(8,128)(2,1)S(1)} %get-tuple-element.107.refs_1_, bf16[1024,1024]{1,0:T(8,128)(2,1)S(1)} %get-tuple-element.82.refs_2_, f32[1024,1024]{1,0:T(8,128)S(1)} %copy-done, bf16[1024,192]{1,0:T(8,128)(2,1)S(1)} %get-tuple-element.84.refs_4_, ...), custom_call_target="tpu_custom_call" | custom-call | flops 1000 | bytes 1000 | tf_op jit(solution)/shard_map/leaf/pallas_call | solution.py:48
  36.2 0.0 collective-permute-done.14.got
  36.2 0.2 level3.1.q3
  36.4 0.0 collective-permute-done.11.r3
  36.4 1.3 %collective-permute-done.12.r2 = f32[192,128]{1,0:T(8,128)S(1)} collective-permute-done((f32[192,128]{1,0:T(8,128)S(1)}, f32[192,128]{1,0:T(8,128)S(1)}, u32[]{:S(2)}, u32[]{:S(2)}) %collective-permute-start.12) | collective-permute-done | bytes 98336 | tf_op jit(solution)/shard_map/ppermute | solution.py:255
  37.8 0.0 collective-permute-done.13.r1
  37.8 0.1 assemble.1.refs_5_
  37.8 3.9 %collective-permute-start.15 = (f32[256,512]{1,0:T(8,128)S(1)}, f32[256,512]{1,0:T(8,128)S(1)}, u32[]{:S(2)}, u32[]{:S(2)}) collective-permute-start(f32[256,512]{1,0:T(8,128)S(1)} %assemble.1.refs_5_), channel_id=1, source_target_pairs={{0,4},{4,0},{8,12},{12,8},{16,20},{20,16},{24,28},{28,24},{32,36},... | collective-permute-start | bytes 1572872 | tf_op jit(solution)/shard_map/ppermute | solution.py:251
  41.8 1.9 %finish.2.refs_6_ = f32[1024,1024]{1,0:T(8,128)} custom-call(s32[1]{0:T(128)} %bitcast.me_ref.refs_0_, f32[1024,512]{1,0:T(8,128)S(1)} %leaf.3.refs_1_.refs_2_, f32[1024,512]{1,0:T(8,128)S(1)} %leaf.3.refs_1_.refs_2_, bf16[1024,256]{1,0:T(8,128)(2,1)S(1)} %get-tuple-element.111.refs_3_, bf16[1024,256]{1,0:T(8,128)(2,1)S(1)} %get-tuple-element.112.refs_4_, ...), custom_call_target="tpu_custom_call" | custom-call | flops 1000000000 | bytes 5242880 | tf_op jit(solution)/shard_map/finish/pallas_call | solution.py:345
  43.6 0.0 collective-permute-done.15.refs_5_
  43.6 1.9 %finish.3 = f32[1024,1024]{1,0:T(8,128)} custom-call(s32[1]{0:T(128)} %bitcast.me_ref.refs_0_, f32[1024,256]{1,0:T(8,128)S(1)} %leaf.4.refs_1_, f32[1024,256]{1,0:T(8,128)S(1)} %leaf.5.refs_2_, bf16[1024,256]{1,0:T(8,128)(2,1)S(1)} %get-tuple-element.111.refs_3_, bf16[1024,256]{1,0:T(8,128)(2,1)S(1)} %get-tuple-element.112.refs_4_, ...), custom_call_target="tpu_custom_call", output_to_operand_aliasing={{}: (6, {})} | custom-call | flops 1000000000 | bytes 5242880 | tf_op jit(solution)/shard_map/finish/pallas_call | solution.py:345
Async XLA Ops:
  0.0 5.7 %copy-start.2 = (f32[1024,1024]{1,0:T(8,128)S(1)}, f32[1024,1024]{1,0:T(8,128)}, u32[]{:S(2)}) copy-start(f32[1024,1024]{1,0:T(8,128)} %l.1) | copy-start | bytes 12582916
  2.7 6.6 %collective-permute-start = (f32[192,128]{1,0:T(8,128)S(1)}, f32[192,128]{1,0:T(8,128)S(1)}, u32[]{:S(2)}, u32[]{:S(2)}) collective-permute-start(f32[192,128]{1,0:T(8,128)S(1)} %get-tuple-element.62), channel_id=1, source_target_pairs={{0,8},{4,12},{8,0},{12,4},{16,24},{20,28},{24,16},{28,20},{32,40},... | collective-permute-start | bytes 294920 | tf_op jit(solution)/shard_map/ppermute | solution.py:255
  4.8 6.7 %collective-permute-start.3 = (f32[256,256]{1,0:T(8,128)S(1)}, f32[256,256]{1,0:T(8,128)S(1)}, u32[]{:S(2)}, u32[]{:S(2)}) collective-permute-start(f32[256,256]{1,0:T(8,128)S(1)} %get-tuple-element.70.w), channel_id=1, source_target_pairs={{0,4},{4,0},{8,12},{12,8},{16,20},{20,16},{24,28},{28,24},{32,36},... | collective-permute-start | bytes 786440 | tf_op jit(solution)/shard_map/ppermute | solution.py:251
  5.7 2.2 %copy-start = (f32[1024,1024]{1,0:T(8,128)S(1)}, f32[1024,1024]{1,0:T(8,128)}, u32[]{:S(2)}) copy-start(f32[1024,1024]{1,0:T(8,128)} %refs_3_.9) | copy-start | bytes 12582916
  9.2 2.4 %collective-permute-start.2 = (f32[320,512]{1,0:T(8,128)S(1)}, f32[320,512]{1,0:T(8,128)S(1)}, u32[]{:S(2)}, u32[]{:S(2)}) collective-permute-start(f32[320,512]{1,0:T(8,128)S(1)} %columns.2), channel_id=1, source_target_pairs={{0,4},{4,0},{8,12},{12,8},{16,20},{20,16},{24,28},{28,24},{32,36},... | collective-permute-start | bytes 1966088 | tf_op jit(solution)/shard_map/ppermute | solution.py:251
  9.3 2.2 %collective-permute-start.1 = (f32[192,128]{1,0:T(8,128)S(1)}, f32[192,128]{1,0:T(8,128)S(1)}, u32[]{:S(2)}, u32[]{:S(2)}) collective-permute-start(f32[192,128]{1,0:T(8,128)S(1)} %collective-permute-done.far), channel_id=1, source_target_pairs={{0,4},{4,0},{8,12},{12,8},{16,20},{20,16},{24,28},{28,24},{32,36},... | collective-permute-start | bytes 294920 | tf_op jit(solution)/shard_map/ppermute | solution.py:251
  11.0 5.0 %copy-start.1 = (f32[5,1024,64]{1,2,0:T(8,128)S(1)}, f32[5,1024,64]{1,2,0:T(8,128)}, u32[]{:S(2)}) copy-start(f32[5,1024,64]{1,2,0:T(8,128)} %param.7) | copy-start | bytes 3932164
  12.6 8.7 %collective-permute-start.6 = (f32[288,128]{1,0:T(8,128)S(1)}, f32[288,128]{1,0:T(8,128)S(1)}, u32[]{:S(2)}, u32[]{:S(2)}) collective-permute-start(f32[288,128]{1,0:T(8,128)S(1)} %get-tuple-element.78), channel_id=1, source_target_pairs={{0,24},{4,28},{8,16},{12,20},{16,8},{20,12},{24,0},{28,4},{32,56},... | collective-permute-start | bytes 442376 | tf_op jit(solution)/shard_map/ppermute | solution.py:255
  14.5 6.8 %collective-permute-start.4 = (f32[192,128]{1,0:T(8,128)S(1)}, f32[192,128]{1,0:T(8,128)S(1)}, u32[]{:S(2)}, u32[]{:S(2)}) collective-permute-start(f32[192,128]{1,0:T(8,128)S(1)} %get-tuple-element.76), channel_id=1, source_target_pairs={{0,16},{4,20},{8,24},{12,28},{16,0},{20,4},{24,8},{28,12},{32,48},... | collective-permute-start | bytes 294920 | tf_op jit(solution)/shard_map/ppermute | solution.py:255
  15.2 6.1 %collective-permute-start.5 = (f32[192,128]{1,0:T(8,128)S(1)}, f32[192,128]{1,0:T(8,128)S(1)}, u32[]{:S(2)}, u32[]{:S(2)}) collective-permute-start(f32[192,128]{1,0:T(8,128)S(1)} %get-tuple-element.77), channel_id=1, source_target_pairs={{0,8},{4,12},{8,0},{12,4},{16,24},{20,28},{24,16},{28,20},{32,40},... | collective-permute-start | bytes 294920 | tf_op jit(solution)/shard_map/ppermute | solution.py:255
  20.2 6.5 %collective-permute-start.10 = (f32[64,512]{1,0:T(8,128)S(1)}, f32[64,512]{1,0:T(8,128)S(1)}, u32[]{:S(2)}, u32[]{:S(2)}) collective-permute-start(f32[64,512]{1,0:T(8,128)S(1)} %get-tuple-element.97), channel_id=1, source_target_pairs={{0,4},{4,0},{8,12},{12,8},{16,20},{20,16},{24,28},{28,24},{32,36},... | collective-permute-start | bytes 393224 | tf_op jit(solution)/shard_map/ppermute | solution.py:251
  21.6 7.0 %collective-permute-start.7 = (f32[160,128]{1,0:T(8,128)S(1)}, f32[160,128]{1,0:T(8,128)S(1)}, u32[]{:S(2)}, u32[]{:S(2)}) collective-permute-start(f32[160,128]{1,0:T(8,128)S(1)} %get-tuple-element.91), channel_id=1, source_target_pairs={{0,96},{4,100},{8,104},{12,108},{16,112},{20,116},{24,120},{28,124... | collective-permute-start | bytes 245768 | tf_op jit(solution)/shard_map/ppermute | solution.py:255
  25.5 4.8 %collective-permute-start.8 = (f32[160,128]{1,0:T(8,128)S(1)}, f32[160,128]{1,0:T(8,128)S(1)}, u32[]{:S(2)}, u32[]{:S(2)}) collective-permute-start(f32[160,128]{1,0:T(8,128)S(1)} %get-tuple-element.92), channel_id=1, source_target_pairs={{0,64},{4,68},{8,72},{12,76},{16,80},{20,84},{24,88},{28,92},{32,9... | collective-permute-start | bytes 245768 | tf_op jit(solution)/shard_map/ppermute | solution.py:255
  25.5 4.8 %collective-permute-start.9 = (f32[160,128]{1,0:T(8,128)S(1)}, f32[160,128]{1,0:T(8,128)S(1)}, u32[]{:S(2)}, u32[]{:S(2)}) collective-permute-start(f32[160,128]{1,0:T(8,128)S(1)} %get-tuple-element.93), channel_id=1, source_target_pairs={{0,32},{4,36},{8,40},{12,44},{16,48},{20,52},{24,56},{28,60},{32,0... | collective-permute-start | bytes 245768 | tf_op jit(solution)/shard_map/ppermute | solution.py:255
  26.1 10.0 %collective-permute-start.14 = (f32[64,512]{1,0:T(8,128)S(1)}, f32[64,512]{1,0:T(8,128)S(1)}, u32[]{:S(2)}, u32[]{:S(2)}) collective-permute-start(f32[64,512]{1,0:T(8,128)S(1)} %get-tuple-element.109.own), channel_id=1, source_target_pairs={{0,8},{4,12},{8,0},{12,4},{16,24},{20,28},{24,16},{28,20},{32,40},... | collective-permute-start | bytes 393224 | tf_op jit(solution)/shard_map/ppermute | solution.py:255
  30.8 5.6 %collective-permute-start.11 = (f32[192,128]{1,0:T(8,128)S(1)}, f32[192,128]{1,0:T(8,128)S(1)}, u32[]{:S(2)}, u32[]{:S(2)}) collective-permute-start(f32[192,128]{1,0:T(8,128)S(1)} %get-tuple-element.104), channel_id=1, source_target_pairs={{0,24},{4,28},{8,16},{12,20},{16,8},{20,12},{24,0},{28,4},{32,56},... | collective-permute-start | bytes 294920 | tf_op jit(solution)/shard_map/ppermute | solution.py:255
  32.8 5.0 %collective-permute-start.12 = (f32[192,128]{1,0:T(8,128)S(1)}, f32[192,128]{1,0:T(8,128)S(1)}, u32[]{:S(2)}, u32[]{:S(2)}) collective-permute-start(f32[192,128]{1,0:T(8,128)S(1)} %get-tuple-element.105), channel_id=1, source_target_pairs={{0,16},{4,20},{8,24},{12,28},{16,0},{20,4},{24,8},{28,12},{32,48},... | collective-permute-start | bytes 294920 | tf_op jit(solution)/shard_map/ppermute | solution.py:255
  33.5 4.3 %collective-permute-start.13 = (f32[192,128]{1,0:T(8,128)S(1)}, f32[192,128]{1,0:T(8,128)S(1)}, u32[]{:S(2)}, u32[]{:S(2)}) collective-permute-start(f32[192,128]{1,0:T(8,128)S(1)} %get-tuple-element.106), channel_id=1, source_target_pairs={{0,8},{4,12},{8,0},{12,4},{16,24},{20,28},{24,16},{28,20},{32,40},... | collective-permute-start | bytes 294920 | tf_op jit(solution)/shard_map/ppermute | solution.py:255
  37.8 5.8 %collective-permute-start.15 = (f32[256,512]{1,0:T(8,128)S(1)}, f32[256,512]{1,0:T(8,128)S(1)}, u32[]{:S(2)}, u32[]{:S(2)}) collective-permute-start(f32[256,512]{1,0:T(8,128)S(1)} %assemble.1.refs_5_), channel_id=1, source_target_pairs={{0,4},{4,0},{8,12},{12,8},{16,20},{20,16},{24,28},{28,24},{32,36},... | collective-permute-start | bytes 1572872 | tf_op jit(solution)/shard_map/ppermute | solution.py:251
